TPU v7x, 32 devices: a whole 2x2x4 slice. The times are simulated.
32 devices in a mesh: ctx: 8 (over z, core), tab: 4 (over y, x).
Axes of the slice: x: 2, y: 2, z: 4, core: 2. Of those that a mesh axis runs over, the one named last changes fastest.
Arguments:
- queries: bfloat16 [32, 4, 8192], P(('ctx', 'tab')), may hold values from -80 to 80
- prefix_key_value: bfloat16 [4096, 2, 1024], P('ctx'), may hold values from -6 to 6
- tab_key_value: bfloat16 [4, 512, 2, 1024], P('tab', 'ctx'), may hold values from -6 to 6
- tab_owner: int32 [4], replicated, may hold values from 0 to 3, each once
- session_tab: int32 [32], P(('ctx', 'tab')), may hold values from 0 to 3
- suffix_key_value: bfloat16 [32, 256, 2, 1024], P(('ctx', 'tab')), may hold values from -6 to 6
- suffix_len: int32 [32], P(('ctx', 'tab')), may hold values from 1 to 256, as said below
- token_keys: bfloat16 [32, 4, 1024], P(('ctx', 'tab')), may hold values from -12 to 12
- token_values: bfloat16 [32, 4, 1024], P(('ctx', 'tab')), may hold values from -6 to 6
Outputs:
- attention: bfloat16 [32, 4, 8192], P(('ctx', 'tab'))
Inputs may be any that keep to these rules, and one draw needn't show every extreme that they name: `tab_owner`: each tab has its own slot. `suffix_len`: some session of every draw uses all 256 slots.
All inputs are finite; a program needn't handle non-finite values.
Results may differ from a plain program's by a relative error of at most 0.0023.
Values may be sent and summed in bfloat16 or wider, within the bound.
No kernel may reach another device: no remote copies, remote signals or barrier semaphores. Data moves between devices by JAX's collectives and lax.ppermute only.
A program may use at most 64 MiB of HBM per device.

v0:
```python
import math

import jax
import jax.numpy as jnp
from jax import lax
from jax.sharding import PartitionSpec as P

KEY_VALUE_HEADS = 8
HEAD_SIZE = 128


NEGATIVE_FILLER = -1e30


def heads_view(row_block_size):
    return row_block_size.reshape(
        row_block_size.shape[0], row_block_size.shape[1], KEY_VALUE_HEADS, -1, HEAD_SIZE
    )


def split_pairs(paired_block):
    leading_shape = paired_block.shape[:-2]
    return (
        paired_block[..., 0, :].reshape(leading_shape + (KEY_VALUE_HEADS, HEAD_SIZE)),
        paired_block[..., 1, :].reshape(leading_shape + (KEY_VALUE_HEADS, HEAD_SIZE)),
    )


def softmax_parts(scores):
    largest = jnp.max(scores, axis=-1)
    weights = jnp.exp(scores - largest[..., None]).astype(jnp.bfloat16)
    totals = jnp.sum(weights.astype(jnp.float32), axis=-1)
    return (largest, weights, totals)


def context_state(queries_block, shared_keys, shared_values, tab_keys, tab_values):
    shared_scores = jnp.einsum(
        "rtkgd,pkd->rtkgp", queries_block, shared_keys, preferred_element_type=jnp.float32
    )
    tab_scores = jnp.einsum(
        "rtkgd,rnkd->rtkgn", queries_block, tab_keys, preferred_element_type=jnp.float32
    )
    scores = jnp.concatenate([shared_scores, tab_scores], axis=-1) * HEAD_SIZE ** (-0.5)
    largest, weights, totals = softmax_parts(scores)
    shared_rows = shared_keys.shape[0]
    summed = jnp.einsum(
        "rtkgp,pkd->rtkgd",
        weights[..., :shared_rows],
        shared_values,
        preferred_element_type=jnp.float32,
    )
    summed = summed + jnp.einsum(
        "rtkgn,rnkd->rtkgd",
        weights[..., shared_rows:],
        tab_values,
        preferred_element_type=jnp.float32,
    )
    return (largest, totals, summed)


def suffix_state(queries_block, suffix_key_value, lengths, token_keys, token_values):
    cache_keys, cache_values = split_pairs(suffix_key_value)
    session_list, step_list = (token_keys.shape[0], token_keys.shape[1])
    newest_keys = token_keys.reshape(session_list, step_list, KEY_VALUE_HEADS, HEAD_SIZE)
    newest_values = token_values.reshape(session_list, step_list, KEY_VALUE_HEADS, HEAD_SIZE)
    cache_scores = jnp.einsum(
        "rtkgd,rnkd->rtkgn", queries_block, cache_keys, preferred_element_type=jnp.float32
    )
    fresh_scores = jnp.einsum(
        "rtkgd,rukd->rtkgu", queries_block, newest_keys, preferred_element_type=jnp.float32
    )
    scores = jnp.concatenate([cache_scores, fresh_scores], axis=-1) * HEAD_SIZE ** (-0.5)
    slots_cache = cache_keys.shape[1]
    cache_valid = jnp.arange(slots_cache, dtype=jnp.int32)[None, :] < lengths[:, None]
    steps_index = jnp.arange(step_list, dtype=jnp.int32)
    fresh_valid = steps_index[None, :] <= steps_index[:, None]
    valid = jnp.concatenate(
        [
            jnp.broadcast_to(cache_valid[:, None, :], (session_list, step_list, slots_cache)),
            fresh_valid[None],
        ],
        axis=-1,
    )
    scores = jnp.where(valid[:, :, None, None, :], scores, NEGATIVE_FILLER)
    largest, weights, totals = softmax_parts(scores)
    summed = jnp.einsum(
        "rtkgn,rnkd->rtkgd",
        weights[..., :slots_cache],
        cache_values,
        preferred_element_type=jnp.float32,
    )
    summed = summed + jnp.einsum(
        "rtkgu,rukd->rtkgd",
        weights[..., slots_cache:],
        newest_values,
        preferred_element_type=jnp.float32,
    )
    return (largest, totals, summed)


def combine_states(earlier, later):
    largest = jnp.maximum(earlier[0], later[0])
    weight_one = jnp.exp(earlier[0] - largest)
    weight_two = jnp.exp(later[0] - largest)
    return (
        largest,
        earlier[1] * weight_one + later[1] * weight_two,
        earlier[2] * weight_one[..., None] + later[2] * weight_two[..., None],
    )


def shards(
    queries,
    prefix_key_value,
    tab_key_value,
    tab_owner,
    session_tab,
    suffix_key_value,
    suffix_len,
    token_keys,
    token_values,
):
    session_list = queries.shape[0]
    ctx_count = lax.axis_size("ctx")
    table_index = jnp.arange(tab_owner.shape[0], dtype=jnp.int32)
    matches = session_tab[:, None] == table_index[None, :]
    owner_slot = jnp.sum(jnp.where(matches, tab_owner[None, :], 0), axis=1)
    all_queries, slot_wire = (
        lax.all_gather(queries, "ctx", axis=0, tiled=True),
        lax.all_gather(owner_slot.astype(jnp.bfloat16), "ctx", axis=0, tiled=True),
    )
    all_slots = slot_wire.astype(jnp.int32)
    tab_blocks = lax.all_gather(tab_key_value, "tab", axis=0, tiled=True)
    shared_keys, shared_values = split_pairs(prefix_key_value)
    query_head_count = heads_view(all_queries)
    total_rows = query_head_count.shape[0]
    block_rows = math.gcd(total_rows, 8)

    def one_block(packed):
        queries_block, slot_block = packed
        tab_keys, tab_values = split_pairs(jnp.take(tab_blocks, slot_block, axis=0))
        return context_state(queries_block, shared_keys, shared_values, tab_keys, tab_values)

    grouped = lax.map(
        one_block,
        (
            query_head_count.reshape(
                (total_rows // block_rows, block_rows) + query_head_count.shape[1:]
            ),
            all_slots.reshape(total_rows // block_rows, block_rows),
        ),
    )
    partial_value = jax.tree.map(
        lambda part_array: part_array.reshape((ctx_count, session_list) + part_array.shape[2:]),
        grouped,
    )
    received = (
        lax.all_to_all(partial_value[0], "ctx", split_axis=0, concat_axis=0, tiled=True),
        lax.all_to_all(partial_value[1], "ctx", split_axis=0, concat_axis=0, tiled=True),
        lax.all_to_all(partial_value[2], "ctx", split_axis=0, concat_axis=0, tiled=True),
    )
    largest = jnp.max(received[0], axis=0)
    scaling = jnp.exp(received[0] - largest[None])
    state = (
        largest,
        jnp.sum(received[1] * scaling, axis=0),
        jnp.sum(received[2] * scaling[..., None], axis=0),
    )
    local_state = suffix_state(
        heads_view(queries), suffix_key_value, suffix_len, token_keys, token_values
    )
    merged = combine_states(state, local_state)
    result = merged[2] / merged[1][..., None]
    return result.reshape(session_list, queries.shape[1], queries.shape[2]).astype(jnp.bfloat16)


def solution(mesh):
    placed = (
        P(("ctx", "tab"), None, None),
        P("ctx", None, None),
        P("tab", "ctx", None, None),
        P(),
        P(("ctx", "tab")),
        P(("ctx", "tab"), None, None, None),
        P(("ctx", "tab")),
        P(("ctx", "tab"), None, None),
        P(("ctx", "tab"), None, None),
    )
    return jax.shard_map(
        shards, mesh=mesh, in_specs=placed, out_specs=P(("ctx", "tab"), None, None), check_vma=False
    )
```

profile of v0, /device:TPU:0, one launch (start us, length us, event | category | flops | bytes accessed | tf_op | source)
XLA Modules:
  0.0 130.4 jit_solution(10720035247611196357)
XLA Ops:
  7.3 1.4 %fusion.32 = s32[]{:T(128)} fusion(s32[4]{0:T(128)} %param.12, s32[]{:T(128)} %bitcast.145), kind=kLoop, calls=%fused_computation.59 | loop fusion | flops 11 | bytes 24 | tf_op jit(solution)/shard_map/reduce_sum | solution.py:127
  9.4 1.7 %copy.70 = bf16[1,64,2,1024]{3,1,2,0:T(8,128)(2,1)} copy(bf16[1,64,2,1024]{3,2,1,0:T(2,128)(2,1)} %param.11) | data formatting | bytes 524288 | tf_op args[2]
  11.1 1.3 %dynamic-slice.1 = u32[1]{0:T(128)} dynamic-slice(u32[32]{0:T(128)} %constant.59, u32[]{:T(128)S(6)} %add.43), dynamic_slice_sizes={1} | dynamic-slice | bytes 12
  12.4 0.8 dynamic-update-slice
  13.3 18.1 %all-reduce = bf16[8]{0:T(256)(128)(2,1)S(1)} all-reduce(bf16[8]{0:T(256)(128)(2,1)S(1)} %dynamic-update-slice), channel_id=1, replica_groups=mesh['ctx'=8,'tab'=4] {'ctx'}, use_global_device_ids=true, to_apply=%add | all-reduce | flops 8 | bytes 32
  31.4 15.1 %all_gather.9 = bf16[8,4,8192]{2,1,0:T(4,128)(2,1)S(1)} all-gather(bf16[1,4,8192]{2,1,0:T(4,128)(2,1)} %param.9), channel_id=1, replica_groups=mesh['ctx'=8,'tab'=4] {'ctx'}, dimensions={0}, use_global_device_ids=true | all-gather | bytes 589824 | tf_op jit(solution)/shard_map/all_gather | solution.py:129
  47.0 4.2 %fusion.35 = (bf16[512,1,1024]{2,1,0:T(2,128)(2,1)}, bf16[512,1,1024]{2,1,0:T(2,128)(2,1)}) fusion(bf16[512,2,1024]{2,1,0:T(2,128)(2,1)S(1)} %copy-done.2), kind=kLoop, calls=%fused_computation.60 | loop fusion | bytes 4194304 | tf_op jit(solution)/shard_map/slice | solution.py:25
  51.2 6.0 %copy.116 = bf16[512,1,1024]{0,2,1:T(8,128)(2,1)} copy(bf16[512,1,1024]{2,1,0:T(2,128)(2,1)} %get-tuple-element.38) | data formatting | bytes 2097152
  57.2 4.2 %copy.115 = bf16[512,1,1024]{0,2,1:T(8,128)(2,1)} copy(bf16[512,1,1024]{2,1,0:T(2,128)(2,1)S(1)} %copy-done.3) | data formatting | bytes 2097152
  61.4 3.8 %convolution_bitcast_fusion = f32[8,4,8,8,512]{4,3,1,0,2:T(8,128)} fusion(bf16[512,8,128,1,1]{0,2,4,3,1:T(8,128)(2,1)} %bitcast.152, bf16[8,4,8,8,128]{4,3,2,1,0:T(8,128)(2,1)S(1)} %reshape.298), kind=kOutput, calls=%fused_computation.5 | convolution fusion | flops 268435456 | bytes 5767168 | tf_op jit(solution)/shard_map/while/body/eval_jaxpr/rtkgd,pkd->rtkgp/dot_general | solution.py:37
  65.3 1.9 %gather_fusion = bf16[8,64,2,1024]{3,1,2,0:T(8,128)(2,1)S(1)} fusion(bf16[4,64,2,1024]{3,1,2,0:T(8,128)(2,1)} %all-gather.2.cloned.1.call-done, s32[1024]{0:T(1024)S(1)} %pad_clamp_fusion), kind=kCustom, calls=%fused_computation | custom fusion | bytes 4194336 | tf_op jit(solution)/shard_map/while/body/eval_jaxpr/jit(_take)/gather | solution.py:141
  68.0 0.7 convolution_bitcast_fusion.2
  68.7 1.5 %copy-done.1 = f32[8,4,8,8,512]{4,3,1,0,2:T(8,128)S(1)} copy-done((f32[8,4,8,8,512]{4,3,1,0,2:T(8,128)S(1)}, f32[8,4,8,8,512]{4,3,1,0,2:T(8,128)}, u32[]{:S(2)}) %copy-start.1) | copy-done | bytes 4194328
  70.7 1.5 %convert_reduce_fusion = (f32[8,4,8,8]{3,1,0,2:T(4,128)S(1)}, bf16[8,4,8,8,576]{4,3,1,0,2:T(8,128)(2,1)S(1)}) fusion(f32[8,4,8,8]{3,1,0,2:T(4,128)S(1)} %fusion, f32[8,4,8,8,64]{4,3,1,0,2:T(8,128)S(1)} %convolution_bitcast_fusion.2, f32[8,4,8,8,512]{4,3,1,0,2:T(8,128)S(1)} %copy-done.1), kind=kLoop, calls=%fused_computation.2 | loop fusion | flops 7075840 | bytes 7094272 | tf_op jit(solution)/shard_map/while/body/eval_jaxpr/reduce_sum | solution.py:32
  72.5 1.1 bitcast_bitcast_fusion
  73.6 0.8 reshape.300
  74.4 3.3 %all-to-all-start.1 = ((f32[8,1,256]{2,1,0:T(1,128)}), f32[8,1,256]{2,1,0:T(1,128)S(1)}, u32[]{:S(2)}, u32[]{:S(2)}) async-start(f32[8,1,256]{2,1,0:T(1,128)} %reshape.300), calls=%async_computation.1 | async-start | bytes 16384 | tf_op jit(solution)/shard_map/all_to_all | solution.py:158
  77.8 2.6 %convolution_bitcast_fusion.1 = f32[8,4,8,8,128]{4,3,1,0,2:T(8,128)} fusion(bf16[8,64,8,128,1]{3,2,1,0,4:T(8,128)(2,1)} %bitcast_bitcast_fusion, bf16[8,4,8,8,576]{4,3,1,0,2:T(8,128)(2,1)S(1)} %get-tuple-element.25), kind=kOutput, calls=%fused_computation.12 | convolution fusion | flops 33554432 | bytes 2621440 | tf_op jit(solution)/shard_map/while/body/eval_jaxpr/rtkgn,rnkd->rtkgd/dot_general | solution.py:52
  80.4 0.8 reshape.302
  81.2 2.1 %all-to-all-done.1 = f32[8,1,256]{2,1,0:T(1,128)S(1)} async-done(((f32[8,1,256]{2,1,0:T(1,128)}), f32[8,1,256]{2,1,0:T(1,128)S(1)}, u32[]{:S(2)}, u32[]{:S(2)}) %all-to-all-start.1) | async-done | bytes 8224 | tf_op jit(solution)/shard_map/all_to_all | solution.py:158
  83.3 3.3 %all-to-all-start.2 = ((f32[8,1,256]{2,1,0:T(1,128)}), f32[8,1,256]{2,1,0:T(1,128)S(1)}, u32[]{:S(2)}, u32[]{:S(2)}) async-start(f32[8,1,256]{2,1,0:T(1,128)} %reshape.302), calls=%async_computation.2 | async-start | bytes 16384 | tf_op jit(solution)/shard_map/all_to_all | solution.py:159
  86.6 2.3 %fusion.9 = f32[8,1,4,8,8,128]{5,4,2,0,3,1:T(8,128)S(1)} fusion(f32[8,4,8,8,128]{4,3,1,0,2:T(8,128)} %convolution_bitcast_fusion.1, bf16[512,8,128,1,1]{0,2,4,3,1:T(8,128)(2,1)} %bitcast.147, bf16[8,4,8,8,576]{4,3,1,0,2:T(8,128)(2,1)S(1)} %get-tuple-element.25), kind=kOutput, calls=%fused_computation.11 | convolution fusion | flops 268697600 | bytes 5242880 | tf_op jit(solution)/shard_map/while/body/eval_jaxpr/rtkgp,pkd->rtkgd/dot_general | solution.py:46
  88.9 1.1 copy.76
  90.0 2.2 %all-to-all-done.2 = f32[8,1,256]{2,1,0:T(1,128)S(1)} async-done(((f32[8,1,256]{2,1,0:T(1,128)}), f32[8,1,256]{2,1,0:T(1,128)S(1)}, u32[]{:S(2)}, u32[]{:S(2)}) %all-to-all-start.2) | async-done | bytes 8224 | tf_op jit(solution)/shard_map/all_to_all | solution.py:159
  92.2 3.6 %all-to-all-start = ((f32[8,1,4,8,8,128]{5,4,2,3,1,0:T(8,128)}), f32[8,1,4,8,8,128]{5,4,2,3,1,0:T(8,128)S(1)}, u32[]{:S(2)}, u32[]{:S(2)}) async-start(f32[8,1,4,8,8,128]{5,4,2,3,1,0:T(8,128)} %copy.76), calls=%async_computation | async-start | bytes 2097152 | tf_op jit(solution)/shard_map/all_to_all | solution.py:160
  95.7 2.3 %fusion.37 = (bf16[1,256,1,1024]{3,2,1,0:T(2,128)(2,1)}, bf16[1,256,1,1024]{3,2,1,0:T(2,128)(2,1)S(1)}) fusion(bf16[1,256,2,1024]{3,2,1,0:T(2,128)(2,1)S(1)} %copy-done.4), kind=kLoop, calls=%fused_computation.62 | loop fusion | bytes 2097152 | tf_op jit(solution)/shard_map/slice | solution.py:25
  98.7 2.3 %copy.118 = bf16[1,256,1,1024]{1,3,2,0:T(8,128)(2,1)S(1)} copy(bf16[1,256,1,1024]{3,2,1,0:T(2,128)(2,1)} %get-tuple-element.43) | data formatting | bytes 1048576
  101.1 2.0 %copy.117 = bf16[1,256,1,1024]{1,3,2,0:T(8,128)(2,1)} copy(bf16[1,256,1,1024]{3,2,1,0:T(2,128)(2,1)S(1)} %get-tuple-element.44) | data formatting | bytes 1048576
  103.2 1.2 convolution_bitcast_fusion.3
  105.5 0.7 reduce.7
  106.4 0.7 reduce.8
  107.4 14.8 %all-to-all-done = f32[8,1,4,8,8,128]{5,4,2,3,1,0:T(8,128)S(1)} async-done(((f32[8,1,4,8,8,128]{5,4,2,3,1,0:T(8,128)}), f32[8,1,4,8,8,128]{5,4,2,3,1,0:T(8,128)S(1)}, u32[]{:S(2)}, u32[]{:S(2)}) %all-to-all-start) | async-done | bytes 1048608 | tf_op jit(solution)/shard_map/all_to_all | solution.py:160
  (47 shorter events, 5.3 us)
Async XLA Ops:
  6.5 98.3 %copy-start = (bf16[1,4,1024]{2,1,0:T(4,128)(2,1)S(1)}, bf16[1,4,1024]{2,1,0:T(4,128)(2,1)}, u32[]{:S(2)}) copy-start(bf16[1,4,1024]{2,1,0:T(4,128)(2,1)} %param.17) | copy-start | bytes 24580
  6.5 40.5 %copy-start.2 = (bf16[512,2,1024]{2,1,0:T(2,128)(2,1)S(1)}, bf16[512,2,1024]{2,1,0:T(2,128)(2,1)}, u32[]{:S(2)}) copy-start(bf16[512,2,1024]{2,1,0:T(2,128)(2,1)} %param.10) | copy-start | bytes 6291460
  6.5 58.7 %all-gather.2.cloned.1.call-start = ((), (), s32[]{:S(2)}) async-start(), calls=%async_computation.3 | async-start | bytes 1310720 | tf_op jit(solution)/shard_map/all_gather | solution.py:133
  51.2 6.0 %copy-start.3 = (bf16[512,1,1024]{2,1,0:T(2,128)(2,1)S(1)}, bf16[512,1,1024]{2,1,0:T(2,128)(2,1)}, u32[]{:S(2)}) copy-start(bf16[512,1,1024]{2,1,0:T(2,128)(2,1)} %get-tuple-element.40) | copy-start | bytes 3145732
  68.0 2.2 %copy-start.1 = (f32[8,4,8,8,512]{4,3,1,0,2:T(8,128)S(1)}, f32[8,4,8,8,512]{4,3,1,0,2:T(8,128)}, u32[]{:S(2)}) copy-start(f32[8,4,8,8,512]{4,3,1,0,2:T(8,128)} %convolution_bitcast_fusion) | copy-start | bytes 12582916
  74.4 8.9 %all-to-all-start.1 = ((f32[8,1,256]{2,1,0:T(1,128)}), f32[8,1,256]{2,1,0:T(1,128)S(1)}, u32[]{:S(2)}, u32[]{:S(2)}) async-start(f32[8,1,256]{2,1,0:T(1,128)} %reshape.300), calls=%async_computation.1 | async-start | bytes 16384 | tf_op jit(solution)/shard_map/all_to_all | solution.py:158
  83.3 8.9 %all-to-all-start.2 = ((f32[8,1,256]{2,1,0:T(1,128)}), f32[8,1,256]{2,1,0:T(1,128)S(1)}, u32[]{:S(2)}, u32[]{:S(2)}) async-start(f32[8,1,256]{2,1,0:T(1,128)} %reshape.302), calls=%async_computation.2 | async-start | bytes 16384 | tf_op jit(solution)/shard_map/all_to_all | solution.py:159
  88.9 6.8 %copy-start.4 = (bf16[1,256,2,1024]{3,2,1,0:T(2,128)(2,1)S(1)}, bf16[1,256,2,1024]{3,2,1,0:T(2,128)(2,1)}, u32[]{:S(2)}) copy-start(bf16[1,256,2,1024]{3,2,1,0:T(2,128)(2,1)} %param.14) | copy-start | bytes 3145732
  92.2 30.1 %all-to-all-start = ((f32[8,1,4,8,8,128]{5,4,2,3,1,0:T(8,128)}), f32[8,1,4,8,8,128]{5,4,2,3,1,0:T(8,128)S(1)}, u32[]{:S(2)}, u32[]{:S(2)}) async-start(f32[8,1,4,8,8,128]{5,4,2,3,1,0:T(8,128)} %copy.76), calls=%async_computation | async-start | bytes 2097152 | tf_op jit(solution)/shard_map/all_to_all | solution.py:160
  98.0 5.0 %copy-start.5 = (bf16[1,4,8192]{2,1,0:T(4,128)(2,1)S(1)}, bf16[1,4,8192]{2,1,0:T(4,128)(2,1)}, u32[]{:S(2)}) copy-start(bf16[1,4,8192]{2,1,0:T(4,128)(2,1)} %param.9) | copy-start | bytes 196612
  98.0 5.0 %copy-start.6 = (bf16[1,4,1024]{2,1,0:T(4,128)(2,1)S(1)}, bf16[1,4,1024]{2,1,0:T(4,128)(2,1)}, u32[]{:S(2)}) copy-start(bf16[1,4,1024]{2,1,0:T(4,128)(2,1)} %param.16) | copy-start | bytes 24580
Sparse Core Ops, SparseCore 0:
  13.4 29.3 all-gather.1
where the time goes:
time: 131 us; the launch traced here: 130 us
  local copies, waits for them, and re-layouts  34.9 us (27%)
  blocking collectives  33.2 us (25%)
  waiting for transfers between devices  19.1 us (15%)
  between operations  15.8 us (12%)
  matrix products  11.2 us (9%)
  starting transfers between devices  10.2 us (8%)
  other arithmetic  5.95 us (5%)
    unnamed x30, local copies, waits for them, and re-layouts  22.3 us
    unnamed x1, blocking collectives  18.1 us
    all_gather x1, blocking collectives, shards(): lax.all_gather(queries, 'ctx', axis=0, tiled=True)  15.1 us
    all_to_all x1, waiting for transfers between devices, shards(): lax.all_to_all(partial_value[2], 'ctx', split_axis=0, concat_axis=0, tile...  14.8 us
    slice x2, local copies, waits for them, and re-layouts, split_pairs(): paired_block[..., 1, :]  6.52 us
    dot_general x1, matrix products, context_state(): jnp.einsum('rtkgd,pkd->rtkgp', queries_block, shared_keys, preferred_elem...  3.84 us
    all_to_all x1, starting transfers between devices, shards(): lax.all_to_all(partial_value[2], 'ctx', split_axis=0, concat_axis=0, tile...  3.56 us
    all_to_all x1, starting transfers between devices, shards(): lax.all_to_all(partial_value[0], 'ctx', split_axis=0, concat_axis=0, tile...  3.33 us
  transfers between devices with their start and end apart: 4, of which 3 were waited for; matrix products, arithmetic and copies ran while one was open for 28% of the time, Pallas kernels for 0%

commit v1 on v0

v1 whole, which is shorter than its diff:
```python
import functools

import jax
import jax.numpy as jnp
from jax import lax
from jax.experimental import pallas as pl
from jax.experimental.pallas import tpu as pltpu
from jax.sharding import PartitionSpec as P

KEY_VALUE_HEADS = 8
HEAD_SIZE = 128
SCALE = HEAD_SIZE**-0.5
FILLER = -1e30
VMEM_LIMIT = 56 * 1024 * 1024
CODE_TOP = 32000.0
REST_TOP = 65000.0

NT = (((1,), (1,)), ((), ()))


def head_lanes(h):
    return pl.ds(h * HEAD_SIZE, HEAD_SIZE)


def put_lane(slab, lane, column):
    at = lax.broadcasted_iota(jnp.int32, slab.shape, 1)
    return jnp.where(at == lane, column, slab)


def block_softmax(score_parts, value_parts):
    largest = functools.reduce(
        jnp.maximum, [jnp.max(s, axis=-1, keepdims=True) for s in score_parts]
    )
    total, summed = 0.0, 0.0
    for scores, values in zip(score_parts, value_parts):
        weights = jnp.exp(scores - largest).astype(jnp.bfloat16)
        total += jnp.sum(weights.astype(jnp.float32), axis=-1, keepdims=True)
        summed += jnp.dot(weights, values, preferred_element_type=jnp.float32)
    return summed / total, largest + jnp.log(total)


def context_kernel(members, slots, key_ref, value_ref, column_slot_ref, *refs):
    query_refs, tab_refs, out_ref = refs[:members], refs[members : members + slots], refs[-1]
    rows = query_refs[0].shape[1]
    owner = jnp.concatenate([q[KEY_VALUE_HEADS, :, 0:1] for q in query_refs], axis=0)
    mine = owner.astype(jnp.float32) == column_slot_ref[0:1, :]
    ends = jnp.zeros((members * rows, HEAD_SIZE), jnp.float32)
    for h in range(KEY_VALUE_HEADS):
        at = head_lanes(h)
        query = jnp.concatenate([q[h] for q in query_refs], axis=0)
        tab_keys = jnp.concatenate([t[0, :, at] for t in tab_refs], axis=0)
        tab_values = jnp.concatenate([t[1, :, at] for t in tab_refs], axis=0)
        shared = lax.dot_general(query, key_ref[:, at], NT, preferred_element_type=jnp.float32)
        tab = lax.dot_general(query, tab_keys, NT, preferred_element_type=jnp.float32)
        tab = jnp.where(mine, tab * SCALE, FILLER)
        mean, end = block_softmax([shared * SCALE, tab], [value_ref[:, at], tab_values])
        for i in range(members):
            out_ref[i, h] = mean[i * rows : (i + 1) * rows]
        ends = put_lane(ends, h, end)
    for i in range(members):
        out_ref[i, KEY_VALUE_HEADS] = ends[i * rows : (i + 1) * rows]


def context_states(query_messages, keys, values, column_slot, tabs):
    members, rows = len(query_messages), query_messages[0].shape[1]
    key_count = keys.shape[0] + column_slot.shape[1]
    work = members * rows * KEY_VALUE_HEADS * key_count
    return pl.pallas_call(
        functools.partial(context_kernel, members, len(tabs)),
        out_shape=jax.ShapeDtypeStruct(
            (members, KEY_VALUE_HEADS + 1, rows, HEAD_SIZE), jnp.float32
        ),
        compiler_params=pltpu.CompilerParams(vmem_limit_bytes=VMEM_LIMIT),
        cost_estimate=pl.CostEstimate(
            flops=4 * work * HEAD_SIZE, transcendentals=work, bytes_accessed=4 * keys.size
        ),
        name="context_states",
    )(keys, values, column_slot, *query_messages, *tabs)


def suffix_kernel(steps, length_ref, query_ref, key_ref, value_ref, new_key_ref, new_value_ref, out_ref):
    rows, slots = query_ref.shape[1], key_ref.shape[0]
    used = lax.broadcasted_iota(jnp.int32, (rows, slots), 1) < length_ref[0]
    step = lax.rem(lax.broadcasted_iota(jnp.int32, (rows, steps), 0), steps)
    seen = lax.broadcasted_iota(jnp.int32, (rows, steps), 1) <= step
    ends = jnp.zeros((rows, HEAD_SIZE), jnp.float32)
    for h in range(KEY_VALUE_HEADS):
        at = head_lanes(h)
        query = query_ref[h]
        cached = lax.dot_general(query, key_ref[:, at], NT, preferred_element_type=jnp.float32)
        fresh = lax.dot_general(query, new_key_ref[:, at], NT, preferred_element_type=jnp.float32)
        cached = jnp.where(used, cached * SCALE, FILLER)
        fresh = jnp.where(seen, fresh * SCALE, FILLER)
        mean, end = block_softmax([cached, fresh], [value_ref[:, at], new_value_ref[:, at]])
        out_ref[h] = mean
        ends = put_lane(ends, h, end)
    out_ref[KEY_VALUE_HEADS] = ends


def suffix_state(query_message, cache_keys, cache_values, length, new_keys, new_values):
    rows, steps = query_message.shape[1], new_keys.shape[0]
    work = rows * KEY_VALUE_HEADS * cache_keys.shape[0]
    whole = pl.BlockSpec(memory_space=pltpu.VMEM)
    return pl.pallas_call(
        functools.partial(suffix_kernel, steps),
        in_specs=[pl.BlockSpec(memory_space=pltpu.SMEM)] + [whole] * 5,
        out_specs=whole,
        out_shape=jax.ShapeDtypeStruct((KEY_VALUE_HEADS + 1, rows, HEAD_SIZE), jnp.float32),
        compiler_params=pltpu.CompilerParams(vmem_limit_bytes=VMEM_LIMIT),
        cost_estimate=pl.CostEstimate(
            flops=4 * work * HEAD_SIZE, transcendentals=work, bytes_accessed=4 * cache_keys.size
        ),
        name="suffix_state",
    )(length, query_message, cache_keys, cache_values, new_keys, new_values)


def merge(parts):
    top = functools.reduce(jnp.maximum, [end for _, end in parts])
    shares = [jnp.exp(end - top) for _, end in parts]
    total = functools.reduce(jnp.add, shares)
    summed = functools.reduce(jnp.add, [mean * share for (mean, _), share in zip(parts, shares)])
    return summed / total, top + jnp.log(total)


def power(exponent):
    return jnp.exp2(exponent)


def pair_kernel(own_ref, other_ref, home_ref, *coded_refs):
    rows = own_ref.shape[2]
    for i in range(own_ref.shape[0]):
        slab = jnp.zeros((rows, HEAD_SIZE), jnp.float32)
        for h in range(KEY_VALUE_HEADS):
            mean, end = merge(
                [(r[i, h], r[i, KEY_VALUE_HEADS, :, h : h + 1]) for r in (own_ref, other_ref)]
            )
            if i == 0:
                home_ref[h] = mean
                slab = put_lane(slab, h, end)
                continue
            reach = jnp.max(jnp.abs(mean), axis=-1, keepdims=True)
            exponent = jnp.ceil(jnp.log2(jnp.maximum(reach, 1e-30)))
            code = jnp.round(mean * (power(-exponent) * CODE_TOP))
            coded_refs[i - 1][h] = code.astype(jnp.int32).astype(jnp.int16)
            near = jnp.round(end)
            slab = put_lane(slab, h, near)
            slab = put_lane(slab, KEY_VALUE_HEADS + h, jnp.round((end - near) * REST_TOP))
            slab = put_lane(slab, 2 * KEY_VALUE_HEADS + h, exponent)
        if i == 0:
            home_ref[KEY_VALUE_HEADS] = slab
        else:
            coded_refs[i - 1][KEY_VALUE_HEADS] = slab.astype(jnp.int32).astype(jnp.int16)


def pair_states(own, other):
    members, shape = own.shape[0], own.shape[1:]
    return pl.pallas_call(
        pair_kernel,
        out_shape=[jax.ShapeDtypeStruct(shape, jnp.float32)]
        + [jax.ShapeDtypeStruct(shape, jnp.int16)] * (members - 1),
        compiler_params=pltpu.CompilerParams(vmem_limit_bytes=VMEM_LIMIT),
        name="pair_states",
    )(own, other)


def final_kernel(suffix_ref, home_ref, *refs):
    coded_refs, out_ref = refs[:-1], refs[-1]
    steps = out_ref.shape[0]
    groups = suffix_ref.shape[1] // steps
    slabs = [r[KEY_VALUE_HEADS].astype(jnp.int32).astype(jnp.float32) for r in coded_refs]
    for h in range(KEY_VALUE_HEADS):
        parts = [(r[h], r[KEY_VALUE_HEADS, :, h : h + 1]) for r in (suffix_ref, home_ref)]
        for r, slab in zip(coded_refs, slabs):
            near, rest, exponent = (
                slab[:, k * KEY_VALUE_HEADS + h : k * KEY_VALUE_HEADS + h + 1] for k in range(3)
            )
            code = r[h].astype(jnp.int32).astype(jnp.float32)
            parts.append((code * (power(exponent) / CODE_TOP), near + rest / REST_TOP))
        mean, _ = merge(parts)
        for g in range(groups):
            out_ref[:, head_lanes(h * groups + g)] = mean[g * steps : (g + 1) * steps].astype(
                jnp.bfloat16
            )


def final_output(suffix, home, coded, steps):
    width = suffix.shape[1] // steps * KEY_VALUE_HEADS * HEAD_SIZE
    return pl.pallas_call(
        final_kernel,
        out_shape=jax.ShapeDtypeStruct((steps, width), jnp.bfloat16),
        compiler_params=pltpu.CompilerParams(vmem_limit_bytes=VMEM_LIMIT),
        name="final_output",
    )(suffix, home, *coded)


def swap(count, bit):
    return [(i, i ^ bit) for i in range(count)]


def shards(
    queries,
    prefix_key_value,
    tab_key_value,
    tab_owner,
    session_tab,
    suffix_key_value,
    suffix_len,
    token_keys,
    token_values,
):
    ctx_count, tab_count = lax.axis_size("ctx"), lax.axis_size("tab")
    pair_count = ctx_count // 2
    steps = queries.shape[1]
    tab_rows = tab_key_value.shape[1]

    tab_block = jnp.stack([tab_key_value[0, :, 0], tab_key_value[0, :, 1]])
    tabs = [tab_block] + [
        lax.ppermute(tab_block, "tab", swap(tab_count, k)) for k in range(1, tab_count)
    ]
    places = jnp.arange(tab_count * tab_rows, dtype=jnp.int32) // tab_rows
    column_slot = (places ^ lax.axis_index("tab")).astype(jnp.float32)[None]

    table = jnp.arange(tab_owner.shape[0], dtype=jnp.int32)
    slot = jnp.sum(jnp.where(session_tab[0] == table, tab_owner, 0))
    query = queries[0].reshape(steps, KEY_VALUE_HEADS, -1, HEAD_SIZE)
    query = query.transpose(1, 2, 0, 3).reshape(KEY_VALUE_HEADS, -1, HEAD_SIZE)
    slot_slab = jnp.broadcast_to(slot.astype(jnp.bfloat16), (1,) + query.shape[1:])
    message = jnp.concatenate([query, slot_slab], axis=0)
    column = [message] + [
        lax.ppermute(message, "ctx", swap(ctx_count, 2 * k)) for k in range(1, pair_count)
    ]
    other_column = [lax.ppermute(m, "ctx", swap(ctx_count, 1)) for m in column]

    keys, values = prefix_key_value[:, 0], prefix_key_value[:, 1]
    suffix = suffix_state(
        message,
        suffix_key_value[0, :, 0],
        suffix_key_value[0, :, 1],
        suffix_len,
        token_keys[0],
        token_values[0],
    )
    other = context_states(other_column, keys, values, column_slot, tabs)
    own = context_states(column, keys, values, column_slot, tabs)
    home, *coded = pair_states(own, lax.ppermute(other, "ctx", swap(ctx_count, 1)))
    received = [
        lax.ppermute(c, "ctx", swap(ctx_count, 2 * k)) for k, c in enumerate(coded, start=1)
    ]
    return final_output(suffix, home, received, steps)[None]


def solution(mesh):
    sessions = ("ctx", "tab")
    placed = (
        P(sessions, None, None),
        P("ctx", None, None),
        P("tab", "ctx", None, None),
        P(),
        P(sessions),
        P(sessions, None, None, None),
        P(sessions),
        P(sessions, None, None),
        P(sessions, None, None),
    )
    return jax.shard_map(
        shards, mesh=mesh, in_specs=placed, out_specs=P(sessions, None, None), check_vma=False
    )
```

time: 131 us -> 58.9 us (0.45)
  blocking collectives: 33.2 us -> 0 us
  Pallas kernels: 0 us -> 23 us
  local copies, waits for them, and re-layouts: 34.9 us -> 12.7 us
  waiting for transfers between devices: 19.1 us -> 3.81 us
  between operations: 15.8 us -> 2.31 us
  matrix products: 11.2 us -> 0 us
  starting transfers between devices: 10.2 us -> 14.8 us
  other arithmetic: 5.95 us -> 1.96 us
    pallas_call x0 -> x5, Pallas kernels: none -> 23 us  [the longest x2 11 us: context_states(): pl.pallas_call(functools.partial(context_kernel, members, len(tabs)), out...]
    unnamed x30 -> x36, local copies, waits for them, and re-layouts: 22.3 us -> 2.26 us
    all_to_all x3 -> x0, waiting for transfers between devices: 19.1 us -> none  [the longest x1 14.8 us: shards(): lax.all_to_all(partial_value[2], 'ctx', split_axis=0, concat_axis=0, tile...]
    unnamed x1 -> x0, blocking collectives: 18.1 us -> none
    all_gather x1 -> x0, blocking collectives: 15.1 us -> none  [shards(): lax.all_gather(queries, 'ctx', axis=0, tiled=True)]
    ppermute x0 -> x14, starting transfers between devices: none -> 14.8 us  [the longest x3 5.62 us: shards(): lax.ppermute(message, 'ctx', swap(ctx_count, 2 * k))]
    dot_general x8 -> x0, matrix products: 11.2 us -> none  [the longest x1 3.84 us: context_state(): jnp.einsum('rtkgd,pkd->rtkgp', queries_block, shared_keys, preferred_elem...]
    all_to_all x3 -> x0, starting transfers between devices: 10.2 us -> none  [the longest x1 3.56 us: shards(): lax.all_to_all(partial_value[2], 'ctx', split_axis=0, concat_axis=0, tile...]
  transfers between devices with their start and end apart: 4 -> 14, of which waited for: 3 -> 3; matrix products, arithmetic and copies ran while one was open for 28% -> 17% of each run, Pallas kernels for 0% -> 16%
where the time goes in v1:
time: 58.9 us; the launch traced here: 58.6 us
  Pallas kernels  23 us (39%)
  starting transfers between devices  14.8 us (25%)
  local copies, waits for them, and re-layouts  12.7 us (22%)
  waiting for transfers between devices  3.81 us (6%)
  between operations  2.31 us (4%)
  other arithmetic  1.96 us (3%)
    pallas_call x2, Pallas kernels, context_states(): pl.pallas_call(functools.partial(context_kernel, members, len(tabs)), out...  11 us
    pallas_call x1, Pallas kernels, pair_states(): pl.pallas_call(pair_kernel, out_shape=[jax.ShapeDtypeStruct(shape, jnp.fl...  5.77 us
    ppermute x3, starting transfers between devices, shards(): lax.ppermute(message, 'ctx', swap(ctx_count, 2 * k))  5.62 us
    ppermute x3, starting transfers between devices, shards(): lax.ppermute(c, 'ctx', swap(ctx_count, 2 * k))  4.39 us
    pallas_call x1, Pallas kernels, suffix_state(): pl.pallas_call(functools.partial(suffix_kernel, steps), in_specs=[pl.Bloc...  4.09 us
    ppermute x3, starting transfers between devices, shards(): lax.ppermute(tab_block, 'tab', swap(tab_count, k))  3.62 us
    ppermute x3, waiting for transfers between devices, shards(): lax.ppermute(tab_block, 'tab', swap(tab_count, k))  3.42 us
    slice x1, local copies, waits for them, and re-layouts, shards(): keys, values = (prefix_key_value[:, 0], prefix_key_value[:, 1])  2.96 us
  transfers between devices with their start and end apart: 14, of which 3 were waited for; matrix products, arithmetic and copies ran while one was open for 17% of the time, Pallas kernels for 16%

profile of v1, /device:TPU:0, one launch (start us, length us, event | category | flops | bytes accessed | tf_op | source)
XLA Modules:
  0.0 58.6 jit_solution(10501583595651810862)
XLA Ops:
  0.8 1.4 %fusion.2 = s32[]{:T(128)} fusion(s32[4]{0:T(128)} %param.12, s32[]{:T(128)} %bitcast.21), kind=kLoop, calls=%fused_computation.14 | loop fusion | flops 11 | bytes 24 | tf_op jit(solution)/shard_map/reduce_sum | solution.py:224
  2.8 0.8 %concatenate.3.query_ref.refs_0_ = bf16[9,32,128]{2,1,0:T(8,128)(2,1)S(1)} pad(bf16[8,32,128]{2,1,0:T(8,128)(2,1)} %bitcast.22, bf16[]{:T(256)S(6)} %convert_element_type.13), padding=0_1x0_0x0_0 | pad | bytes 139266 | tf_op jit(solution)/shard_map/concatenate | solution.py:228
  3.7 3.0 %collective-permute-start = (bf16[9,32,128]{2,1,0:T(8,128)(2,1)S(1)}, bf16[9,32,128]{2,1,0:T(8,128)(2,1)S(1)}, u32[]{:S(2)}, u32[]{:S(2)}) collective-permute-start(bf16[9,32,128]{2,1,0:T(8,128)(2,1)S(1)} %concatenate.3.query_ref.refs_0_), channel_id=1, source_target_pairs={{0,8},{4,12},{8,0},{12,4},{16,24},{20,28},{24,16},{28,20},{1,9},{5... | collective-permute-start | bytes 221192 | tf_op jit(solution)/shard_map/ppermute | solution.py:230
  6.7 2.6 %collective-permute-start.1 = (bf16[9,32,128]{2,1,0:T(8,128)(2,1)S(1)}, bf16[9,32,128]{2,1,0:T(8,128)(2,1)S(1)}, u32[]{:S(2)}, u32[]{:S(2)}) collective-permute-start(bf16[9,32,128]{2,1,0:T(8,128)(2,1)S(1)} %concatenate.3.query_ref.refs_0_), channel_id=1, source_target_pairs={{0,16},{4,20},{8,24},{12,28},{16,0},{20,4},{24,8},{28,12},{1,17},{... | collective-permute-start | bytes 221192 | tf_op jit(solution)/shard_map/ppermute | solution.py:230
  9.3 1.5 %fusion.5 = (bf16[1,64,1,1024]{3,2,1,0:T(2,128)(2,1)S(1)}, bf16[1,64,1,1024]{3,2,1,0:T(2,128)(2,1)S(1)}) fusion(bf16[1,64,2,1024]{3,2,1,0:T(2,128)(2,1)} %param.11), kind=kLoop, calls=%fused_computation.17 | loop fusion | bytes 524288 | tf_op jit(solution)/shard_map/slice | solution.py:216
  10.8 0.1 copy_bitcast_fusion.4
  11.0 1.8 %collective-permute-start.3 = (bf16[2,64,1024]{2,1,0:T(8,128)(2,1)S(1)}, bf16[2,64,1024]{2,1,0:T(8,128)(2,1)S(1)}, u32[]{:S(2)}, u32[]{:S(2)}) collective-permute-start(bf16[2,64,1024]{2,1,0:T(8,128)(2,1)S(1)} %pad_maximum_fusion.refs_4_), channel_id=1, source_target_pairs={{0,1},{1,0},{2,3},{3,2},{4,5},{5,4},{6,7},{7,6},{8,9},{9,8},{10,11... | collective-permute-start | bytes 786440 | tf_op jit(solution)/shard_map/ppermute | solution.py:218
  12.8 1.5 %collective-permute-start.4 = (bf16[2,64,1024]{2,1,0:T(8,128)(2,1)S(1)}, bf16[2,64,1024]{2,1,0:T(8,128)(2,1)S(1)}, u32[]{:S(2)}, u32[]{:S(2)}) collective-permute-start(bf16[2,64,1024]{2,1,0:T(8,128)(2,1)S(1)} %pad_maximum_fusion.refs_4_), channel_id=1, source_target_pairs={{0,2},{1,3},{2,0},{3,1},{4,6},{5,7},{6,4},{7,5},{8,10},{9,11},{10,... | collective-permute-start | bytes 786440 | tf_op jit(solution)/shard_map/ppermute | solution.py:218
  14.3 3.0 %fusion.3 = (bf16[512,1,1024]{2,1,0:T(2,128)(2,1)S(1)}, bf16[512,1,1024]{2,1,0:T(2,128)(2,1)S(1)}) fusion(bf16[512,2,1024]{2,1,0:T(2,128)(2,1)S(1)} %copy-done), kind=kLoop, calls=%fused_computation.15 | loop fusion | bytes 4194304 | tf_op jit(solution)/shard_map/slice | solution.py:234
  17.3 0.3 collective-permute-start.5
  17.7 0.5 collective-permute-start.7
  18.2 2.2 %copy_bitcast_fusion = (bf16[512,1024]{1,0:T(8,128)(2,1)}, bf16[512,1024]{1,0:T(8,128)(2,1)}) fusion(bf16[512,1,1024]{2,1,0:T(2,128)(2,1)S(1)} %get-tuple-element.13, bf16[512,1,1024]{2,1,0:T(2,128)(2,1)S(1)} %get-tuple-element.14), kind=kLoop, calls=%fused_computation | loop fusion | bytes 4194304 | tf_op jit(solution)/shard_map/squeeze | solution.py:234
  20.4 0.1 collective-permute-start.8
  20.5 0.5 collective-permute-start.9
  21.0 0.6 fusion.1.column_slot_ref
  21.6 0.1 collective-permute-done.8.refs_2_
  21.7 0.2 collective-permute-done.9.refs_3_
  21.9 3.4 %collective-permute-done.4.refs_6_ = bf16[2,64,1024]{2,1,0:T(8,128)(2,1)S(1)} collective-permute-done((bf16[2,64,1024]{2,1,0:T(8,128)(2,1)S(1)}, bf16[2,64,1024]{2,1,0:T(8,128)(2,1)S(1)}, u32[]{:S(2)}, u32[]{:S(2)}) %collective-permute-start.4) | collective-permute-done | bytes 262176 | tf_op jit(solution)/shard_map/ppermute | solution.py:218
  25.4 0.6 %copy-done.4 = bf16[2,64,1024]{2,1,0:T(8,128)(2,1)} copy-done((bf16[2,64,1024]{2,1,0:T(8,128)(2,1)}, bf16[2,64,1024]{2,1,0:T(8,128)(2,1)S(1)}, u32[]{:S(2)}) %copy-start.4) | copy-done | bytes 262168
  26.1 0.1 copy-done.5
  26.2 5.5 %context_states.3 = f32[4,9,32,128]{3,2,1,0:T(8,128)} custom-call(bf16[512,1024]{1,0:T(8,128)(2,1)} %get-tuple-element.22.key_ref, bf16[512,1024]{1,0:T(8,128)(2,1)} %get-tuple-element.21.value_ref, f32[1,256]{1,0:T(1,128)} %fusion.1.column_slot_ref, bf16[9,32,128]{2,1,0:T(8,128)(2,1)} %copy-done.14, bf16[9,32,128]{2,1,0:T(8,128)(2,1)} %copy-done.15, ...), custom_call_target="tpu_custom_call" | custom-call | flops 402653184 | bytes 2097152 | tf_op jit(solution)/shard_map/context_states/pallas_call | solution.py:68
  31.6 1.5 %fusion.4 = (bf16[1,256,1,1024]{3,2,1,0:T(2,128)(2,1)S(1)}, bf16[1,256,1,1024]{3,2,1,0:T(2,128)(2,1)S(1)}) fusion(bf16[1,256,2,1024]{3,2,1,0:T(2,128)(2,1)S(1)} %copy-done.1), kind=kLoop, calls=%fused_computation.16 | loop fusion | bytes 2097152 | tf_op jit(solution)/shard_map/slice | solution.py:238
  33.2 5.5 %context_states.2.own_ref = f32[4,9,32,128]{3,2,1,0:T(8,128)} custom-call(bf16[512,1024]{1,0:T(8,128)(2,1)} %get-tuple-element.22.key_ref, bf16[512,1024]{1,0:T(8,128)(2,1)} %get-tuple-element.21.value_ref, f32[1,256]{1,0:T(1,128)} %fusion.1.column_slot_ref, bf16[9,32,128]{2,1,0:T(8,128)(2,1)} %copy-done.6, bf16[9,32,128]{2,1,0:T(8,128)(2,1)} %copy-done.11, ...), custom_call_target="tpu_custom_call" | custom-call | flops 402653184 | bytes 2097152 | tf_op jit(solution)/shard_map/context_states/pallas_call | solution.py:68
  38.6 0.8 %copy-done.7 = f32[4,9,32,128]{3,2,1,0:T(8,128)} copy-done((f32[4,9,32,128]{3,2,1,0:T(8,128)}, f32[4,9,32,128]{3,2,1,0:T(8,128)S(1)}, u32[]{:S(2)}) %copy-start.7) | copy-done | bytes 589848
  39.5 5.8 %pair_states.1 = (f32[9,32,128]{2,1,0:T(8,128)}, s16[9,32,128]{2,1,0:T(8,128)(2,1)}, s16[9,32,128]{2,1,0:T(8,128)(2,1)}, s16[9,32,128]{2,1,0:T(8,128)(2,1)}) custom-call(f32[4,9,32,128]{3,2,1,0:T(8,128)} %context_states.2.own_ref, f32[4,9,32,128]{3,2,1,0:T(8,128)} %copy-done.7), custom_call_target="tpu_custom_call" | custom-call | tf_op jit(solution)/shard_map/pair_states/pallas_call | solution.py:157
  45.2 0.6 %collective-permute-start.11 = (s16[9,32,128]{2,1,0:T(8,128)(2,1)}, s16[9,32,128]{2,1,0:T(8,128)(2,1)S(1)}, u32[]{:S(2)}, u32[]{:S(2)}) collective-permute-start(s16[9,32,128]{2,1,0:T(8,128)(2,1)} %get-tuple-element.10), channel_id=1, source_target_pairs={{0,8},{4,12},{8,0},{12,4},{16,24},{20,28},{24,16},{28,20},{1,9},{5... | collective-permute-start | bytes 221192 | tf_op jit(solution)/shard_map/ppermute | solution.py:247
  45.9 3.5 %collective-permute-start.12 = (s16[9,32,128]{2,1,0:T(8,128)(2,1)}, s16[9,32,128]{2,1,0:T(8,128)(2,1)S(1)}, u32[]{:S(2)}, u32[]{:S(2)}) collective-permute-start(s16[9,32,128]{2,1,0:T(8,128)(2,1)} %get-tuple-element.11), channel_id=1, source_target_pairs={{0,16},{4,20},{8,24},{12,28},{16,0},{20,4},{24,8},{28,12},{1,17},{... | collective-permute-start | bytes 221192 | tf_op jit(solution)/shard_map/ppermute | solution.py:247
  49.3 0.3 collective-permute-start.13
  49.6 1.4 %copy_bitcast_fusion.2 = (bf16[256,1024]{1,0:T(8,128)(2,1)}, bf16[256,1024]{1,0:T(8,128)(2,1)}) fusion(bf16[1,256,1,1024]{3,2,1,0:T(2,128)(2,1)S(1)} %get-tuple-element.15, bf16[1,256,1,1024]{3,2,1,0:T(2,128)(2,1)S(1)} %get-tuple-element.16), kind=kLoop, calls=%fused_computation.2 | loop fusion | bytes 2097152 | tf_op jit(solution)/shard_map/squeeze | solution.py:238
  51.6 4.1 %suffix_state.1.suffix_ref = f32[9,32,128]{2,1,0:T(8,128)} custom-call(s32[1]{0:T(128)S(6)} %copy.30.length_ref, bf16[9,32,128]{2,1,0:T(8,128)(2,1)} %copy-done.6, bf16[256,1024]{1,0:T(8,128)(2,1)} %get-tuple-element.20.key_ref, bf16[256,1024]{1,0:T(8,128)(2,1)} %get-tuple-element.19.value_ref, bf16[4,1024]{1,0:T(4,128)(2,1)} %bitcast.23, ...), custom_call_target="tpu_custom_call" | custom-call | flops 33554432 | bytes 1048576 | tf_op jit(solution)/shard_map/suffix_state/pallas_call | solution.py:104
  55.8 0.6 %copy-done.8 = s16[9,32,128]{2,1,0:T(8,128)(2,1)} copy-done((s16[9,32,128]{2,1,0:T(8,128)(2,1)}, s16[9,32,128]{2,1,0:T(8,128)(2,1)S(1)}, u32[]{:S(2)}) %copy-start.8) | copy-done | bytes 73752
  56.4 2.2 %final_output.1 = bf16[4,8192]{1,0:T(4,128)(2,1)} custom-call(f32[9,32,128]{2,1,0:T(8,128)} %suffix_state.1.suffix_ref, f32[9,32,128]{2,1,0:T(8,128)} %get-tuple-element.9.home_ref, s16[9,32,128]{2,1,0:T(8,128)(2,1)} %copy-done.8, s16[9,32,128]{2,1,0:T(8,128)(2,1)} %copy-done.9, s16[9,32,128]{2,1,0:T(8,128)(2,1)} %copy-done.10), custom_call_target="tpu_custom_call" | custom-call | tf_op jit(solution)/shard_map/final_output/pallas_call | solution.py:188
  (47 shorter events, 0.3 us)
Async XLA Ops:
  0.0 14.3 %copy-start = (bf16[512,2,1024]{2,1,0:T(2,128)(2,1)S(1)}, bf16[512,2,1024]{2,1,0:T(2,128)(2,1)}, u32[]{:S(2)}) copy-start(bf16[512,2,1024]{2,1,0:T(2,128)(2,1)} %param.10) | copy-start | bytes 6291460
  3.7 13.9 %copy-start.6 = (bf16[9,32,128]{2,1,0:T(8,128)(2,1)}, bf16[9,32,128]{2,1,0:T(8,128)(2,1)S(1)}, u32[]{:S(2)}) copy-start(bf16[9,32,128]{2,1,0:T(8,128)(2,1)S(1)} %concatenate.3.query_ref.refs_0_) | copy-start | bytes 221188
  3.7 13.5 %collective-permute-start = (bf16[9,32,128]{2,1,0:T(8,128)(2,1)S(1)}, bf16[9,32,128]{2,1,0:T(8,128)(2,1)S(1)}, u32[]{:S(2)}, u32[]{:S(2)}) collective-permute-start(bf16[9,32,128]{2,1,0:T(8,128)(2,1)S(1)} %concatenate.3.query_ref.refs_0_), channel_id=1, source_target_pairs={{0,8},{4,12},{8,0},{12,4},{16,24},{20,28},{24,16},{28,20},{1,9},{5... | collective-permute-start | bytes 221192 | tf_op jit(solution)/shard_map/ppermute | solution.py:230
  6.7 10.9 %collective-permute-start.1 = (bf16[9,32,128]{2,1,0:T(8,128)(2,1)S(1)}, bf16[9,32,128]{2,1,0:T(8,128)(2,1)S(1)}, u32[]{:S(2)}, u32[]{:S(2)}) collective-permute-start(bf16[9,32,128]{2,1,0:T(8,128)(2,1)S(1)} %concatenate.3.query_ref.refs_0_), channel_id=1, source_target_pairs={{0,16},{4,20},{8,24},{12,28},{16,0},{20,4},{24,8},{28,12},{1,17},{... | collective-permute-start | bytes 221192 | tf_op jit(solution)/shard_map/ppermute | solution.py:230
  9.3 8.4 %collective-permute-start.2 = (bf16[9,32,128]{2,1,0:T(8,128)(2,1)S(1)}, bf16[9,32,128]{2,1,0:T(8,128)(2,1)S(1)}, u32[]{:S(2)}, u32[]{:S(2)}) collective-permute-start(bf16[9,32,128]{2,1,0:T(8,128)(2,1)S(1)} %concatenate.3.query_ref.refs_0_), channel_id=1, source_target_pairs={{0,24},{4,28},{8,16},{12,20},{16,8},{20,12},{24,0},{28,4},{1,25},{... | collective-permute-start | bytes 221192 | tf_op jit(solution)/shard_map/ppermute | solution.py:230
  11.0 6.3 %copy-start.2 = (bf16[2,64,1024]{2,1,0:T(8,128)(2,1)}, bf16[2,64,1024]{2,1,0:T(8,128)(2,1)S(1)}, u32[]{:S(2)}) copy-start(bf16[2,64,1024]{2,1,0:T(8,128)(2,1)S(1)} %pad_maximum_fusion.refs_4_) | copy-start | bytes 786436
  11.0 11.0 %collective-permute-start.3 = (bf16[2,64,1024]{2,1,0:T(8,128)(2,1)S(1)}, bf16[2,64,1024]{2,1,0:T(8,128)(2,1)S(1)}, u32[]{:S(2)}, u32[]{:S(2)}) collective-permute-start(bf16[2,64,1024]{2,1,0:T(8,128)(2,1)S(1)} %pad_maximum_fusion.refs_4_), channel_id=1, source_target_pairs={{0,1},{1,0},{2,3},{3,2},{4,5},{5,4},{6,7},{7,6},{8,9},{9,8},{10,11... | collective-permute-start | bytes 786440 | tf_op jit(solution)/shard_map/ppermute | solution.py:218
  12.8 12.6 %collective-permute-start.4 = (bf16[2,64,1024]{2,1,0:T(8,128)(2,1)S(1)}, bf16[2,64,1024]{2,1,0:T(8,128)(2,1)S(1)}, u32[]{:S(2)}, u32[]{:S(2)}) collective-permute-start(bf16[2,64,1024]{2,1,0:T(8,128)(2,1)S(1)} %pad_maximum_fusion.refs_4_), channel_id=1, source_target_pairs={{0,2},{1,3},{2,0},{3,1},{4,6},{5,7},{6,4},{7,5},{8,10},{9,11},{10,... | collective-permute-start | bytes 786440 | tf_op jit(solution)/shard_map/ppermute | solution.py:218
  17.3 3.1 %copy-start.11 = (bf16[9,32,128]{2,1,0:T(8,128)(2,1)}, bf16[9,32,128]{2,1,0:T(8,128)(2,1)S(1)}, u32[]{:S(2)}) copy-start(bf16[9,32,128]{2,1,0:T(8,128)(2,1)S(1)} %collective-permute-done.refs_1_) | copy-start | bytes 221188
  17.3 8.1 %collective-permute-start.5 = (bf16[2,64,1024]{2,1,0:T(8,128)(2,1)S(1)}, bf16[2,64,1024]{2,1,0:T(8,128)(2,1)S(1)}, u32[]{:S(2)}, u32[]{:S(2)}) collective-permute-start(bf16[2,64,1024]{2,1,0:T(8,128)(2,1)S(1)} %pad_maximum_fusion.refs_4_), channel_id=1, source_target_pairs={{0,3},{1,2},{2,1},{3,0},{4,7},{5,6},{6,5},{7,4},{8,11},{9,10},{10,... | collective-permute-start | bytes 786440 | tf_op jit(solution)/shard_map/ppermute | solution.py:218
  17.6 2.8 %copy-start.12 = (bf16[9,32,128]{2,1,0:T(8,128)(2,1)}, bf16[9,32,128]{2,1,0:T(8,128)(2,1)S(1)}, u32[]{:S(2)}) copy-start(bf16[9,32,128]{2,1,0:T(8,128)(2,1)S(1)} %collective-permute-done.1.refs_2_) | copy-start | bytes 221188
  17.6 2.8 %collective-permute-start.6 = (bf16[9,32,128]{2,1,0:T(8,128)(2,1)S(1)}, bf16[9,32,128]{2,1,0:T(8,128)(2,1)S(1)}, u32[]{:S(2)}, u32[]{:S(2)}) collective-permute-start(bf16[9,32,128]{2,1,0:T(8,128)(2,1)S(1)} %concatenate.3.query_ref.refs_0_), channel_id=1, source_target_pairs={{0,4},{4,0},{8,12},{12,8},{16,20},{20,16},{24,28},{28,24},{1,5},{5... | collective-permute-start | bytes 221192 | tf_op jit(solution)/shard_map/ppermute | solution.py:232
  17.7 2.8 %copy-start.13 = (bf16[9,32,128]{2,1,0:T(8,128)(2,1)}, bf16[9,32,128]{2,1,0:T(8,128)(2,1)S(1)}, u32[]{:S(2)}) copy-start(bf16[9,32,128]{2,1,0:T(8,128)(2,1)S(1)} %collective-permute-done.2.refs_3_) | copy-start | bytes 221188
  17.7 2.8 %collective-permute-start.7 = (bf16[9,32,128]{2,1,0:T(8,128)(2,1)S(1)}, bf16[9,32,128]{2,1,0:T(8,128)(2,1)S(1)}, u32[]{:S(2)}, u32[]{:S(2)}) collective-permute-start(bf16[9,32,128]{2,1,0:T(8,128)(2,1)S(1)} %collective-permute-done.refs_1_), channel_id=1, source_target_pairs={{0,4},{4,0},{8,12},{12,8},{16,20},{20,16},{24,28},{28,24},{1,5},{5... | collective-permute-start | bytes 221192 | tf_op jit(solution)/shard_map/ppermute | solution.py:232
  20.3 11.3 %copy-start.1 = (bf16[1,256,2,1024]{3,2,1,0:T(2,128)(2,1)S(1)}, bf16[1,256,2,1024]{3,2,1,0:T(2,128)(2,1)}, u32[]{:S(2)}) copy-start(bf16[1,256,2,1024]{3,2,1,0:T(2,128)(2,1)} %param.14) | copy-start | bytes 3145732
  20.4 5.0 %copy-start.14 = (bf16[9,32,128]{2,1,0:T(8,128)(2,1)}, bf16[9,32,128]{2,1,0:T(8,128)(2,1)S(1)}, u32[]{:S(2)}) copy-start(bf16[9,32,128]{2,1,0:T(8,128)(2,1)S(1)} %collective-permute-done.6.refs_0_) | copy-start | bytes 221188
  20.4 1.3 %collective-permute-start.8 = (bf16[9,32,128]{2,1,0:T(8,128)(2,1)S(1)}, bf16[9,32,128]{2,1,0:T(8,128)(2,1)S(1)}, u32[]{:S(2)}, u32[]{:S(2)}) collective-permute-start(bf16[9,32,128]{2,1,0:T(8,128)(2,1)S(1)} %collective-permute-done.1.refs_2_), channel_id=1, source_target_pairs={{0,4},{4,0},{8,12},{12,8},{16,20},{20,16},{24,28},{28,24},{1,5},{5... | collective-permute-start | bytes 221192 | tf_op jit(solution)/shard_map/ppermute | solution.py:232
  20.5 4.8 %copy-start.15 = (bf16[9,32,128]{2,1,0:T(8,128)(2,1)}, bf16[9,32,128]{2,1,0:T(8,128)(2,1)S(1)}, u32[]{:S(2)}) copy-start(bf16[9,32,128]{2,1,0:T(8,128)(2,1)S(1)} %collective-permute-done.7.refs_1_) | copy-start | bytes 221188
  20.5 1.4 %collective-permute-start.9 = (bf16[9,32,128]{2,1,0:T(8,128)(2,1)S(1)}, bf16[9,32,128]{2,1,0:T(8,128)(2,1)S(1)}, u32[]{:S(2)}, u32[]{:S(2)}) collective-permute-start(bf16[9,32,128]{2,1,0:T(8,128)(2,1)S(1)} %collective-permute-done.2.refs_3_), channel_id=1, source_target_pairs={{0,4},{4,0},{8,12},{12,8},{16,20},{20,16},{24,28},{28,24},{1,5},{5... | collective-permute-start | bytes 221192 | tf_op jit(solution)/shard_map/ppermute | solution.py:232
  21.7 3.7 %copy-start.16 = (bf16[9,32,128]{2,1,0:T(8,128)(2,1)}, bf16[9,32,128]{2,1,0:T(8,128)(2,1)S(1)}, u32[]{:S(2)}) copy-start(bf16[9,32,128]{2,1,0:T(8,128)(2,1)S(1)} %collective-permute-done.8.refs_2_) | copy-start | bytes 221188
  21.9 3.5 %copy-start.17 = (bf16[9,32,128]{2,1,0:T(8,128)(2,1)}, bf16[9,32,128]{2,1,0:T(8,128)(2,1)S(1)}, u32[]{:S(2)}) copy-start(bf16[9,32,128]{2,1,0:T(8,128)(2,1)S(1)} %collective-permute-done.9.refs_3_) | copy-start | bytes 221188
  21.9 3.5 %copy-start.3 = (bf16[2,64,1024]{2,1,0:T(8,128)(2,1)}, bf16[2,64,1024]{2,1,0:T(8,128)(2,1)S(1)}, u32[]{:S(2)}) copy-start(bf16[2,64,1024]{2,1,0:T(8,128)(2,1)S(1)} %collective-permute-done.3.refs_5_) | copy-start | bytes 786436
  25.4 0.7 %copy-start.4 = (bf16[2,64,1024]{2,1,0:T(8,128)(2,1)}, bf16[2,64,1024]{2,1,0:T(8,128)(2,1)S(1)}, u32[]{:S(2)}) copy-start(bf16[2,64,1024]{2,1,0:T(8,128)(2,1)S(1)} %collective-permute-done.4.refs_6_) | copy-start | bytes 786436
  25.4 0.8 %copy-start.5 = (bf16[2,64,1024]{2,1,0:T(8,128)(2,1)}, bf16[2,64,1024]{2,1,0:T(8,128)(2,1)S(1)}, u32[]{:S(2)}) copy-start(bf16[2,64,1024]{2,1,0:T(8,128)(2,1)S(1)} %collective-permute-done.5.refs_7_) | copy-start | bytes 786436
  31.6 7.0 %collective-permute-start.10 = (f32[4,9,32,128]{3,2,1,0:T(8,128)}, f32[4,9,32,128]{3,2,1,0:T(8,128)S(1)}, u32[]{:S(2)}, u32[]{:S(2)}) collective-permute-start(f32[4,9,32,128]{3,2,1,0:T(8,128)} %context_states.3), channel_id=1, source_target_pairs={{0,4},{4,0},{8,12},{12,8},{16,20},{20,16},{24,28},{28,24},{1,5},{5... | collective-permute-start | bytes 1769480 | tf_op jit(solution)/shard_map/ppermute | solution.py:245
  38.6 0.8 %copy-start.7 = (f32[4,9,32,128]{3,2,1,0:T(8,128)}, f32[4,9,32,128]{3,2,1,0:T(8,128)S(1)}, u32[]{:S(2)}) copy-start(f32[4,9,32,128]{3,2,1,0:T(8,128)S(1)} %collective-permute-done.10.other_ref) | copy-start | bytes 1769476
  45.2 10.5 %collective-permute-start.11 = (s16[9,32,128]{2,1,0:T(8,128)(2,1)}, s16[9,32,128]{2,1,0:T(8,128)(2,1)S(1)}, u32[]{:S(2)}, u32[]{:S(2)}) collective-permute-start(s16[9,32,128]{2,1,0:T(8,128)(2,1)} %get-tuple-element.10), channel_id=1, source_target_pairs={{0,8},{4,12},{8,0},{12,4},{16,24},{20,28},{24,16},{28,20},{1,9},{5... | collective-permute-start | bytes 221192 | tf_op jit(solution)/shard_map/ppermute | solution.py:247
  45.9 9.9 %collective-permute-start.12 = (s16[9,32,128]{2,1,0:T(8,128)(2,1)}, s16[9,32,128]{2,1,0:T(8,128)(2,1)S(1)}, u32[]{:S(2)}, u32[]{:S(2)}) collective-permute-start(s16[9,32,128]{2,1,0:T(8,128)(2,1)} %get-tuple-element.11), channel_id=1, source_target_pairs={{0,16},{4,20},{8,24},{12,28},{16,0},{20,4},{24,8},{28,12},{1,17},{... | collective-permute-start | bytes 221192 | tf_op jit(solution)/shard_map/ppermute | solution.py:247
  49.3 6.4 %collective-permute-start.13 = (s16[9,32,128]{2,1,0:T(8,128)(2,1)}, s16[9,32,128]{2,1,0:T(8,128)(2,1)S(1)}, u32[]{:S(2)}, u32[]{:S(2)}) collective-permute-start(s16[9,32,128]{2,1,0:T(8,128)(2,1)} %get-tuple-element.12), channel_id=1, source_target_pairs={{0,24},{4,28},{8,16},{12,20},{16,8},{20,12},{24,0},{28,4},{1,25},{... | collective-permute-start | bytes 221192 | tf_op jit(solution)/shard_map/ppermute | solution.py:247
  55.7 0.6 %copy-start.8 = (s16[9,32,128]{2,1,0:T(8,128)(2,1)}, s16[9,32,128]{2,1,0:T(8,128)(2,1)S(1)}, u32[]{:S(2)}) copy-start(s16[9,32,128]{2,1,0:T(8,128)(2,1)S(1)} %collective-permute-done.11.refs_0_) | copy-start | bytes 221188
  55.8 0.6 %copy-start.9 = (s16[9,32,128]{2,1,0:T(8,128)(2,1)}, s16[9,32,128]{2,1,0:T(8,128)(2,1)S(1)}, u32[]{:S(2)}) copy-start(s16[9,32,128]{2,1,0:T(8,128)(2,1)S(1)} %collective-permute-done.12.refs_1_) | copy-start | bytes 221188
  55.8 0.6 %copy-start.10 = (s16[9,32,128]{2,1,0:T(8,128)(2,1)}, s16[9,32,128]{2,1,0:T(8,128)(2,1)S(1)}, u32[]{:S(2)}) copy-start(s16[9,32,128]{2,1,0:T(8,128)(2,1)S(1)} %collective-permute-done.13.refs_2_) | copy-start | bytes 221188

commit v2 on v1

v2 whole, which is shorter than its diff:
```python
import functools

import jax
import jax.numpy as jnp
from jax import lax
from jax.experimental import pallas as pl
from jax.experimental.pallas import tpu as pltpu
from jax.sharding import PartitionSpec as P

KEY_VALUE_HEADS = 8
HEAD_SIZE = 128
SCALE = HEAD_SIZE**-0.5
SCALE_TWO = SCALE * 1.4426950408889634
MIB = 1024 * 1024
FILLER = -1e30
CODE_TOP = 32000.0
REST_TOP = 65000.0

NT = (((1,), (1,)), ((), ()))


def head_lanes(h):
    return pl.ds(h * HEAD_SIZE, HEAD_SIZE)


def put_lane(slab, lane, column):
    at = lax.broadcasted_iota(jnp.int32, slab.shape, 1)
    return jnp.where(at == lane, column, slab)


def vmem_limit(members, slots):
    return (16 if members * slots <= 32 else 48) * MIB


def in_any(count):
    return [pl.BlockSpec(memory_space=pl.ANY)] * count


def in_vmem(count):
    return [pl.BlockSpec(memory_space=pltpu.VMEM)] * count


def in_smem(count):
    return [pl.BlockSpec(memory_space=pltpu.SMEM)] * count


def prepare_kernel(tab_count, session_ref, owner_ref, query_ref, tab_ref, message_ref, block_ref):
    slot = jnp.int32(0)
    for k in range(tab_count):
        slot = jnp.where(session_ref[0] == k, owner_ref[k], slot)
    message_ref[:KEY_VALUE_HEADS] = query_ref[...]
    filled = jnp.full(message_ref.shape[1:], slot.astype(jnp.float32), jnp.float32)
    message_ref[KEY_VALUE_HEADS] = filled.astype(jnp.bfloat16)
    block_ref[0] = tab_ref[:, 0, :]
    block_ref[1] = tab_ref[:, 1, :]


def prepare(session_tab, tab_owner, query, tab):
    return pl.pallas_call(
        functools.partial(prepare_kernel, tab_owner.shape[0]),
        in_specs=in_smem(2) + in_vmem(2),
        out_shape=[
            jax.ShapeDtypeStruct((KEY_VALUE_HEADS + 1,) + query.shape[1:], jnp.bfloat16),
            jax.ShapeDtypeStruct((2, tab.shape[0], tab.shape[2]), jnp.bfloat16),
        ],
        compiler_params=pltpu.CompilerParams(vmem_limit_bytes=16 * MIB),
        name="prepare",
    )(session_tab, tab_owner, query, tab)


def split_kernel(paired_ref, key_ref, value_ref):
    key_ref[...] = paired_ref[:, 0, :]
    value_ref[...] = paired_ref[:, 1, :]


def split_pairs(paired):
    shape = jax.ShapeDtypeStruct((paired.shape[0], paired.shape[2]), paired.dtype)
    return pl.pallas_call(
        split_kernel,
        out_shape=[shape, shape],
        cost_estimate=pl.CostEstimate(
            flops=8 * paired.size, transcendentals=0, bytes_accessed=4 * paired.size
        ),
        compiler_params=pltpu.CompilerParams(vmem_limit_bytes=16 * MIB),
        name="split_pairs",
    )(paired)


def block_softmax(score_parts, value_parts):
    largest = functools.reduce(
        jnp.maximum, [jnp.max(s, axis=-1, keepdims=True) for s in score_parts]
    )
    product = 0.0
    for scores, values in zip(score_parts, value_parts):
        weights = jnp.exp2((scores - largest) * SCALE_TWO).astype(jnp.bfloat16)
        values = jnp.concatenate([values, jnp.ones_like(values)], axis=1)
        product += jnp.dot(weights, values, preferred_element_type=jnp.float32)
    summed, total = product[:, :HEAD_SIZE], product[:, HEAD_SIZE:]
    return summed / total, largest * SCALE + jnp.log(total)


def context_kernel(members, slots, after, key_ref, value_ref, column_slot_ref, *refs):
    query_refs, tab_refs, out_ref = refs[:members], refs[members : members + slots], refs[-1]
    rows = query_refs[0].shape[1]
    owner = jnp.concatenate([q[KEY_VALUE_HEADS, :, 0:1] for q in query_refs], axis=0)
    mine = owner.astype(jnp.float32) == column_slot_ref[0:1, :]
    ends = jnp.zeros((members * rows, HEAD_SIZE), jnp.float32)
    for h in range(KEY_VALUE_HEADS):
        at = head_lanes(h)
        query = jnp.concatenate([q[h] for q in query_refs], axis=0)
        tab_keys = jnp.concatenate([t[0, :, at] for t in tab_refs], axis=0)
        tab_values = jnp.concatenate([t[1, :, at] for t in tab_refs], axis=0)
        shared = lax.dot_general(query, key_ref[:, at], NT, preferred_element_type=jnp.float32)
        tab = lax.dot_general(query, tab_keys, NT, preferred_element_type=jnp.float32)
        tab = jnp.where(mine, tab, FILLER)
        mean, end = block_softmax([shared, tab], [value_ref[:, at], tab_values])
        for i in range(members):
            out_ref[i, h] = mean[i * rows : (i + 1) * rows]
        ends = put_lane(ends, h, end)
    for i in range(members):
        out_ref[i, KEY_VALUE_HEADS] = ends[i * rows : (i + 1) * rows]


def context_states(query_messages, keys, values, column_slot, tabs, after=()):
    members, rows = len(query_messages), query_messages[0].shape[1]
    key_count = keys.shape[0] + column_slot.shape[1]
    work = members * rows * KEY_VALUE_HEADS * key_count
    return pl.pallas_call(
        functools.partial(context_kernel, members, len(tabs), len(after)),
        in_specs=in_vmem(3 + members + len(tabs)) + in_any(len(after)),
        out_shape=jax.ShapeDtypeStruct(
            (members, KEY_VALUE_HEADS + 1, rows, HEAD_SIZE), jnp.float32
        ),
        compiler_params=pltpu.CompilerParams(vmem_limit_bytes=vmem_limit(members, len(tabs))),
        cost_estimate=pl.CostEstimate(
            flops=4 * work * HEAD_SIZE, transcendentals=work, bytes_accessed=4 * keys.size
        ),
        name="context_states",
    )(keys, values, column_slot, *query_messages, *tabs, *after)


def suffix_kernel(steps, length_ref, query_ref, pair_ref, new_key_ref, new_value_ref, *refs):
    out_ref = refs[-1]
    rows, slots = query_ref.shape[1], pair_ref.shape[0]
    used = lax.broadcasted_iota(jnp.int32, (rows, slots), 1) < length_ref[0]
    step = lax.rem(lax.broadcasted_iota(jnp.int32, (rows, steps), 0), steps)
    seen = lax.broadcasted_iota(jnp.int32, (rows, steps), 1) <= step
    ends = jnp.zeros((rows, HEAD_SIZE), jnp.float32)
    for h in range(KEY_VALUE_HEADS):
        at = head_lanes(h)
        query = query_ref[h]
        keys, values = pair_ref[:, 0, at], pair_ref[:, 1, at]
        cached = lax.dot_general(query, keys, NT, preferred_element_type=jnp.float32)
        fresh = lax.dot_general(query, new_key_ref[:, at], NT, preferred_element_type=jnp.float32)
        cached = jnp.where(used, cached, FILLER)
        fresh = jnp.where(seen, fresh, FILLER)
        mean, end = block_softmax([cached, fresh], [values, new_value_ref[:, at]])
        out_ref[h] = mean
        ends = put_lane(ends, h, end)
    out_ref[KEY_VALUE_HEADS] = ends


def suffix_state(query_message, cache, length, new_keys, new_values, after=()):
    rows, steps = query_message.shape[1], new_keys.shape[0]
    work = rows * KEY_VALUE_HEADS * cache.shape[0]
    return pl.pallas_call(
        functools.partial(suffix_kernel, steps),
        in_specs=in_smem(1) + in_vmem(4) + in_any(len(after)),
        out_shape=jax.ShapeDtypeStruct((KEY_VALUE_HEADS + 1, rows, HEAD_SIZE), jnp.float32),
        compiler_params=pltpu.CompilerParams(vmem_limit_bytes=16 * MIB),
        cost_estimate=pl.CostEstimate(
            flops=4 * work * HEAD_SIZE, transcendentals=work, bytes_accessed=4 * cache.size
        ),
        name="suffix_state",
    )(length, query_message, cache, new_keys, new_values, *after)


def shares_of(ends):
    top = functools.reduce(jnp.maximum, ends)
    shares = [jnp.exp(end - top) for end in ends]
    total = functools.reduce(jnp.add, shares)
    return [share / total for share in shares], top + jnp.log(total)


def mixed(parts, shares, h):
    return functools.reduce(
        jnp.add, [part * share[:, h : h + 1] for part, share in zip(parts, shares)]
    )


def pair_kernel(own_ref, other_ref, *coded_refs):
    rows = own_ref.shape[2]
    for i, coded_ref in enumerate(coded_refs):
        refs = (own_ref, other_ref)
        shares, end = shares_of([r[i, KEY_VALUE_HEADS] for r in refs])
        means = [mixed([r[i, h] for r in refs], shares, h) for h in range(KEY_VALUE_HEADS)]
        reach = jnp.ones((rows, HEAD_SIZE), jnp.float32)
        for h, mean in enumerate(means):
            reach = put_lane(reach, h, jnp.max(jnp.abs(mean), axis=-1, keepdims=True))
        exponent = jnp.ceil(jnp.log2(jnp.maximum(reach, 1e-30)))
        factor = jnp.exp2(-exponent) * CODE_TOP
        for h, mean in enumerate(means):
            code = jnp.round(mean * factor[:, h : h + 1])
            coded_ref[h] = code.astype(jnp.int32).astype(jnp.int16)
        near = jnp.round(end)
        rest = jnp.round((end - near) * REST_TOP)
        slab = jnp.zeros((rows, HEAD_SIZE), jnp.float32)
        for k, kind in enumerate((near, rest, exponent)):
            at = lax.broadcasted_iota(jnp.int32, slab.shape, 1)
            moved = pltpu.roll(kind, k * KEY_VALUE_HEADS, 1) if k else kind
            slab = jnp.where(at // KEY_VALUE_HEADS == k, moved, slab)
        coded_ref[KEY_VALUE_HEADS] = slab.astype(jnp.int32).astype(jnp.int16)


def pair_states(own, other):
    members, shape = own.shape[0], own.shape[1:]
    return pl.pallas_call(
        pair_kernel,
        out_shape=[jax.ShapeDtypeStruct(shape, jnp.int16)] * members,
        compiler_params=pltpu.CompilerParams(vmem_limit_bytes=16 * MIB),
        name="pair_states",
    )(own, other)


def final_kernel(suffix_ref, own_ref, other_ref, *refs):
    coded_refs, out_ref = refs[:-1], refs[-1]
    plain_refs = (suffix_ref, own_ref.at[0], other_ref.at[0])
    ends = [r[KEY_VALUE_HEADS] for r in plain_refs]
    factors = []
    for r in coded_refs:
        near = r[KEY_VALUE_HEADS].astype(jnp.int32).astype(jnp.float32)
        rest, exponent = (
            pltpu.roll(near, HEAD_SIZE - k * KEY_VALUE_HEADS, 1) for k in range(1, 3)
        )
        ends.append(near + rest / REST_TOP)
        factors.append(jnp.exp2(exponent) / CODE_TOP)
    head_lane = lax.broadcasted_iota(jnp.int32, ends[0].shape, 1) < KEY_VALUE_HEADS
    shares, _ = shares_of([jnp.where(head_lane, end, 0.0) for end in ends])
    for i, factor in enumerate(factors, start=len(plain_refs)):
        shares[i] = shares[i] * jnp.where(head_lane, factor, 0.0)
    for h in range(KEY_VALUE_HEADS):
        parts = [r[h] for r in plain_refs]
        parts += [r[h].astype(jnp.int32).astype(jnp.float32) for r in coded_refs]
        out_ref[h] = mixed(parts, shares, h).astype(jnp.bfloat16)


def final_output(suffix, own, other, coded):
    return pl.pallas_call(
        final_kernel,
        out_shape=jax.ShapeDtypeStruct((KEY_VALUE_HEADS,) + suffix.shape[1:], jnp.bfloat16),
        compiler_params=pltpu.CompilerParams(vmem_limit_bytes=16 * MIB),
        name="final_output",
    )(suffix, own, other, *coded)


def swap(count, bit):
    return [(i, i ^ bit) for i in range(count)]


def shards(
    queries,
    prefix_key_value,
    tab_key_value,
    tab_owner,
    session_tab,
    suffix_key_value,
    suffix_len,
    token_keys,
    token_values,
):
    ctx_count, tab_count = lax.axis_size("ctx"), lax.axis_size("tab")
    pair_count = ctx_count // 2
    steps = queries.shape[1]
    tab_rows = tab_key_value.shape[1]

    query = queries[0].reshape(steps, KEY_VALUE_HEADS, -1, HEAD_SIZE)
    query = query.transpose(1, 2, 0, 3).reshape(KEY_VALUE_HEADS, -1, HEAD_SIZE)
    message, tab_block = prepare(session_tab, tab_owner, query, tab_key_value[0])
    tabs = [tab_block] + [
        lax.ppermute(tab_block, "tab", swap(tab_count, k)) for k in range(1, tab_count)
    ]
    places = jnp.arange(tab_count * tab_rows, dtype=jnp.int32) // tab_rows
    column_slot = (places ^ lax.axis_index("tab")).astype(jnp.float32)[None]
    column = [message] + [
        lax.ppermute(message, "ctx", swap(ctx_count, 2 * k)) for k in range(1, pair_count)
    ]
    other_column = [lax.ppermute(m, "ctx", swap(ctx_count, 1)) for m in column]

    keys, values = split_pairs(prefix_key_value)
    shared = (keys, values, column_slot, tabs)
    other_far = context_states(other_column[1:], *shared)
    own_far = context_states(column[1:], *shared)
    coded = pair_states(own_far, lax.ppermute(other_far, "ctx", swap(ctx_count, 1)))
    received = [
        lax.ppermute(c, "ctx", swap(ctx_count, 2 * k)) for k, c in enumerate(coded, start=1)
    ]
    other_near = context_states(other_column[:1], *shared, after=coded[:1])
    own_near = context_states(column[:1], *shared, after=coded[:1])
    suffix = suffix_state(
        message, suffix_key_value[0], suffix_len, token_keys[0], token_values[0], after=coded[:1]
    )
    result = final_output(
        suffix, own_near, lax.ppermute(other_near, "ctx", swap(ctx_count, 1)), received
    )
    result = result.reshape(KEY_VALUE_HEADS, -1, steps, HEAD_SIZE)
    return result.transpose(2, 0, 1, 3).reshape(queries.shape)


def solution(mesh):
    sessions = ("ctx", "tab")
    placed = (
        P(sessions, None, None),
        P("ctx", None, None),
        P("tab", "ctx", None, None),
        P(),
        P(sessions),
        P(sessions, None, None, None),
        P(sessions),
        P(sessions, None, None),
        P(sessions, None, None),
    )
    return jax.shard_map(
        shards, mesh=mesh, in_specs=placed, out_specs=P(sessions, None, None), check_vma=False
    )
```

time: 58.9 us -> 43.5 us (0.74)
  local copies, waits for them, and re-layouts: 12.7 us -> 4.05 us
  Pallas kernels: 23 us -> 16.5 us
  starting transfers between devices: 14.8 us -> 18.3 us
  other arithmetic: 1.96 us -> 0.01 us
  waiting for transfers between devices: 3.81 us -> 2.84 us
  between operations: 2.31 us -> 1.48 us
    pallas_call x5 -> x9, Pallas kernels: 23 us -> 16.5 us  [the longest x4 5.63 us: context_states(): pl.pallas_call(functools.partial(context_kernel, members, len(tabs), len(...]
    slice x3 -> x0, local copies, waits for them, and re-layouts: 5.98 us -> none  [the longest x1 2.96 us: shards(): keys, values = (prefix_key_value[:, 0], prefix_key_value[:, 1])]
    squeeze x2 -> x0, local copies, waits for them, and re-layouts: 3.52 us -> none  [the longest x1 2.17 us: shards(): keys, values = (prefix_key_value[:, 0], prefix_key_value[:, 1])]
    ppermute x3, waiting for transfers between devices: 3.42 us -> 0.01 us  [shards(): lax.ppermute(tab_block, 'tab', swap(tab_count, k))]
    ppermute x3, starting transfers between devices: 5.62 us -> 7.95 us  [shards(): lax.ppermute(message, 'ctx', swap(ctx_count, 2 * k))]
    unnamed x36 -> x14, local copies, waits for them, and re-layouts: 2.26 us -> 4.05 us
    ppermute x3, waiting for transfers between devices: 0.01 us -> 1.64 us  [shards(): lax.ppermute(message, 'ctx', swap(ctx_count, 2 * k))]
    reduce_sum x1 -> x0, other arithmetic: 1.36 us -> none  [shards(): slot = jnp.sum(jnp.where(session_tab[0] == table, tab_owner, 0))]
  transfers between devices with their start and end apart: 14 -> 15, of which waited for: 3 -> 4; matrix products, arithmetic and copies ran while one was open for 17% -> 0% of each run, Pallas kernels for 16% -> 27%
where the time goes in v2:
time: 43.5 us; the launch traced here: 43.2 us
  starting transfers between devices  18.3 us (42%)
  Pallas kernels  16.5 us (38%)
  local copies, waits for them, and re-layouts  4.05 us (9%)
  waiting for transfers between devices  2.84 us (7%)
  between operations  1.48 us (3%)
    ppermute x3, starting transfers between devices, shards(): lax.ppermute(message, 'ctx', swap(ctx_count, 2 * k))  7.95 us
    pallas_call x4, Pallas kernels, context_states(): pl.pallas_call(functools.partial(context_kernel, members, len(tabs), len(...  5.63 us
    pallas_call x1, Pallas kernels, split_pairs(): pl.pallas_call(split_kernel, out_shape=[shape, shape], cost_estimate=pl.C...  4.59 us
    ppermute x3, starting transfers between devices, shards(): lax.ppermute(tab_block, 'tab', swap(tab_count, k))  4.54 us
    ppermute x3, starting transfers between devices, shards(): lax.ppermute(c, 'ctx', swap(ctx_count, 2 * k))  4.39 us
    unnamed x14, local copies, waits for them, and re-layouts  4.05 us
    pallas_call x1, Pallas kernels, suffix_state(): pl.pallas_call(functools.partial(suffix_kernel, steps), in_specs=in_smem(...  3.15 us
    ppermute x3, waiting for transfers between devices, shards(): lax.ppermute(message, 'ctx', swap(ctx_count, 2 * k))  1.64 us
  transfers between devices with their start and end apart: 15, of which 4 were waited for; matrix products, arithmetic and copies ran while one was open for 0% of the time, Pallas kernels for 27%

profile of v2, /device:TPU:0, one launch (start us, length us, event | category | flops | bytes accessed | tf_op | source)
XLA Modules:
  0.0 43.2 jit_solution(11585729721894013358)
XLA Ops:
  0.7 0.9 %copy-done.2 = bf16[1,64,2,1024]{3,2,1,0:T(2,128)(2,1)S(1)} copy-done((bf16[1,64,2,1024]{3,2,1,0:T(2,128)(2,1)S(1)}, bf16[1,64,2,1024]{3,2,1,0:T(2,128)(2,1)}, u32[]{:S(2)}) %copy-start.2) | copy-done | bytes 262168
  1.6 0.8 %copy-done.3 = bf16[1,4,8192]{2,1,0:T(4,128)(2,1)S(1)} copy-done((bf16[1,4,8192]{2,1,0:T(4,128)(2,1)S(1)}, bf16[1,4,8192]{2,1,0:T(4,128)(2,1)}, u32[]{:S(2)}) %copy-start.3) | copy-done | bytes 65560
  2.4 0.7 %copy-done.6 = s32[4]{0:T(128)S(1)} copy-done((s32[4]{0:T(128)S(1)}, s32[4]{0:T(128)}, u32[]{:S(2)}) %copy-start.6) | copy-done | bytes 40
  3.1 1.1 %prepare.1 = (bf16[9,32,128]{2,1,0:T(8,128)(2,1)S(1)}, bf16[2,64,1024]{2,1,0:T(8,128)(2,1)S(1)}) custom-call(s32[1]{0:T(128)S(6)} %copy.12.session_ref, s32[4]{0:T(128)S(1)} %copy-done.6, bf16[8,32,128]{2,1,0:T(8,128)(2,1)S(1)} %bitcast.16, bf16[64,2,1024]{2,1,0:T(2,128)(2,1)S(1)} %bitcast.15), custom_call_target="tpu_custom_call" | custom-call | tf_op jit(solution)/shard_map/prepare/pallas_call | solution.py:59
  4.2 3.0 %collective-permute-start.3 = (bf16[2,64,1024]{2,1,0:T(8,128)(2,1)S(1)}, bf16[2,64,1024]{2,1,0:T(8,128)(2,1)S(1)}, u32[]{:S(2)}, u32[]{:S(2)}) collective-permute-start(bf16[2,64,1024]{2,1,0:T(8,128)(2,1)S(1)} %get-tuple-element.15.refs_3_.refs_1_), channel_id=1, source_target_pairs={{0,1},{1,0},{2,3},{3,2},{4,5},{5,4},{6,7},{7,6},{8,9},{9,8},{10,11... | collective-permute-start | bytes 786440 | tf_op jit(solution)/shard_map/ppermute | solution.py:280
  7.2 1.5 %collective-permute-start.4 = (bf16[2,64,1024]{2,1,0:T(8,128)(2,1)S(1)}, bf16[2,64,1024]{2,1,0:T(8,128)(2,1)S(1)}, u32[]{:S(2)}, u32[]{:S(2)}) collective-permute-start(bf16[2,64,1024]{2,1,0:T(8,128)(2,1)S(1)} %get-tuple-element.15.refs_3_.refs_1_), channel_id=1, source_target_pairs={{0,2},{1,3},{2,0},{3,1},{4,6},{5,7},{6,4},{7,5},{8,10},{9,11},{10,... | collective-permute-start | bytes 786440 | tf_op jit(solution)/shard_map/ppermute | solution.py:280
  8.8 0.0 collective-permute-start.5
  8.8 2.0 %collective-permute-start = (bf16[9,32,128]{2,1,0:T(8,128)(2,1)S(1)}, bf16[9,32,128]{2,1,0:T(8,128)(2,1)S(1)}, u32[]{:S(2)}, u32[]{:S(2)}) collective-permute-start(bf16[9,32,128]{2,1,0:T(8,128)(2,1)S(1)} %get-tuple-element.12.query_ref.refs_0_), channel_id=1, source_target_pairs={{0,8},{4,12},{8,0},{12,4},{16,24},{20,28},{24,16},{28,20},{1,9},{5... | collective-permute-start | bytes 221192 | tf_op jit(solution)/shard_map/ppermute | solution.py:285
  10.8 2.6 %collective-permute-start.1 = (bf16[9,32,128]{2,1,0:T(8,128)(2,1)S(1)}, bf16[9,32,128]{2,1,0:T(8,128)(2,1)S(1)}, u32[]{:S(2)}, u32[]{:S(2)}) collective-permute-start(bf16[9,32,128]{2,1,0:T(8,128)(2,1)S(1)} %get-tuple-element.12.query_ref.refs_0_), channel_id=1, source_target_pairs={{0,16},{4,20},{8,24},{12,28},{16,0},{20,4},{24,8},{28,12},{1,17},{... | collective-permute-start | bytes 221192 | tf_op jit(solution)/shard_map/ppermute | solution.py:285
  13.4 0.5 %collective-permute-done.refs_0_ = bf16[9,32,128]{2,1,0:T(8,128)(2,1)S(1)} collective-permute-done((bf16[9,32,128]{2,1,0:T(8,128)(2,1)S(1)}, bf16[9,32,128]{2,1,0:T(8,128)(2,1)S(1)}, u32[]{:S(2)}, u32[]{:S(2)}) %collective-permute-start) | collective-permute-done | bytes 73760 | tf_op jit(solution)/shard_map/ppermute | solution.py:285
  13.9 3.3 %collective-permute-start.2 = (bf16[9,32,128]{2,1,0:T(8,128)(2,1)S(1)}, bf16[9,32,128]{2,1,0:T(8,128)(2,1)S(1)}, u32[]{:S(2)}, u32[]{:S(2)}) collective-permute-start(bf16[9,32,128]{2,1,0:T(8,128)(2,1)S(1)} %get-tuple-element.12.query_ref.refs_0_), channel_id=1, source_target_pairs={{0,24},{4,28},{8,16},{12,20},{16,8},{20,12},{24,0},{28,4},{1,25},{... | collective-permute-start | bytes 221192 | tf_op jit(solution)/shard_map/ppermute | solution.py:285
  17.2 1.2 %collective-permute-done.1.refs_1_ = bf16[9,32,128]{2,1,0:T(8,128)(2,1)S(1)} collective-permute-done((bf16[9,32,128]{2,1,0:T(8,128)(2,1)S(1)}, bf16[9,32,128]{2,1,0:T(8,128)(2,1)S(1)}, u32[]{:S(2)}, u32[]{:S(2)}) %collective-permute-start.1) | collective-permute-done | bytes 73760 | tf_op jit(solution)/shard_map/ppermute | solution.py:285
  18.4 1.6 %copy-done = bf16[512,2,1024]{2,1,0:T(2,128)(2,1)S(1)} copy-done((bf16[512,2,1024]{2,1,0:T(2,128)(2,1)S(1)}, bf16[512,2,1024]{2,1,0:T(2,128)(2,1)}, u32[]{:S(2)}) %copy-start) | copy-done | bytes 2097176
  20.0 4.6 %split_pairs.1 = (bf16[512,1024]{1,0:T(8,128)(2,1)S(1)}, bf16[512,1024]{1,0:T(8,128)(2,1)S(1)}) custom-call(bf16[512,2,1024]{2,1,0:T(2,128)(2,1)S(1)} %copy-done), custom_call_target="tpu_custom_call" | custom-call | flops 8388608 | bytes 4194304 | tf_op jit(solution)/shard_map/split_pairs/pallas_call | solution.py:78
  24.6 0.6 %collective-permute-start.7 = (bf16[9,32,128]{2,1,0:T(8,128)(2,1)S(1)}, bf16[9,32,128]{2,1,0:T(8,128)(2,1)S(1)}, u32[]{:S(2)}, u32[]{:S(2)}) collective-permute-start(bf16[9,32,128]{2,1,0:T(8,128)(2,1)S(1)} %collective-permute-done.1.refs_1_), channel_id=1, source_target_pairs={{0,4},{4,0},{8,12},{12,8},{16,20},{20,16},{24,28},{28,24},{1,5},{5... | collective-permute-start | bytes 221192 | tf_op jit(solution)/shard_map/ppermute | solution.py:287
  25.1 0.1 collective-permute-start.8
  25.2 0.8 %collective-permute-done.7.refs_1_ = bf16[9,32,128]{2,1,0:T(8,128)(2,1)S(1)} collective-permute-done((bf16[9,32,128]{2,1,0:T(8,128)(2,1)S(1)}, bf16[9,32,128]{2,1,0:T(8,128)(2,1)S(1)}, u32[]{:S(2)}, u32[]{:S(2)}) %collective-permute-start.7) | collective-permute-done | bytes 73760 | tf_op jit(solution)/shard_map/ppermute | solution.py:287
  26.0 0.4 collective-permute-done.8.refs_2_
  26.4 1.5 %context_states.5 = f32[3,9,32,128]{3,2,1,0:T(8,128)S(1)} custom-call(bf16[512,1024]{1,0:T(8,128)(2,1)S(1)} %get-tuple-element.13.key_ref, bf16[512,1024]{1,0:T(8,128)(2,1)S(1)} %get-tuple-element.14.value_ref, f32[1,256]{1,0:T(1,128)S(1)} %fusion.1.column_slot_ref, bf16[9,32,128]{2,1,0:T(8,128)(2,1)S(1)} %collective-permute-done.6.refs_0_, ...), custom_call_target="tpu_custom_call" | custom-call | flops 301989888 | bytes 2097152 | tf_op jit(solution)/shard_map/context_states/pallas_call | solution.py:128
  27.9 0.2 collective-permute-start.9
  28.1 0.4 collective-permute-start.10
  28.5 1.4 %context_states.4.own_ref = f32[3,9,32,128]{3,2,1,0:T(8,128)S(1)} custom-call(bf16[512,1024]{1,0:T(8,128)(2,1)S(1)} %get-tuple-element.13.key_ref, bf16[512,1024]{1,0:T(8,128)(2,1)S(1)} %get-tuple-element.14.value_ref, f32[1,256]{1,0:T(1,128)S(1)} %fusion.1.column_slot_ref, bf16[9,32,128]{2,1,0:T(8,128)(2,1)S(1)} %collective-permute-done.refs_0_, ...), custom_call_target="tpu_custom_call" | custom-call | flops 301989888 | bytes 2097152 | tf_op jit(solution)/shard_map/context_states/pallas_call | solution.py:128
  29.9 0.0 copy-start.1
  29.9 0.0 copy-start.4
  30.0 1.0 %pair_states.1 = (s16[9,32,128]{2,1,0:T(8,128)(2,1)S(1)}, s16[9,32,128]{2,1,0:T(8,128)(2,1)S(1)}, s16[9,32,128]{2,1,0:T(8,128)(2,1)S(1)}) custom-call(f32[3,9,32,128]{3,2,1,0:T(8,128)S(1)} %context_states.4.own_ref, f32[3,9,32,128]{3,2,1,0:T(8,128)S(1)} %collective-permute-done.9.other_ref), custom_call_target="tpu_custom_call" | custom-call | tf_op jit(solution)/shard_map/pair_states/pallas_call | solution.py:217
  31.0 1.4 %context_states.7 = f32[1,9,32,128]{3,2,1,0:T(8,128)S(1)} custom-call(bf16[512,1024]{1,0:T(8,128)(2,1)S(1)} %get-tuple-element.13.key_ref, bf16[512,1024]{1,0:T(8,128)(2,1)S(1)} %get-tuple-element.14.value_ref, f32[1,256]{1,0:T(1,128)S(1)} %fusion.1.column_slot_ref, bf16[9,32,128]{2,1,0:T(8,128)(2,1)S(1)} %collective-permute-done.10.refs_0_, ...), custom_call_target="tpu_custom_call" | custom-call | flops 100663296 | bytes 2097152 | tf_op jit(solution)/shard_map/context_states/pallas_call | solution.py:128
  32.3 0.2 collective-permute-start.11
  32.6 3.0 %collective-permute-start.13 = (s16[9,32,128]{2,1,0:T(8,128)(2,1)S(1)}, s16[9,32,128]{2,1,0:T(8,128)(2,1)S(1)}, u32[]{:S(2)}, u32[]{:S(2)}) collective-permute-start(s16[9,32,128]{2,1,0:T(8,128)(2,1)S(1)} %get-tuple-element.17), channel_id=1, source_target_pairs={{0,16},{4,20},{8,24},{12,28},{16,0},{20,4},{24,8},{28,12},{1,17},{... | collective-permute-start | bytes 221192 | tf_op jit(solution)/shard_map/ppermute | solution.py:295
  35.6 1.3 %collective-permute-start.14 = (s16[9,32,128]{2,1,0:T(8,128)(2,1)S(1)}, s16[9,32,128]{2,1,0:T(8,128)(2,1)S(1)}, u32[]{:S(2)}, u32[]{:S(2)}) collective-permute-start(s16[9,32,128]{2,1,0:T(8,128)(2,1)S(1)} %get-tuple-element.18), channel_id=1, source_target_pairs={{0,24},{4,28},{8,16},{12,20},{16,8},{20,12},{24,0},{28,4},{1,25},{... | collective-permute-start | bytes 221192 | tf_op jit(solution)/shard_map/ppermute | solution.py:295
  37.6 3.2 %suffix_state.1.suffix_ref = f32[9,32,128]{2,1,0:T(8,128)S(1)} custom-call(s32[1]{0:T(128)S(6)} %copy.13.length_ref, bf16[9,32,128]{2,1,0:T(8,128)(2,1)S(1)} %get-tuple-element.12.query_ref.refs_0_, bf16[256,2,1024]{2,1,0:T(2,128)(2,1)S(1)} %bitcast.14, bf16[4,1024]{1,0:T(4,128)(2,1)S(1)} %bitcast.17, bf16[4,1024]{1,0:T(4,128)(2,1)S(1)} %bitcast.18, ...), custom_call_target="tpu_custom_call" | custom-call | flops 33554432 | bytes 2097152 | tf_op jit(solution)/shard_map/suffix_state/pallas_call | solution.py:166
  40.8 1.4 %context_states.6.own_ref = f32[1,9,32,128]{3,2,1,0:T(8,128)S(1)} custom-call(bf16[512,1024]{1,0:T(8,128)(2,1)S(1)} %get-tuple-element.13.key_ref, bf16[512,1024]{1,0:T(8,128)(2,1)S(1)} %get-tuple-element.14.value_ref, f32[1,256]{1,0:T(1,128)S(1)} %fusion.1.column_slot_ref, bf16[9,32,128]{2,1,0:T(8,128)(2,1)S(1)} %get-tuple-element.12.query_ref.refs_0_, ...), custom_call_target="tpu_custom_call" | custom-call | flops 100663296 | bytes 2097152 | tf_op jit(solution)/shard_map/context_states/pallas_call | solution.py:128
  42.2 1.0 %final_output.1 = bf16[8,32,128]{2,1,0:T(8,128)(2,1)} custom-call(f32[9,32,128]{2,1,0:T(8,128)S(1)} %suffix_state.1.suffix_ref, f32[1,9,32,128]{3,2,1,0:T(8,128)S(1)} %context_states.6.own_ref, f32[1,9,32,128]{3,2,1,0:T(8,128)S(1)} %collective-permute-done.11.other_ref, s16[9,32,128]{2,1,0:T(8,128)(2,1)S(1)} %collective-permute-done.12.refs_0_, ...), custom_call_target="tpu_custom_call" | custom-call | tf_op jit(solution)/shard_map/final_output/pallas_call | solution.py:248
  (22 shorter events, 0.1 us)
Async XLA Ops:
  0.7 1.0 %copy-start.2 = (bf16[1,64,2,1024]{3,2,1,0:T(2,128)(2,1)S(1)}, bf16[1,64,2,1024]{3,2,1,0:T(2,128)(2,1)}, u32[]{:S(2)}) copy-start(bf16[1,64,2,1024]{3,2,1,0:T(2,128)(2,1)} %param.11) | copy-start | bytes 786436
  1.6 0.8 %copy-start.3 = (bf16[1,4,8192]{2,1,0:T(4,128)(2,1)S(1)}, bf16[1,4,8192]{2,1,0:T(4,128)(2,1)}, u32[]{:S(2)}) copy-start(bf16[1,4,8192]{2,1,0:T(4,128)(2,1)} %param.9) | copy-start | bytes 196612
  2.4 0.7 %copy-start.6 = (s32[4]{0:T(128)S(1)}, s32[4]{0:T(128)}, u32[]{:S(2)}) copy-start(s32[4]{0:T(128)} %owner_ref.1) | copy-start | bytes 52
  4.2 22.2 %collective-permute-start.3 = (bf16[2,64,1024]{2,1,0:T(8,128)(2,1)S(1)}, bf16[2,64,1024]{2,1,0:T(8,128)(2,1)S(1)}, u32[]{:S(2)}, u32[]{:S(2)}) collective-permute-start(bf16[2,64,1024]{2,1,0:T(8,128)(2,1)S(1)} %get-tuple-element.15.refs_3_.refs_1_), channel_id=1, source_target_pairs={{0,1},{1,0},{2,3},{3,2},{4,5},{5,4},{6,7},{7,6},{8,9},{9,8},{10,11... | collective-permute-start | bytes 786440 | tf_op jit(solution)/shard_map/ppermute | solution.py:280
  7.2 19.2 %collective-permute-start.4 = (bf16[2,64,1024]{2,1,0:T(8,128)(2,1)S(1)}, bf16[2,64,1024]{2,1,0:T(8,128)(2,1)S(1)}, u32[]{:S(2)}, u32[]{:S(2)}) collective-permute-start(bf16[2,64,1024]{2,1,0:T(8,128)(2,1)S(1)} %get-tuple-element.15.refs_3_.refs_1_), channel_id=1, source_target_pairs={{0,2},{1,3},{2,0},{3,1},{4,6},{5,7},{6,4},{7,5},{8,10},{9,11},{10,... | collective-permute-start | bytes 786440 | tf_op jit(solution)/shard_map/ppermute | solution.py:280
  8.8 17.7 %collective-permute-start.5 = (bf16[2,64,1024]{2,1,0:T(8,128)(2,1)S(1)}, bf16[2,64,1024]{2,1,0:T(8,128)(2,1)S(1)}, u32[]{:S(2)}, u32[]{:S(2)}) collective-permute-start(bf16[2,64,1024]{2,1,0:T(8,128)(2,1)S(1)} %get-tuple-element.15.refs_3_.refs_1_), channel_id=1, source_target_pairs={{0,3},{1,2},{2,1},{3,0},{4,7},{5,6},{6,5},{7,4},{8,11},{9,10},{10,... | collective-permute-start | bytes 786440 | tf_op jit(solution)/shard_map/ppermute | solution.py:280
  8.8 5.1 %collective-permute-start = (bf16[9,32,128]{2,1,0:T(8,128)(2,1)S(1)}, bf16[9,32,128]{2,1,0:T(8,128)(2,1)S(1)}, u32[]{:S(2)}, u32[]{:S(2)}) collective-permute-start(bf16[9,32,128]{2,1,0:T(8,128)(2,1)S(1)} %get-tuple-element.12.query_ref.refs_0_), channel_id=1, source_target_pairs={{0,8},{4,12},{8,0},{12,4},{16,24},{20,28},{24,16},{28,20},{1,9},{5... | collective-permute-start | bytes 221192 | tf_op jit(solution)/shard_map/ppermute | solution.py:285
  10.8 7.6 %collective-permute-start.1 = (bf16[9,32,128]{2,1,0:T(8,128)(2,1)S(1)}, bf16[9,32,128]{2,1,0:T(8,128)(2,1)S(1)}, u32[]{:S(2)}, u32[]{:S(2)}) collective-permute-start(bf16[9,32,128]{2,1,0:T(8,128)(2,1)S(1)} %get-tuple-element.12.query_ref.refs_0_), channel_id=1, source_target_pairs={{0,16},{4,20},{8,24},{12,28},{16,0},{20,4},{24,8},{28,12},{1,17},{... | collective-permute-start | bytes 221192 | tf_op jit(solution)/shard_map/ppermute | solution.py:285
  13.9 10.7 %collective-permute-start.2 = (bf16[9,32,128]{2,1,0:T(8,128)(2,1)S(1)}, bf16[9,32,128]{2,1,0:T(8,128)(2,1)S(1)}, u32[]{:S(2)}, u32[]{:S(2)}) collective-permute-start(bf16[9,32,128]{2,1,0:T(8,128)(2,1)S(1)} %get-tuple-element.12.query_ref.refs_0_), channel_id=1, source_target_pairs={{0,24},{4,28},{8,16},{12,20},{16,8},{20,12},{24,0},{28,4},{1,25},{... | collective-permute-start | bytes 221192 | tf_op jit(solution)/shard_map/ppermute | solution.py:285
  18.4 6.8 %collective-permute-start.6 = (bf16[9,32,128]{2,1,0:T(8,128)(2,1)S(1)}, bf16[9,32,128]{2,1,0:T(8,128)(2,1)S(1)}, u32[]{:S(2)}, u32[]{:S(2)}) collective-permute-start(bf16[9,32,128]{2,1,0:T(8,128)(2,1)S(1)} %collective-permute-done.refs_0_), channel_id=1, source_target_pairs={{0,4},{4,0},{8,12},{12,8},{16,20},{20,16},{24,28},{28,24},{1,5},{5... | collective-permute-start | bytes 221192 | tf_op jit(solution)/shard_map/ppermute | solution.py:287
  18.4 1.6 %copy-start = (bf16[512,2,1024]{2,1,0:T(2,128)(2,1)S(1)}, bf16[512,2,1024]{2,1,0:T(2,128)(2,1)}, u32[]{:S(2)}) copy-start(bf16[512,2,1024]{2,1,0:T(2,128)(2,1)} %paired_ref.1) | copy-start | bytes 6291460
  24.6 1.5 %collective-permute-start.7 = (bf16[9,32,128]{2,1,0:T(8,128)(2,1)S(1)}, bf16[9,32,128]{2,1,0:T(8,128)(2,1)S(1)}, u32[]{:S(2)}, u32[]{:S(2)}) collective-permute-start(bf16[9,32,128]{2,1,0:T(8,128)(2,1)S(1)} %collective-permute-done.1.refs_1_), channel_id=1, source_target_pairs={{0,4},{4,0},{8,12},{12,8},{16,20},{20,16},{24,28},{28,24},{1,5},{5... | collective-permute-start | bytes 221192 | tf_op jit(solution)/shard_map/ppermute | solution.py:287
  25.1 1.3 %collective-permute-start.8 = (bf16[9,32,128]{2,1,0:T(8,128)(2,1)S(1)}, bf16[9,32,128]{2,1,0:T(8,128)(2,1)S(1)}, u32[]{:S(2)}, u32[]{:S(2)}) collective-permute-start(bf16[9,32,128]{2,1,0:T(8,128)(2,1)S(1)} %collective-permute-done.2.refs_2_), channel_id=1, source_target_pairs={{0,4},{4,0},{8,12},{12,8},{16,20},{20,16},{24,28},{28,24},{1,5},{5... | collective-permute-start | bytes 221192 | tf_op jit(solution)/shard_map/ppermute | solution.py:287
  27.9 2.1 %collective-permute-start.9 = (f32[3,9,32,128]{3,2,1,0:T(8,128)S(1)}, f32[3,9,32,128]{3,2,1,0:T(8,128)S(1)}, u32[]{:S(2)}, u32[]{:S(2)}) collective-permute-start(f32[3,9,32,128]{3,2,1,0:T(8,128)S(1)} %context_states.5), channel_id=1, source_target_pairs={{0,4},{4,0},{8,12},{12,8},{16,20},{20,16},{24,28},{28,24},{1,5},{5... | collective-permute-start | bytes 1327112 | tf_op jit(solution)/shard_map/ppermute | solution.py:293
  28.1 2.9 %collective-permute-start.10 = (bf16[9,32,128]{2,1,0:T(8,128)(2,1)S(1)}, bf16[9,32,128]{2,1,0:T(8,128)(2,1)S(1)}, u32[]{:S(2)}, u32[]{:S(2)}) collective-permute-start(bf16[9,32,128]{2,1,0:T(8,128)(2,1)S(1)} %get-tuple-element.12.query_ref.refs_0_), channel_id=1, source_target_pairs={{0,4},{4,0},{8,12},{12,8},{16,20},{20,16},{24,28},{28,24},{1,5},{5... | collective-permute-start | bytes 221192 | tf_op jit(solution)/shard_map/ppermute | solution.py:287
  29.9 7.7 %copy-start.1 = (bf16[1,256,2,1024]{3,2,1,0:T(2,128)(2,1)S(1)}, bf16[1,256,2,1024]{3,2,1,0:T(2,128)(2,1)}, u32[]{:S(2)}) copy-start(bf16[1,256,2,1024]{3,2,1,0:T(2,128)(2,1)} %param.14) | copy-start | bytes 3145732
  29.9 7.7 %copy-start.4 = (bf16[1,4,1024]{2,1,0:T(4,128)(2,1)S(1)}, bf16[1,4,1024]{2,1,0:T(4,128)(2,1)}, u32[]{:S(2)}) copy-start(bf16[1,4,1024]{2,1,0:T(4,128)(2,1)} %param.16) | copy-start | bytes 24580
  29.9 7.7 %copy-start.5 = (bf16[1,4,1024]{2,1,0:T(4,128)(2,1)S(1)}, bf16[1,4,1024]{2,1,0:T(4,128)(2,1)}, u32[]{:S(2)}) copy-start(bf16[1,4,1024]{2,1,0:T(4,128)(2,1)} %param.17) | copy-start | bytes 24580
  32.3 9.9 %collective-permute-start.11 = (f32[1,9,32,128]{3,2,1,0:T(8,128)S(1)}, f32[1,9,32,128]{3,2,1,0:T(8,128)S(1)}, u32[]{:S(2)}, u32[]{:S(2)}) collective-permute-start(f32[1,9,32,128]{3,2,1,0:T(8,128)S(1)} %context_states.7), channel_id=1, source_target_pairs={{0,4},{4,0},{8,12},{12,8},{16,20},{20,16},{24,28},{28,24},{1,5},{5... | collective-permute-start | bytes 442376 | tf_op jit(solution)/shard_map/ppermute | solution.py:303
  32.6 9.6 %collective-permute-start.12 = (s16[9,32,128]{2,1,0:T(8,128)(2,1)S(1)}, s16[9,32,128]{2,1,0:T(8,128)(2,1)S(1)}, u32[]{:S(2)}, u32[]{:S(2)}) collective-permute-start(s16[9,32,128]{2,1,0:T(8,128)(2,1)S(1)} %get-tuple-element.16.refs_0_.refs_5_), channel_id=1, source_target_pairs={{0,8},{4,12},{8,0},{12,4},{16,24},{20,28},{24,16},{28,20},{1,9},{5... | collective-permute-start | bytes 221192 | tf_op jit(solution)/shard_map/ppermute | solution.py:295
  32.6 9.6 %collective-permute-start.13 = (s16[9,32,128]{2,1,0:T(8,128)(2,1)S(1)}, s16[9,32,128]{2,1,0:T(8,128)(2,1)S(1)}, u32[]{:S(2)}, u32[]{:S(2)}) collective-permute-start(s16[9,32,128]{2,1,0:T(8,128)(2,1)S(1)} %get-tuple-element.17), channel_id=1, source_target_pairs={{0,16},{4,20},{8,24},{12,28},{16,0},{20,4},{24,8},{28,12},{1,17},{... | collective-permute-start | bytes 221192 | tf_op jit(solution)/shard_map/ppermute | solution.py:295
  35.6 6.6 %collective-permute-start.14 = (s16[9,32,128]{2,1,0:T(8,128)(2,1)S(1)}, s16[9,32,128]{2,1,0:T(8,128)(2,1)S(1)}, u32[]{:S(2)}, u32[]{:S(2)}) collective-permute-start(s16[9,32,128]{2,1,0:T(8,128)(2,1)S(1)} %get-tuple-element.18), channel_id=1, source_target_pairs={{0,24},{4,28},{8,16},{12,20},{16,8},{20,12},{24,0},{28,4},{1,25},{... | collective-permute-start | bytes 221192 | tf_op jit(solution)/shard_map/ppermute | solution.py:295

commit v3 on v2

--- a/solution.py
+++ b/solution.py
@@ -36,6 +36,10 @@
     return [pl.BlockSpec(memory_space=pl.ANY)] * count
 
 
+def in_hbm(count):
+    return [pl.BlockSpec(memory_space=pltpu.HBM)] * count
+
+
 def in_vmem(count):
     return [pl.BlockSpec(memory_space=pltpu.VMEM)] * count
 
@@ -44,46 +48,83 @@
     return [pl.BlockSpec(memory_space=pltpu.SMEM)] * count
 
 
-def prepare_kernel(tab_count, session_ref, owner_ref, query_ref, tab_ref, message_ref, block_ref):
+def prepare_kernel(
+    session, owner_hbm, query_hbm, tab_hbm, message_ref, block_ref, paired, owner, sems
+):
+    moves = [
+        (tab_hbm, paired),
+        (owner_hbm, owner),
+        (query_hbm, message_ref.at[pl.ds(0, KEY_VALUE_HEADS)]),
+    ]
+    copies = [pltpu.make_async_copy(*move, sems.at[i]) for i, move in enumerate(moves)]
+    for copy in copies:
+        copy.start()
+    copies[1].wait()
     slot = jnp.int32(0)
-    for k in range(tab_count):
-        slot = jnp.where(session_ref[0] == k, owner_ref[k], slot)
-    message_ref[:KEY_VALUE_HEADS] = query_ref[...]
+    for k in range(owner.shape[0]):
+        slot = jnp.where(session[0] == k, owner[k], slot)
     filled = jnp.full(message_ref.shape[1:], slot.astype(jnp.float32), jnp.float32)
     message_ref[KEY_VALUE_HEADS] = filled.astype(jnp.bfloat16)
-    block_ref[0] = tab_ref[:, 0, :]
-    block_ref[1] = tab_ref[:, 1, :]
+    copies[0].wait()
+    block_ref[0] = paired[:, 0, :]
+    block_ref[1] = paired[:, 1, :]
+    copies[2].wait()
+
+
+def stay(arrays):
+    return [pltpu.with_memory_space_constraint(array, pltpu.HBM) for array in arrays]
 
 
 def prepare(session_tab, tab_owner, query, tab):
     return pl.pallas_call(
-        functools.partial(prepare_kernel, tab_owner.shape[0]),
-        in_specs=in_smem(2) + in_vmem(2),
+        prepare_kernel,
+        in_specs=in_smem(1) + in_hbm(3),
+        out_specs=in_vmem(2),
         out_shape=[
             jax.ShapeDtypeStruct((KEY_VALUE_HEADS + 1,) + query.shape[1:], jnp.bfloat16),
             jax.ShapeDtypeStruct((2, tab.shape[0], tab.shape[2]), jnp.bfloat16),
         ],
+        scratch_shapes=[
+            pltpu.VMEM(tab.shape, tab.dtype),
+            pltpu.SMEM(tab_owner.shape, tab_owner.dtype),
+            pltpu.SemaphoreType.DMA((4,)),
+        ],
         compiler_params=pltpu.CompilerParams(vmem_limit_bytes=16 * MIB),
         name="prepare",
-    )(session_tab, tab_owner, query, tab)
-
-
-def split_kernel(paired_ref, key_ref, value_ref):
-    key_ref[...] = paired_ref[:, 0, :]
-    value_ref[...] = paired_ref[:, 1, :]
-
-
-def split_pairs(paired):
+    )(session_tab, *stay([tab_owner, query, tab]))
+
+
+def split_kernel(chunks, paired_ref, key_ref, value_ref, buffer, sems):
+    rows = key_ref.shape[0] // chunks
+    copies = [
+        pltpu.make_async_copy(paired_ref.at[pl.ds(i * rows, rows)], buffer.at[i], sems.at[i])
+        for i in range(chunks)
+    ]
+    for copy in copies:
+        copy.start()
+    for i, copy in enumerate(copies):
+        copy.wait()
+        key_ref[pl.ds(i * rows, rows)] = buffer[i, :, 0, :]
+        value_ref[pl.ds(i * rows, rows)] = buffer[i, :, 1, :]
+
+
+def split_pairs(paired, chunks=8):
     shape = jax.ShapeDtypeStruct((paired.shape[0], paired.shape[2]), paired.dtype)
     return pl.pallas_call(
-        split_kernel,
+        functools.partial(split_kernel, chunks),
+        in_specs=in_hbm(1),
+        out_specs=in_vmem(2),
         out_shape=[shape, shape],
+        scratch_shapes=[
+            pltpu.VMEM((chunks, paired.shape[0] // chunks) + paired.shape[1:], paired.dtype),
+            pltpu.SemaphoreType.DMA((chunks,)),
+        ],
         cost_estimate=pl.CostEstimate(
             flops=8 * paired.size, transcendentals=0, bytes_accessed=4 * paired.size
         ),
         compiler_params=pltpu.CompilerParams(vmem_limit_bytes=16 * MIB),
         name="split_pairs",
-    )(paired)
+    )(*stay([paired]))
 
 
 def block_softmax(score_parts, value_parts):
@@ -99,7 +140,7 @@
     return summed / total, largest * SCALE + jnp.log(total)
 
 
-def context_kernel(members, slots, after, key_ref, value_ref, column_slot_ref, *refs):
+def context_kernel(members, slots, key_ref, value_ref, column_slot_ref, *refs):
     query_refs, tab_refs, out_ref = refs[:members], refs[members : members + slots], refs[-1]
     rows = query_refs[0].shape[1]
     owner = jnp.concatenate([q[KEY_VALUE_HEADS, :, 0:1] for q in query_refs], axis=0)
@@ -121,13 +162,13 @@
         out_ref[i, KEY_VALUE_HEADS] = ends[i * rows : (i + 1) * rows]
 
 
-def context_states(query_messages, keys, values, column_slot, tabs, after=()):
+def context_states(query_messages, keys, values, column_slot, tabs):
     members, rows = len(query_messages), query_messages[0].shape[1]
     key_count = keys.shape[0] + column_slot.shape[1]
     work = members * rows * KEY_VALUE_HEADS * key_count
     return pl.pallas_call(
-        functools.partial(context_kernel, members, len(tabs), len(after)),
-        in_specs=in_vmem(3 + members + len(tabs)) + in_any(len(after)),
+        functools.partial(context_kernel, members, len(tabs)),
+        in_specs=in_vmem(3 + members + len(tabs)),
         out_shape=jax.ShapeDtypeStruct(
             (members, KEY_VALUE_HEADS + 1, rows, HEAD_SIZE), jnp.float32
         ),
@@ -136,7 +177,7 @@
             flops=4 * work * HEAD_SIZE, transcendentals=work, bytes_accessed=4 * keys.size
         ),
         name="context_states",
-    )(keys, values, column_slot, *query_messages, *tabs, *after)
+    )(keys, values, column_slot, *query_messages, *tabs)
 
 
 def suffix_kernel(steps, length_ref, query_ref, pair_ref, new_key_ref, new_value_ref, *refs):
@@ -213,10 +254,10 @@
 
 
 def pair_states(own, other):
-    members, shape = own.shape[0], own.shape[1:]
+    far, shape = own.shape[0] - 1, own.shape[1:]
     return pl.pallas_call(
         pair_kernel,
-        out_shape=[jax.ShapeDtypeStruct(shape, jnp.int16)] * members,
+        out_shape=[jax.ShapeDtypeStruct(shape, jnp.int16)] * far,
         compiler_params=pltpu.CompilerParams(vmem_limit_bytes=16 * MIB),
         name="pair_states",
     )(own, other)
@@ -224,7 +265,8 @@
 
 def final_kernel(suffix_ref, own_ref, other_ref, *refs):
     coded_refs, out_ref = refs[:-1], refs[-1]
-    plain_refs = (suffix_ref, own_ref.at[0], other_ref.at[0])
+    near = own_ref.shape[0] - 1
+    plain_refs = (suffix_ref, own_ref.at[near], other_ref.at[near])
     ends = [r[KEY_VALUE_HEADS] for r in plain_refs]
     factors = []
     for r in coded_refs:
@@ -279,29 +321,25 @@
     tabs = [tab_block] + [
         lax.ppermute(tab_block, "tab", swap(tab_count, k)) for k in range(1, tab_count)
     ]
+    far = [lax.ppermute(message, "ctx", swap(ctx_count, 2 * k)) for k in range(1, pair_count)]
     places = jnp.arange(tab_count * tab_rows, dtype=jnp.int32) // tab_rows
     column_slot = (places ^ lax.axis_index("tab")).astype(jnp.float32)[None]
-    column = [message] + [
-        lax.ppermute(message, "ctx", swap(ctx_count, 2 * k)) for k in range(1, pair_count)
-    ]
+
+    keys, values = split_pairs(prefix_key_value)
+    far, keys = lax.optimization_barrier((far, keys))
+    column = far + [message]
     other_column = [lax.ppermute(m, "ctx", swap(ctx_count, 1)) for m in column]
-
-    keys, values = split_pairs(prefix_key_value)
-    shared = (keys, values, column_slot, tabs)
-    other_far = context_states(other_column[1:], *shared)
-    own_far = context_states(column[1:], *shared)
-    coded = pair_states(own_far, lax.ppermute(other_far, "ctx", swap(ctx_count, 1)))
+    theirs = context_states(other_column, keys, values, column_slot, tabs)
+    ours = context_states(column, keys, values, column_slot, tabs)
+    theirs = lax.ppermute(theirs, "ctx", swap(ctx_count, 1))
+    coded = pair_states(ours, theirs)
     received = [
         lax.ppermute(c, "ctx", swap(ctx_count, 2 * k)) for k, c in enumerate(coded, start=1)
     ]
-    other_near = context_states(other_column[:1], *shared, after=coded[:1])
-    own_near = context_states(column[:1], *shared, after=coded[:1])
     suffix = suffix_state(
-        message, suffix_key_value[0], suffix_len, token_keys[0], token_values[0], after=coded[:1]
-    )
-    result = final_output(
-        suffix, own_near, lax.ppermute(other_near, "ctx", swap(ctx_count, 1)), received
-    )
+        message, suffix_key_value[0], suffix_len, token_keys[0], token_values[0], after=coded
+    )
+    result = final_output(suffix, ours, theirs, received)
     result = result.reshape(KEY_VALUE_HEADS, -1, steps, HEAD_SIZE)
     return result.transpose(2, 0, 1, 3).reshape(queries.shape)
 

time: 43.5 us -> 37.4 us (0.86)
  local copies, waits for them, and re-layouts: 4.05 us -> 0.02 us
  starting transfers between devices: 18.3 us -> 14.8 us
  waiting for transfers between devices: 2.84 us -> 4.91 us
  Pallas kernels: 16.5 us -> 16 us
    unnamed x14 -> x6, local copies, waits for them, and re-layouts: 4.05 us -> 0.02 us
    ppermute x3, starting transfers between devices: 7.95 us -> 5.76 us  [shards(): lax.ppermute(message, 'ctx', swap(ctx_count, 2 * k))]
    ppermute x3, waiting for transfers between devices: 0.01 us -> 1.66 us  [shards(): lax.ppermute(tab_block, 'tab', swap(tab_count, k))]
    ppermute x3, waiting for transfers between devices: 1.64 us -> 0.01 us  [shards(): lax.ppermute(message, 'ctx', swap(ctx_count, 2 * k))]
    ppermute x3, starting transfers between devices: 4.54 us -> 3.49 us  [shards(): lax.ppermute(tab_block, 'tab', swap(tab_count, k))]
    ppermute x3, waiting for transfers between devices: 0.01 us -> 0.9 us  [shards(): lax.ppermute(c, 'ctx', swap(ctx_count, 2 * k))]
    ppermute x4, waiting for transfers between devices: 1.18 us -> 1.79 us  [shards(): other_column = [lax.ppermute(m, 'ctx', swap(ctx_count, 1)) for m in column]]
    ppermute x2 -> x1, waiting for transfers between devices: 0.01 us -> 0.55 us  [shards(): theirs = lax.ppermute(theirs, 'ctx', swap(ctx_count, 1))]
  transfers between devices with their start and end apart: 15 -> 14, of which waited for: 4 -> 8; matrix products, arithmetic and copies ran while one was open for 0% -> 0% of each run, Pallas kernels for 27% -> 27%
where the time goes in v3:
time: 37.4 us; the launch traced here: 37.2 us
  Pallas kernels  16 us (43%)
  starting transfers between devices  14.8 us (40%)
  waiting for transfers between devices  4.91 us (13%)
  between operations  1.45 us (4%)
    ppermute x3, starting transfers between devices, shards(): lax.ppermute(message, 'ctx', swap(ctx_count, 2 * k))  5.76 us
    pallas_call x1, Pallas kernels, split_pairs(): pl.pallas_call(functools.partial(split_kernel, chunks), in_specs=in_hbm(1...  5.67 us
    ppermute x3, starting transfers between devices, shards(): lax.ppermute(c, 'ctx', swap(ctx_count, 2 * k))  4.44 us
    pallas_call x2, Pallas kernels, context_states(): pl.pallas_call(functools.partial(context_kernel, members, len(tabs)), in_...  3.74 us
    ppermute x3, starting transfers between devices, shards(): lax.ppermute(tab_block, 'tab', swap(tab_count, k))  3.49 us
    pallas_call x1, Pallas kernels, suffix_state(): pl.pallas_call(functools.partial(suffix_kernel, steps), in_specs=in_smem(...  3.01 us
    ppermute x4, waiting for transfers between devices, shards(): other_column = [lax.ppermute(m, 'ctx', swap(ctx_count, 1)) for m in column]  1.79 us
    ppermute x3, waiting for transfers between devices, shards(): lax.ppermute(tab_block, 'tab', swap(tab_count, k))  1.66 us
  transfers between devices with their start and end apart: 14, of which 8 were waited for; matrix products, arithmetic and copies ran while one was open for 0% of the time, Pallas kernels for 27%

profile of v3, /device:TPU:0, one launch (start us, length us, event | category | flops | bytes accessed | tf_op | source)
XLA Modules:
  0.0 37.2 jit_solution(2451881858637974166)
XLA Ops:
  0.7 1.6 %prepare.1 = (bf16[9,32,128]{2,1,0:T(8,128)(2,1)S(1)}, bf16[2,64,1024]{2,1,0:T(8,128)(2,1)S(1)}) custom-call(s32[1]{0:T(128)S(6)} %copy.12.session, s32[4]{0:T(128)} %owner_hbm.1, bf16[8,32,128]{2,1,0:T(8,128)(2,1)} %bitcast.18, bf16[64,2,1024]{2,1,0:T(2,128)(2,1)} %bitcast.17), custom_call_target="tpu_custom_call" | custom-call | tf_op jit(solution)/shard_map/prepare/pallas_call | solution.py:79
  2.2 5.1 %collective-permute-start.2 = (bf16[9,32,128]{2,1,0:T(8,128)(2,1)S(1)}, bf16[9,32,128]{2,1,0:T(8,128)(2,1)S(1)}, u32[]{:S(2)}, u32[]{:S(2)}) collective-permute-start(bf16[9,32,128]{2,1,0:T(8,128)(2,1)S(1)} %get-tuple-element.16.refs_3_.query_ref), channel_id=1, source_target_pairs={{0,24},{4,28},{8,16},{12,20},{16,8},{20,12},{24,0},{28,4},{1,25},{... | collective-permute-start | bytes 221192 | tf_op jit(solution)/shard_map/ppermute | solution.py:324
  7.3 2.4 %collective-permute-start.5 = (bf16[2,64,1024]{2,1,0:T(8,128)(2,1)S(1)}, bf16[2,64,1024]{2,1,0:T(8,128)(2,1)S(1)}, u32[]{:S(2)}, u32[]{:S(2)}) collective-permute-start(bf16[2,64,1024]{2,1,0:T(8,128)(2,1)S(1)} %get-tuple-element.23.refs_4_), channel_id=1, source_target_pairs={{0,3},{1,2},{2,1},{3,0},{4,7},{5,6},{6,5},{7,4},{8,11},{9,10},{10,... | collective-permute-start | bytes 786440 | tf_op jit(solution)/shard_map/ppermute | solution.py:322
  9.8 0.5 %collective-permute-start.4 = (bf16[2,64,1024]{2,1,0:T(8,128)(2,1)S(1)}, bf16[2,64,1024]{2,1,0:T(8,128)(2,1)S(1)}, u32[]{:S(2)}, u32[]{:S(2)}) collective-permute-start(bf16[2,64,1024]{2,1,0:T(8,128)(2,1)S(1)} %get-tuple-element.23.refs_4_), channel_id=1, source_target_pairs={{0,2},{1,3},{2,0},{3,1},{4,6},{5,7},{6,4},{7,5},{8,10},{9,11},{10,... | collective-permute-start | bytes 786440 | tf_op jit(solution)/shard_map/ppermute | solution.py:322
  10.3 0.5 %collective-permute-start.3 = (bf16[2,64,1024]{2,1,0:T(8,128)(2,1)S(1)}, bf16[2,64,1024]{2,1,0:T(8,128)(2,1)S(1)}, u32[]{:S(2)}, u32[]{:S(2)}) collective-permute-start(bf16[2,64,1024]{2,1,0:T(8,128)(2,1)S(1)} %get-tuple-element.23.refs_4_), channel_id=1, source_target_pairs={{0,1},{1,0},{2,3},{3,2},{4,5},{5,4},{6,7},{7,6},{8,9},{9,8},{10,11... | collective-permute-start | bytes 786440 | tf_op jit(solution)/shard_map/ppermute | solution.py:322
  10.8 0.6 %collective-permute-start = (bf16[9,32,128]{2,1,0:T(8,128)(2,1)S(1)}, bf16[9,32,128]{2,1,0:T(8,128)(2,1)S(1)}, u32[]{:S(2)}, u32[]{:S(2)}) collective-permute-start(bf16[9,32,128]{2,1,0:T(8,128)(2,1)S(1)} %get-tuple-element.16.refs_3_.query_ref), channel_id=1, source_target_pairs={{0,8},{4,12},{8,0},{12,4},{16,24},{20,28},{24,16},{28,20},{1,9},{5... | collective-permute-start | bytes 221192 | tf_op jit(solution)/shard_map/ppermute | solution.py:324
  11.5 5.7 %split_pairs.1 = (bf16[512,1024]{1,0:T(8,128)(2,1)S(1)}, bf16[512,1024]{1,0:T(8,128)(2,1)S(1)}) custom-call(bf16[512,2,1024]{2,1,0:T(2,128)(2,1)} %paired_ref.1), custom_call_target="tpu_custom_call" | custom-call | flops 8388608 | bytes 4194304 | tf_op jit(solution)/shard_map/split_pairs/pallas_call | solution.py:113
  17.2 0.1 collective-permute-start.9
  17.3 0.5 %collective-permute-start.6 = (bf16[9,32,128]{2,1,0:T(8,128)(2,1)S(1)}, bf16[9,32,128]{2,1,0:T(8,128)(2,1)}, u32[]{:S(2)}, u32[]{:S(2)}) collective-permute-start(bf16[9,32,128]{2,1,0:T(8,128)(2,1)S(1)} %collective-permute-done.refs_0_), channel_id=1, source_target_pairs={{0,4},{4,0},{8,12},{12,8},{16,20},{20,16},{24,28},{28,24},{1,5},{5... | collective-permute-start | bytes 221192 | tf_op jit(solution)/shard_map/ppermute | solution.py:331
  17.8 0.8 %collective-permute-done.9.refs_3_ = bf16[9,32,128]{2,1,0:T(8,128)(2,1)S(1)} collective-permute-done((bf16[9,32,128]{2,1,0:T(8,128)(2,1)S(1)}, bf16[9,32,128]{2,1,0:T(8,128)(2,1)S(1)}, u32[]{:S(2)}, u32[]{:S(2)}) %collective-permute-start.9) | collective-permute-done | bytes 73760 | tf_op jit(solution)/shard_map/ppermute | solution.py:331
  18.5 0.2 collective-permute-start.7
  18.7 0.1 collective-permute-done.6.refs_0_
  18.8 0.4 collective-permute-start.8
  19.2 0.6 %collective-permute-done.7.refs_1_ = bf16[9,32,128]{2,1,0:T(8,128)(2,1)S(1)} collective-permute-done((bf16[9,32,128]{2,1,0:T(8,128)(2,1)S(1)}, bf16[9,32,128]{2,1,0:T(8,128)(2,1)S(1)}, u32[]{:S(2)}, u32[]{:S(2)}) %collective-permute-start.7) | collective-permute-done | bytes 73760 | tf_op jit(solution)/shard_map/ppermute | solution.py:331
  19.8 0.3 collective-permute-done.8.refs_2_
  20.1 0.0 collective-permute-done.5.refs_7_
  20.1 1.6 %collective-permute-done.4.refs_6_ = bf16[2,64,1024]{2,1,0:T(8,128)(2,1)S(1)} collective-permute-done((bf16[2,64,1024]{2,1,0:T(8,128)(2,1)S(1)}, bf16[2,64,1024]{2,1,0:T(8,128)(2,1)S(1)}, u32[]{:S(2)}, u32[]{:S(2)}) %collective-permute-start.4) | collective-permute-done | bytes 262176 | tf_op jit(solution)/shard_map/ppermute | solution.py:322
  21.6 0.1 collective-permute-done.3.refs_5_
  21.7 2.3 %context_states.3 = f32[4,9,32,128]{3,2,1,0:T(8,128)S(1)} custom-call(bf16[512,1024]{1,0:T(8,128)(2,1)S(1)} %get-tuple-element.18.key_ref, bf16[512,1024]{1,0:T(8,128)(2,1)S(1)} %get-tuple-element.19.value_ref, f32[1,256]{1,0:T(1,128)S(1)} %fusion.1.column_slot_ref, bf16[9,32,128]{2,1,0:T(8,128)(2,1)} %collective-permute-done.6.refs_0_, ...), custom_call_target="tpu_custom_call" | custom-call | flops 402653184 | bytes 2097152 | tf_op jit(solution)/shard_map/context_states/pallas_call | solution.py:169
  24.0 0.0 copy-start
  24.1 0.0 copy-start.1
  24.1 0.0 copy-start.2
  24.1 0.1 collective-permute-start.10
  24.2 1.4 %context_states.2.own_ref = f32[4,9,32,128]{3,2,1,0:T(8,128)S(1)} custom-call(bf16[512,1024]{1,0:T(8,128)(2,1)S(1)} %get-tuple-element.18.key_ref, bf16[512,1024]{1,0:T(8,128)(2,1)S(1)} %get-tuple-element.19.value_ref, f32[1,256]{1,0:T(1,128)S(1)} %fusion.1.column_slot_ref, bf16[9,32,128]{2,1,0:T(8,128)(2,1)S(1)} %collective-permute-done.refs_0_, ...), custom_call_target="tpu_custom_call" | custom-call | flops 402653184 | bytes 2097152 | tf_op jit(solution)/shard_map/context_states/pallas_call | solution.py:169
  25.6 0.5 %collective-permute-done.10.other_ref = f32[4,9,32,128]{3,2,1,0:T(8,128)S(1)} collective-permute-done((f32[4,9,32,128]{3,2,1,0:T(8,128)S(1)}, f32[4,9,32,128]{3,2,1,0:T(8,128)S(1)}, u32[]{:S(2)}, u32[]{:S(2)}) %collective-permute-start.10) | collective-permute-done | bytes 589856 | tf_op jit(solution)/shard_map/ppermute | solution.py:334
  26.1 1.0 %pair_states.1 = (s16[9,32,128]{2,1,0:T(8,128)(2,1)S(1)}, s16[9,32,128]{2,1,0:T(8,128)(2,1)S(1)}, s16[9,32,128]{2,1,0:T(8,128)(2,1)S(1)}) custom-call(f32[4,9,32,128]{3,2,1,0:T(8,128)S(1)} %context_states.2.own_ref, f32[4,9,32,128]{3,2,1,0:T(8,128)S(1)} %collective-permute-done.10.other_ref), custom_call_target="tpu_custom_call" | custom-call | tf_op jit(solution)/shard_map/pair_states/pallas_call | solution.py:258
  27.1 0.1 collective-permute-start.11
  27.2 2.6 %collective-permute-start.12 = (s16[9,32,128]{2,1,0:T(8,128)(2,1)S(1)}, s16[9,32,128]{2,1,0:T(8,128)(2,1)S(1)}, u32[]{:S(2)}, u32[]{:S(2)}) collective-permute-start(s16[9,32,128]{2,1,0:T(8,128)(2,1)S(1)} %get-tuple-element.25.refs_1_), channel_id=1, source_target_pairs={{0,16},{4,20},{8,24},{12,28},{16,0},{20,4},{24,8},{28,12},{1,17},{... | collective-permute-start | bytes 221192 | tf_op jit(solution)/shard_map/ppermute | solution.py:337
  29.9 1.7 %collective-permute-start.13 = (s16[9,32,128]{2,1,0:T(8,128)(2,1)S(1)}, s16[9,32,128]{2,1,0:T(8,128)(2,1)S(1)}, u32[]{:S(2)}, u32[]{:S(2)}) collective-permute-start(s16[9,32,128]{2,1,0:T(8,128)(2,1)S(1)} %get-tuple-element.26.refs_2_), channel_id=1, source_target_pairs={{0,24},{4,28},{8,16},{12,20},{16,8},{20,12},{24,0},{28,4},{1,25},{... | collective-permute-start | bytes 221192 | tf_op jit(solution)/shard_map/ppermute | solution.py:337
  32.3 3.0 %suffix_state.1.suffix_ref = f32[9,32,128]{2,1,0:T(8,128)S(1)} custom-call(s32[1]{0:T(128)S(6)} %copy.13.length_ref, bf16[9,32,128]{2,1,0:T(8,128)(2,1)S(1)} %get-tuple-element.16.refs_3_.query_ref, bf16[256,2,1024]{2,1,0:T(2,128)(2,1)S(1)} %bitcast.14, bf16[4,1024]{1,0:T(4,128)(2,1)S(1)} %bitcast.15, bf16[4,1024]{1,0:T(4,128)(2,1)S(1)} %bitcast.16, ...), custom_call_target="tpu_custom_call" | custom-call | flops 33554432 | bytes 2097152 | tf_op jit(solution)/shard_map/suffix_state/pallas_call | solution.py:207
  35.3 0.9 %collective-permute-done.12.refs_1_ = s16[9,32,128]{2,1,0:T(8,128)(2,1)S(1)} collective-permute-done((s16[9,32,128]{2,1,0:T(8,128)(2,1)S(1)}, s16[9,32,128]{2,1,0:T(8,128)(2,1)S(1)}, u32[]{:S(2)}, u32[]{:S(2)}) %collective-permute-start.12) | collective-permute-done | bytes 73760 | tf_op jit(solution)/shard_map/ppermute | solution.py:337
  36.2 1.0 %final_output.1 = bf16[8,32,128]{2,1,0:T(8,128)(2,1)} custom-call(f32[9,32,128]{2,1,0:T(8,128)S(1)} %suffix_state.1.suffix_ref, f32[4,9,32,128]{3,2,1,0:T(8,128)S(1)} %context_states.2.own_ref, f32[4,9,32,128]{3,2,1,0:T(8,128)S(1)} %collective-permute-done.10.other_ref, s16[9,32,128]{2,1,0:T(8,128)(2,1)S(1)} %collective-permute-done.11.refs_0_, ...), custom_call_target="tpu_custom_call" | custom-call | tf_op jit(solution)/shard_map/final_output/pallas_call | solution.py:290
  (10 shorter events, 0.0 us)
Async XLA Ops:
  2.2 8.6 %collective-permute-start.2 = (bf16[9,32,128]{2,1,0:T(8,128)(2,1)S(1)}, bf16[9,32,128]{2,1,0:T(8,128)(2,1)S(1)}, u32[]{:S(2)}, u32[]{:S(2)}) collective-permute-start(bf16[9,32,128]{2,1,0:T(8,128)(2,1)S(1)} %get-tuple-element.16.refs_3_.query_ref), channel_id=1, source_target_pairs={{0,24},{4,28},{8,16},{12,20},{16,8},{20,12},{24,0},{28,4},{1,25},{... | collective-permute-start | bytes 221192 | tf_op jit(solution)/shard_map/ppermute | solution.py:324
  7.3 12.7 %collective-permute-start.5 = (bf16[2,64,1024]{2,1,0:T(8,128)(2,1)S(1)}, bf16[2,64,1024]{2,1,0:T(8,128)(2,1)S(1)}, u32[]{:S(2)}, u32[]{:S(2)}) collective-permute-start(bf16[2,64,1024]{2,1,0:T(8,128)(2,1)S(1)} %get-tuple-element.23.refs_4_), channel_id=1, source_target_pairs={{0,3},{1,2},{2,1},{3,0},{4,7},{5,6},{6,5},{7,4},{8,11},{9,10},{10,... | collective-permute-start | bytes 786440 | tf_op jit(solution)/shard_map/ppermute | solution.py:322
  9.8 11.8 %collective-permute-start.4 = (bf16[2,64,1024]{2,1,0:T(8,128)(2,1)S(1)}, bf16[2,64,1024]{2,1,0:T(8,128)(2,1)S(1)}, u32[]{:S(2)}, u32[]{:S(2)}) collective-permute-start(bf16[2,64,1024]{2,1,0:T(8,128)(2,1)S(1)} %get-tuple-element.23.refs_4_), channel_id=1, source_target_pairs={{0,2},{1,3},{2,0},{3,1},{4,6},{5,7},{6,4},{7,5},{8,10},{9,11},{10,... | collective-permute-start | bytes 786440 | tf_op jit(solution)/shard_map/ppermute | solution.py:322
  10.3 11.4 %collective-permute-start.3 = (bf16[2,64,1024]{2,1,0:T(8,128)(2,1)S(1)}, bf16[2,64,1024]{2,1,0:T(8,128)(2,1)S(1)}, u32[]{:S(2)}, u32[]{:S(2)}) collective-permute-start(bf16[2,64,1024]{2,1,0:T(8,128)(2,1)S(1)} %get-tuple-element.23.refs_4_), channel_id=1, source_target_pairs={{0,1},{1,0},{2,3},{3,2},{4,5},{5,4},{6,7},{7,6},{8,9},{9,8},{10,11... | collective-permute-start | bytes 786440 | tf_op jit(solution)/shard_map/ppermute | solution.py:322
  10.8 6.3 %collective-permute-start.1 = (bf16[9,32,128]{2,1,0:T(8,128)(2,1)S(1)}, bf16[9,32,128]{2,1,0:T(8,128)(2,1)S(1)}, u32[]{:S(2)}, u32[]{:S(2)}) collective-permute-start(bf16[9,32,128]{2,1,0:T(8,128)(2,1)S(1)} %get-tuple-element.16.refs_3_.query_ref), channel_id=1, source_target_pairs={{0,16},{4,20},{8,24},{12,28},{16,0},{20,4},{24,8},{28,12},{1,17},{... | collective-permute-start | bytes 221192 | tf_op jit(solution)/shard_map/ppermute | solution.py:324
  10.8 6.4 %collective-permute-start = (bf16[9,32,128]{2,1,0:T(8,128)(2,1)S(1)}, bf16[9,32,128]{2,1,0:T(8,128)(2,1)S(1)}, u32[]{:S(2)}, u32[]{:S(2)}) collective-permute-start(bf16[9,32,128]{2,1,0:T(8,128)(2,1)S(1)} %get-tuple-element.16.refs_3_.query_ref), channel_id=1, source_target_pairs={{0,8},{4,12},{8,0},{12,4},{16,24},{20,28},{24,16},{28,20},{1,9},{5... | collective-permute-start | bytes 221192 | tf_op jit(solution)/shard_map/ppermute | solution.py:324
  17.2 1.3 %collective-permute-start.9 = (bf16[9,32,128]{2,1,0:T(8,128)(2,1)S(1)}, bf16[9,32,128]{2,1,0:T(8,128)(2,1)S(1)}, u32[]{:S(2)}, u32[]{:S(2)}) collective-permute-start(bf16[9,32,128]{2,1,0:T(8,128)(2,1)S(1)} %get-tuple-element.16.refs_3_.query_ref), channel_id=1, source_target_pairs={{0,4},{4,0},{8,12},{12,8},{16,20},{20,16},{24,28},{28,24},{1,5},{5... | collective-permute-start | bytes 221192 | tf_op jit(solution)/shard_map/ppermute | solution.py:331
  17.3 1.5 %collective-permute-start.6 = (bf16[9,32,128]{2,1,0:T(8,128)(2,1)S(1)}, bf16[9,32,128]{2,1,0:T(8,128)(2,1)}, u32[]{:S(2)}, u32[]{:S(2)}) collective-permute-start(bf16[9,32,128]{2,1,0:T(8,128)(2,1)S(1)} %collective-permute-done.refs_0_), channel_id=1, source_target_pairs={{0,4},{4,0},{8,12},{12,8},{16,20},{20,16},{24,28},{28,24},{1,5},{5... | collective-permute-start | bytes 221192 | tf_op jit(solution)/shard_map/ppermute | solution.py:331
  18.5 1.3 %collective-permute-start.7 = (bf16[9,32,128]{2,1,0:T(8,128)(2,1)S(1)}, bf16[9,32,128]{2,1,0:T(8,128)(2,1)S(1)}, u32[]{:S(2)}, u32[]{:S(2)}) collective-permute-start(bf16[9,32,128]{2,1,0:T(8,128)(2,1)S(1)} %collective-permute-done.1.refs_1_), channel_id=1, source_target_pairs={{0,4},{4,0},{8,12},{12,8},{16,20},{20,16},{24,28},{28,24},{1,5},{5... | collective-permute-start | bytes 221192 | tf_op jit(solution)/shard_map/ppermute | solution.py:331
  18.8 1.3 %collective-permute-start.8 = (bf16[9,32,128]{2,1,0:T(8,128)(2,1)S(1)}, bf16[9,32,128]{2,1,0:T(8,128)(2,1)S(1)}, u32[]{:S(2)}, u32[]{:S(2)}) collective-permute-start(bf16[9,32,128]{2,1,0:T(8,128)(2,1)S(1)} %collective-permute-done.2.refs_2_), channel_id=1, source_target_pairs={{0,4},{4,0},{8,12},{12,8},{16,20},{20,16},{24,28},{28,24},{1,5},{5... | collective-permute-start | bytes 221192 | tf_op jit(solution)/shard_map/ppermute | solution.py:331
  24.0 8.2 %copy-start = (bf16[1,256,2,1024]{3,2,1,0:T(2,128)(2,1)S(1)}, bf16[1,256,2,1024]{3,2,1,0:T(2,128)(2,1)}, u32[]{:S(2)}) copy-start(bf16[1,256,2,1024]{3,2,1,0:T(2,128)(2,1)} %param.14) | copy-start | bytes 3145732
  24.1 8.2 %copy-start.1 = (bf16[1,4,1024]{2,1,0:T(4,128)(2,1)S(1)}, bf16[1,4,1024]{2,1,0:T(4,128)(2,1)}, u32[]{:S(2)}) copy-start(bf16[1,4,1024]{2,1,0:T(4,128)(2,1)} %param.16) | copy-start | bytes 24580
  24.1 8.2 %copy-start.2 = (bf16[1,4,1024]{2,1,0:T(4,128)(2,1)S(1)}, bf16[1,4,1024]{2,1,0:T(4,128)(2,1)}, u32[]{:S(2)}) copy-start(bf16[1,4,1024]{2,1,0:T(4,128)(2,1)} %param.17) | copy-start | bytes 24580
  24.1 2.1 %collective-permute-start.10 = (f32[4,9,32,128]{3,2,1,0:T(8,128)S(1)}, f32[4,9,32,128]{3,2,1,0:T(8,128)S(1)}, u32[]{:S(2)}, u32[]{:S(2)}) collective-permute-start(f32[4,9,32,128]{3,2,1,0:T(8,128)S(1)} %context_states.3), channel_id=1, source_target_pairs={{0,4},{4,0},{8,12},{12,8},{16,20},{20,16},{24,28},{28,24},{1,5},{5... | collective-permute-start | bytes 1769480 | tf_op jit(solution)/shard_map/ppermute | solution.py:334
  27.1 8.2 %collective-permute-start.11 = (s16[9,32,128]{2,1,0:T(8,128)(2,1)S(1)}, s16[9,32,128]{2,1,0:T(8,128)(2,1)S(1)}, u32[]{:S(2)}, u32[]{:S(2)}) collective-permute-start(s16[9,32,128]{2,1,0:T(8,128)(2,1)S(1)} %get-tuple-element.24.refs_0_), channel_id=1, source_target_pairs={{0,8},{4,12},{8,0},{12,4},{16,24},{20,28},{24,16},{28,20},{1,9},{5... | collective-permute-start | bytes 221192 | tf_op jit(solution)/shard_map/ppermute | solution.py:337
  27.2 9.0 %collective-permute-start.12 = (s16[9,32,128]{2,1,0:T(8,128)(2,1)S(1)}, s16[9,32,128]{2,1,0:T(8,128)(2,1)S(1)}, u32[]{:S(2)}, u32[]{:S(2)}) collective-permute-start(s16[9,32,128]{2,1,0:T(8,128)(2,1)S(1)} %get-tuple-element.25.refs_1_), channel_id=1, source_target_pairs={{0,16},{4,20},{8,24},{12,28},{16,0},{20,4},{24,8},{28,12},{1,17},{... | collective-permute-start | bytes 221192 | tf_op jit(solution)/shard_map/ppermute | solution.py:337
  29.9 6.3 %collective-permute-start.13 = (s16[9,32,128]{2,1,0:T(8,128)(2,1)S(1)}, s16[9,32,128]{2,1,0:T(8,128)(2,1)S(1)}, u32[]{:S(2)}, u32[]{:S(2)}) collective-permute-start(s16[9,32,128]{2,1,0:T(8,128)(2,1)S(1)} %get-tuple-element.26.refs_2_), channel_id=1, source_target_pairs={{0,24},{4,28},{8,16},{12,20},{16,8},{20,12},{24,0},{28,4},{1,25},{... | collective-permute-start | bytes 221192 | tf_op jit(solution)/shard_map/ppermute | solution.py:337

commit v4 on v3

v4 whole, which is shorter than its diff:
```python
import functools

import jax
import jax.numpy as jnp
from jax import lax
from jax.experimental import pallas as pl
from jax.experimental.pallas import tpu as pltpu
from jax.sharding import PartitionSpec as P

KEY_VALUE_HEADS = 8
HEAD_SIZE = 128
SCALE = HEAD_SIZE**-0.5
SCALE_TWO = SCALE * 1.4426950408889634
MIB = 1024 * 1024
FILLER = -1e30
CODE_TOP = 32000.0
REST_TOP = 65000.0

NT = (((1,), (1,)), ((), ()))


def head_lanes(h):
    return pl.ds(h * HEAD_SIZE, HEAD_SIZE)


def put_lane(slab, lane, column):
    at = lax.broadcasted_iota(jnp.int32, slab.shape, 1)
    return jnp.where(at == lane, column, slab)


def vmem_limit(members, slots=4):
    return (8 if members * slots <= 32 else 48) * MIB


def in_any(count):
    return [pl.BlockSpec(memory_space=pl.ANY)] * count


def in_hbm(count):
    return [pl.BlockSpec(memory_space=pltpu.HBM)] * count


def in_vmem(count):
    return [pl.BlockSpec(memory_space=pltpu.VMEM)] * count


def in_smem(count):
    return [pl.BlockSpec(memory_space=pltpu.SMEM)] * count


def tile_rows(paired):
    tiles = paired.reshape(paired.shape[0], 2, KEY_VALUE_HEADS, HEAD_SIZE)
    return tiles.transpose(0, 2, 1, 3).reshape(-1, HEAD_SIZE)


PER_ROW = 2 * KEY_VALUE_HEADS
EXTRA = 8


def split_rows(tiles, wide, first, count, key_ref, value_ref):
    start = first * PER_ROW
    wide[pl.ds(start, count * PER_ROW)] = tiles[pl.ds(start, count * PER_ROW)].astype(jnp.float32)
    for h in range(KEY_VALUE_HEADS):
        for k, ref in enumerate((key_ref, value_ref)):
            rows = wide[pl.ds(start + 2 * h + k, count, stride=PER_ROW), :]
            ref[pl.ds(first, count), head_lanes(h)] = rows.astype(ref.dtype)


def prepare_kernel(
    session, owner_hbm, query_hbm, tab_hbm, message_ref, block_ref, tiles, wide, owner, sems
):
    moves = [
        (tab_hbm, tiles),
        (owner_hbm, owner),
        (query_hbm, message_ref.at[0, pl.ds(0, query_hbm.shape[0])]),
    ]
    copies = [pltpu.make_async_copy(*move, sems.at[i]) for i, move in enumerate(moves)]
    for copy in copies:
        copy.start()
    copies[1].wait()
    slot = jnp.int32(0)
    for k in range(owner.shape[0]):
        slot = jnp.where(session[0] == k, owner[k], slot)
    filled = jnp.full((EXTRA, HEAD_SIZE), slot.astype(jnp.float32), jnp.float32)
    message_ref[0, pl.ds(query_hbm.shape[0], EXTRA)] = filled.astype(jnp.bfloat16)
    copies[0].wait()
    split_rows(tiles, wide, 0, block_ref.shape[1], block_ref.at[0], block_ref.at[1])
    copies[2].wait()


def stay(arrays):
    return [pltpu.with_memory_space_constraint(array, pltpu.HBM) for array in arrays]


def prepare(session_tab, tab_owner, query, tab):
    tiles = tile_rows(tab)
    return pl.pallas_call(
        prepare_kernel,
        in_specs=in_smem(1) + in_hbm(3),
        out_specs=in_vmem(2),
        out_shape=[
            jax.ShapeDtypeStruct((1, query.shape[0] + EXTRA, HEAD_SIZE), jnp.bfloat16),
            jax.ShapeDtypeStruct((2, tab.shape[0], tab.shape[2]), jnp.bfloat16),
        ],
        scratch_shapes=[
            pltpu.VMEM(tiles.shape, tiles.dtype),
            pltpu.VMEM(tiles.shape, jnp.float32),
            pltpu.SMEM(tab_owner.shape, tab_owner.dtype),
            pltpu.SemaphoreType.DMA((4,)),
        ],
        compiler_params=pltpu.CompilerParams(vmem_limit_bytes=6 * MIB),
        name="prepare",
    )(session_tab, *stay([tab_owner, query, tiles]))


def split_kernel(first, chunks, tiles_hbm, key_ref, value_ref, tiles, wide, sems):
    rows = key_ref.shape[0] // chunks
    piece = rows * PER_ROW
    copies = [
        pltpu.make_async_copy(
            tiles_hbm.at[pl.ds(first * PER_ROW + i * piece, piece)],
            tiles.at[pl.ds(i * piece, piece)],
            sems.at[i],
        )
        for i in range(chunks)
    ]
    for copy in copies:
        copy.start()
    for i, copy in enumerate(copies):
        copy.wait()
        split_rows(tiles, wide, i * rows, rows, key_ref, value_ref)


def split_pairs(tiles, first, rows, chunks=4):
    shape = jax.ShapeDtypeStruct((rows, KEY_VALUE_HEADS * HEAD_SIZE), tiles.dtype)
    scratch = (rows * PER_ROW, HEAD_SIZE)
    return pl.pallas_call(
        functools.partial(split_kernel, first, chunks),
        in_specs=in_hbm(1),
        out_specs=in_vmem(2),
        out_shape=[shape, shape],
        scratch_shapes=[
            pltpu.VMEM(scratch, tiles.dtype),
            pltpu.VMEM(scratch, jnp.float32),
            pltpu.SemaphoreType.DMA((chunks,)),
        ],
        compiler_params=pltpu.CompilerParams(vmem_limit_bytes=6 * MIB),
        name="split_pairs",
    )(*stay([tiles]))


def block_softmax(score_parts, value_parts):
    largest = functools.reduce(
        jnp.maximum, [jnp.max(s, axis=-1, keepdims=True) for s in score_parts]
    )
    product = 0.0
    for scores, values in zip(score_parts, value_parts):
        weights = jnp.exp2((scores - largest) * SCALE_TWO).astype(jnp.bfloat16)
        values = jnp.concatenate([values, jnp.ones_like(values)], axis=1)
        product += jnp.dot(weights, values, preferred_element_type=jnp.float32)
    summed, total = product[:, :HEAD_SIZE], product[:, HEAD_SIZE:]
    return summed / total, largest * SCALE + jnp.log(total)


def row_count(message):
    return (message.shape[-2] - EXTRA) // KEY_VALUE_HEADS


def rows_of(ref, h):
    rows = row_count(ref)
    return ref[pl.ds(h * rows, rows)]


def extra_of(ref):
    return ref[pl.ds(ref.shape[0] - EXTRA, EXTRA)]


def context_kernel(heads, sizes, pieces, shares, slots, column_slot_ref, *refs):
    query_refs = [r.at[i] for r in refs[:pieces] for i in range(r.shape[0])]
    refs = refs[pieces:]
    key_refs, value_refs, refs = refs[:shares], refs[shares : 2 * shares], refs[2 * shares :]
    tab_refs, out_refs, members = refs[:slots], refs[slots:], len(query_refs)
    places = [r.at[i] for r, size in zip(out_refs, sizes) for i in range(size)]
    rows = row_count(query_refs[0])
    owner = jnp.concatenate([extra_of(q)[:, 0:1] for q in query_refs for _ in range(rows // EXTRA)])
    mine = owner.astype(jnp.float32) == column_slot_ref[0:1, :]
    ends = jnp.zeros((members * rows, HEAD_SIZE), jnp.float32)
    for n, h in enumerate(heads):
        at = head_lanes(h)
        query = jnp.concatenate([rows_of(q, h) for q in query_refs], axis=0)
        tab_keys = jnp.concatenate([t[0, :, at] for t in tab_refs], axis=0)
        tab_values = jnp.concatenate([t[1, :, at] for t in tab_refs], axis=0)
        scores = [
            lax.dot_general(query, keys, NT, preferred_element_type=jnp.float32)
            for keys in [r[:, at] for r in key_refs] + [tab_keys]
        ]
        scores[-1] = jnp.where(mine, scores[-1], FILLER)
        mean, end = block_softmax(scores, [r[:, at] for r in value_refs] + [tab_values])
        for i, place in enumerate(places):
            place[n] = mean[i * rows : (i + 1) * rows]
        ends = put_lane(ends, h, end)
    for i, place in enumerate(places):
        place[len(heads)] = ends[i * rows : (i + 1) * rows]


def context_states(heads, sizes, pieces, keys, values, column_slot, tabs):
    members, rows = sum(sizes), row_count(pieces[0])
    key_count = sum(k.shape[0] for k in keys) + column_slot.shape[1]
    work = members * rows * len(heads) * key_count
    return pl.pallas_call(
        functools.partial(context_kernel, heads, sizes, len(pieces), len(keys), len(tabs)),
        in_specs=in_vmem(1 + len(pieces) + 2 * len(keys) + len(tabs)),
        out_specs=in_vmem(len(sizes)),
        out_shape=[
            jax.ShapeDtypeStruct((size, len(heads) + 1, rows, HEAD_SIZE), jnp.float32)
            for size in sizes
        ],
        compiler_params=pltpu.CompilerParams(vmem_limit_bytes=vmem_limit(members, len(tabs))),
        cost_estimate=pl.CostEstimate(
            flops=4 * work * HEAD_SIZE, transcendentals=work, bytes_accessed=1
        ),
        name="context_states",
    )(column_slot, *pieces, *keys, *values, *tabs)


def shares_of(ends):
    top = functools.reduce(jnp.maximum, ends)
    shares = [jnp.exp(end - top) for end in ends]
    total = functools.reduce(jnp.add, shares)
    return [share / total for share in shares], top + jnp.log(total)


def mixed(parts, shares, h):
    return functools.reduce(
        jnp.add, [part * share[:, h : h + 1] for part, share in zip(parts, shares)]
    )


def both_halves(i, low_ref, high_ref):
    halves = [r.at[i, h] for r in (low_ref, high_ref) for h in range(r.shape[1] - 1)]
    return halves, low_ref[i, low_ref.shape[1] - 1] + high_ref[i, high_ref.shape[1] - 1]


def home_kernel(
    steps, length_ref, query_ref, tiles, new_key_ref, new_value_ref, low_ref, high_ref, other_ref, *refs
):
    out_ref, wide, key_ref, value_ref = refs[-4:]
    rows, slots = row_count(query_ref), key_ref.shape[0]
    split_rows(tiles, wide, 0, slots, key_ref, value_ref)
    used = lax.broadcasted_iota(jnp.int32, (rows, slots), 1) < length_ref[0]
    step = lax.rem(lax.broadcasted_iota(jnp.int32, (rows, steps), 0), steps)
    seen = lax.broadcasted_iota(jnp.int32, (rows, steps), 1) <= step
    ends, means = jnp.zeros((rows, HEAD_SIZE), jnp.float32), []
    for h in range(KEY_VALUE_HEADS):
        at = head_lanes(h)
        query = rows_of(query_ref.at[0], h)
        cached = lax.dot_general(query, key_ref[:, at], NT, preferred_element_type=jnp.float32)
        fresh = lax.dot_general(query, new_key_ref[:, at], NT, preferred_element_type=jnp.float32)
        cached = jnp.where(used, cached, FILLER)
        fresh = jnp.where(seen, fresh, FILLER)
        mean, end = block_softmax([cached, fresh], [value_ref[:, at], new_value_ref[:, at]])
        means.append(mean)
        ends = put_lane(ends, h, end)
    own, own_end = both_halves(0, low_ref, high_ref)
    shares, end = shares_of([ends, own_end, other_ref[0, KEY_VALUE_HEADS]])
    for h, mean in enumerate(means):
        out_ref[h] = mixed([mean, own[h][...], other_ref[0, h]], shares, h)
    out_ref[KEY_VALUE_HEADS] = end


def home_state(query_message, cache, length, new_keys, new_values, low, high, other, after):
    rows, steps = row_count(query_message), new_keys.shape[0]
    work = rows * KEY_VALUE_HEADS * cache.shape[0]
    tiles = tile_rows(cache)
    return pl.pallas_call(
        functools.partial(home_kernel, steps),
        in_specs=in_smem(1) + in_vmem(7) + in_any(len(after)),
        out_shape=jax.ShapeDtypeStruct((KEY_VALUE_HEADS + 1, rows, HEAD_SIZE), jnp.float32),
        scratch_shapes=[
            pltpu.VMEM(tiles.shape, jnp.float32),
            pltpu.VMEM((cache.shape[0], cache.shape[2]), cache.dtype),
            pltpu.VMEM((cache.shape[0], cache.shape[2]), cache.dtype),
        ],
        compiler_params=pltpu.CompilerParams(vmem_limit_bytes=vmem_limit(low.shape[0])),
        cost_estimate=pl.CostEstimate(
            flops=4 * work * HEAD_SIZE, transcendentals=work, bytes_accessed=4 * cache.size
        ),
        name="home_state",
    )(length, query_message, tiles, new_keys, new_values, low, high, other, *after)


def pair_kernel(order, low_ref, high_ref, other_ref, *coded_refs):
    rows = other_ref.shape[2]
    for i, coded_ref in zip(order, coded_refs):
        own, own_end = both_halves(i, low_ref, high_ref)
        shares, end = shares_of([own_end, other_ref[i - 1, KEY_VALUE_HEADS]])
        means = [
            mixed([own[h][...], other_ref[i - 1, h]], shares, h) for h in range(KEY_VALUE_HEADS)
        ]
        reach = jnp.ones((rows, HEAD_SIZE), jnp.float32)
        for h, mean in enumerate(means):
            reach = put_lane(reach, h, jnp.max(jnp.abs(mean), axis=-1, keepdims=True))
        exponent = jnp.ceil(jnp.log2(jnp.maximum(reach, 1e-30)))
        factor = jnp.exp2(-exponent) * CODE_TOP
        for h, mean in enumerate(means):
            code = jnp.round(mean * factor[:, h : h + 1])
            coded_ref[pl.ds(h * rows, rows)] = code.astype(jnp.int32).astype(jnp.int16)
        near = jnp.round(end)
        rest = jnp.round((end - near) * REST_TOP)
        at = lax.broadcasted_iota(jnp.int32, (EXTRA, HEAD_SIZE), 1) // KEY_VALUE_HEADS
        slab, kinds = jnp.zeros((EXTRA, HEAD_SIZE), jnp.float32), (near, rest, exponent)
        for r in range(rows // EXTRA):
            for k, kind in enumerate(kinds):
                place = r * len(kinds) + k
                part = kind[r * EXTRA : (r + 1) * EXTRA]
                moved = pltpu.roll(part, place * KEY_VALUE_HEADS, 1) if place else part
                slab = jnp.where(at == place, moved, slab)
        coded_ref[pl.ds(KEY_VALUE_HEADS * rows, EXTRA)] = slab.astype(jnp.int32).astype(jnp.int16)


def pair_states(order, low, high, other):
    rows = other.shape[2]
    shape = (KEY_VALUE_HEADS * rows + EXTRA, HEAD_SIZE)
    return pl.pallas_call(
        functools.partial(pair_kernel, order),
        out_shape=[jax.ShapeDtypeStruct(shape, jnp.int16)] * len(order),
        compiler_params=pltpu.CompilerParams(vmem_limit_bytes=vmem_limit(low.shape[0])),
        name="pair_states",
    )(low, high, other)


def final_kernel(home_ref, *refs):
    coded_refs, out_ref = refs[:-1], refs[-1]
    rows = home_ref.shape[1]
    ends, factors = [home_ref[KEY_VALUE_HEADS]], []
    head_lane = lax.broadcasted_iota(jnp.int32, ends[0].shape, 1) < KEY_VALUE_HEADS
    for r in coded_refs:
        slab = extra_of(r).astype(jnp.int32).astype(jnp.float32)
        near, rest, exponent = (
            jnp.concatenate(
                [
                    pltpu.roll(slab, (HEAD_SIZE - (3 * i + k) * KEY_VALUE_HEADS) % HEAD_SIZE, 1)
                    for i in range(rows // EXTRA)
                ]
            )
            for k in range(3)
        )
        ends.append(near + rest / REST_TOP)
        factors.append(jnp.exp2(jnp.where(head_lane, exponent, 0.0)) / CODE_TOP)
    shares, _ = shares_of([jnp.where(head_lane, end, 0.0) for end in ends])
    shares = shares[:1] + [share * factor for share, factor in zip(shares[1:], factors)]
    for h in range(KEY_VALUE_HEADS):
        parts = [rows_of(r, h).astype(jnp.int32).astype(jnp.float32) for r in coded_refs]
        out_ref[h] = mixed([home_ref[h]] + parts, shares, h).astype(jnp.bfloat16)


def final_output(home, coded):
    return pl.pallas_call(
        final_kernel,
        out_shape=jax.ShapeDtypeStruct((KEY_VALUE_HEADS,) + home.shape[1:], jnp.bfloat16),
        compiler_params=pltpu.CompilerParams(vmem_limit_bytes=vmem_limit(len(coded))),
        name="final_output",
    )(home, *coded)


def swap(count, bit):
    return [(i, i ^ bit) for i in range(count)]


def shards(
    queries,
    prefix_key_value,
    tab_key_value,
    tab_owner,
    session_tab,
    suffix_key_value,
    suffix_len,
    token_keys,
    token_values,
):
    ctx_count, tab_count = lax.axis_size("ctx"), lax.axis_size("tab")
    pair_count = ctx_count // 2
    steps = queries.shape[1]
    tab_rows = tab_key_value.shape[1]

    query = queries[0].reshape(steps, KEY_VALUE_HEADS, -1, HEAD_SIZE)
    query = query.transpose(1, 2, 0, 3).reshape(-1, HEAD_SIZE)
    message, tab_block = prepare(session_tab, tab_owner, query, tab_key_value[0])
    tabs = [tab_block] + [
        lax.ppermute(tab_block, "tab", swap(tab_count, k)) for k in range(1, tab_count)
    ]
    places = jnp.arange(tab_count * tab_rows, dtype=jnp.int32) // tab_rows
    column_slot = (places ^ lax.axis_index("tab")).astype(jnp.float32)[None]

    tiles = tile_rows(prefix_key_value)
    half = prefix_key_value.shape[0] // 2
    splits = [split_pairs(tiles, i * half, half) for i in range(2)]
    pieces, masks, bit = [message], [0], pair_count // 2
    while bit:
        if len(masks) == 2:
            pieces[-1], splits[0] = lax.optimization_barrier((pieces[-1], splits[0]))
        column = jnp.concatenate(pieces, axis=0) if len(pieces) > 1 else message
        pieces = [column, lax.ppermute(column, "ctx", swap(ctx_count, 2 * bit))]
        masks, bit = masks + [mask ^ bit for mask in masks], bit // 2
    pieces[-1], tabs, splits = lax.optimization_barrier((pieces[-1], tabs, splits))
    other_pieces = [lax.ppermute(piece, "ctx", swap(ctx_count, 1)) for piece in pieces]
    keys, values = zip(*splits)
    shared = (keys, values, column_slot, tabs)
    heads = tuple(range(KEY_VALUE_HEADS))
    first, second = heads[: len(heads) // 2], heads[len(heads) // 2 :]
    (low,) = context_states(first, (pair_count,), pieces, *shared)
    other_pieces, low = lax.optimization_barrier((other_pieces, low))
    near, far = context_states(heads, (1, pair_count - 1), other_pieces, *shared)
    pieces, far = lax.optimization_barrier((pieces, far))
    far = lax.ppermute(far, "ctx", swap(ctx_count, 1))
    near = lax.ppermute(near, "ctx", swap(ctx_count, 1))
    (high,) = context_states(second, (pair_count,), pieces, *shared)
    order = sorted(range(1, pair_count), key=lambda i: masks[i])
    coded = pair_states(order, low, high, far)
    received = [
        lax.ppermute(code, "ctx", swap(ctx_count, 2 * masks[i])) for i, code in zip(order, coded)
    ]
    home = home_state(
        message,
        suffix_key_value[0],
        suffix_len,
        token_keys[0],
        token_values[0],
        low,
        high,
        near,
        after=coded,
    )
    result = final_output(home, received)
    result = result.reshape(KEY_VALUE_HEADS, -1, steps, HEAD_SIZE)
    return result.transpose(2, 0, 1, 3).reshape(queries.shape)


def solution(mesh):
    sessions = ("ctx", "tab")
    placed = (
        P(sessions, None, None),
        P("ctx", None, None),
        P("tab", "ctx", None, None),
        P(),
        P(sessions),
        P(sessions, None, None, None),
        P(sessions),
        P(sessions, None, None),
        P(sessions, None, None),
    )
    return jax.shard_map(
        shards, mesh=mesh, in_specs=placed, out_specs=P(sessions, None, None), check_vma=False
    )
```

time: 37.4 us -> 36.4 us (0.973)
  Pallas kernels: 16 us -> 13 us
  waiting for transfers between devices: 4.91 us -> 7.1 us
    ppermute x11 -> x9, waiting for transfers between devices: 3.25 us -> 5.97 us  [the longest x3 3.18 us: shards(): lax.ppermute(code, 'ctx', swap(ctx_count, 2 * masks[i]))]
    pallas_call x5 -> x7, Pallas kernels: 13.4 us -> 10.9 us  [the longest x3 4.13 us: context_states(): pl.pallas_call(functools.partial(context_kernel, heads, sizes, len(pieces...]
    ppermute x11 -> x9, starting transfers between devices: 11.3 us -> 9.97 us  [the longest x2 4.87 us: shards(): pieces = [column, lax.ppermute(column, 'ctx', swap(ctx_count, 2 * bit))]]
    ppermute x3, starting transfers between devices: 3.49 us -> 4.6 us  [shards(): lax.ppermute(tab_block, 'tab', swap(tab_count, k))]
    ppermute x3, waiting for transfers between devices: 1.66 us -> 1.13 us  [shards(): lax.ppermute(tab_block, 'tab', swap(tab_count, k))]
    pallas_call x1, Pallas kernels: 1.57 us -> 1.2 us  [prepare(): pl.pallas_call(prepare_kernel, in_specs=in_smem(1) + in_hbm(3), out_specs...]
  transfers between devices with their start and end apart: 14 -> 12, of which waited for: 8 -> 8; matrix products, arithmetic and copies ran while one was open for 0% -> 0% of each run, Pallas kernels for 27% -> 23%
where the time goes in v4:
time: 36.4 us; the launch traced here: 36.2 us
  starting transfers between devices  14.6 us (40%)
  Pallas kernels  13 us (36%)
  waiting for transfers between devices  7.1 us (20%)
  between operations  1.43 us (4%)
    ppermute x2, starting transfers between devices, shards(): pieces = [column, lax.ppermute(column, 'ctx', swap(ctx_count, 2 * bit))]  4.87 us
    ppermute x3, starting transfers between devices, shards(): lax.ppermute(tab_block, 'tab', swap(tab_count, k))  4.6 us
    ppermute x3, starting transfers between devices, shards(): lax.ppermute(code, 'ctx', swap(ctx_count, 2 * masks[i]))  4.45 us
    pallas_call x3, Pallas kernels, context_states(): pl.pallas_call(functools.partial(context_kernel, heads, sizes, len(pieces...  4.13 us
    pallas_call x2, Pallas kernels, split_pairs(): pl.pallas_call(functools.partial(split_kernel, first, chunks), in_specs=i...  3.64 us
    ppermute x3, waiting for transfers between devices, shards(): lax.ppermute(code, 'ctx', swap(ctx_count, 2 * masks[i]))  3.18 us
    pallas_call x1, Pallas kernels, home_state(): pl.pallas_call(functools.partial(home_kernel, steps), in_specs=in_smem(1)...  2.09 us
    ppermute x2, waiting for transfers between devices, shards(): pieces = [column, lax.ppermute(column, 'ctx', swap(ctx_count, 2 * bit))]  1.82 us
  transfers between devices with their start and end apart: 12, of which 8 were waited for; matrix products, arithmetic and copies ran while one was open for 0% of the time, Pallas kernels for 23%

profile of v4, /device:TPU:0, one launch (start us, length us, event | category | flops | bytes accessed | tf_op | source)
XLA Modules:
  0.0 36.2 jit_solution(9791075664188062517)
XLA Ops:
  0.7 1.2 %prepare.1 = (bf16[1,264,128]{2,1,0:T(8,128)(2,1)S(1)}, bf16[2,64,1024]{2,1,0:T(8,128)(2,1)S(1)}) custom-call(s32[1]{0:T(128)S(6)} %copy.16.session, s32[4]{0:T(128)} %owner_hbm.1, bf16[256,128]{1,0:T(8,128)(2,1)} %bitcast.33, bf16[1024,128]{1,0:T(8,128)(2,1)} %bitcast.32), custom_call_target="tpu_custom_call" | custom-call | tf_op jit(solution)/shard_map/prepare/pallas_call | solution.py:97
  1.9 4.0 %collective-permute-start.5 = (bf16[2,64,1024]{2,1,0:T(8,128)(2,1)S(1)}, bf16[2,64,1024]{2,1,0:T(8,128)(2,1)S(1)}, u32[]{:S(2)}, u32[]{:S(2)}) collective-permute-start(bf16[2,64,1024]{2,1,0:T(8,128)(2,1)S(1)} %get-tuple-element.48.refs_6_), channel_id=1, source_target_pairs={{0,3},{1,2},{2,1},{3,0},{4,7},{5,6},{6,5},{7,4},{8,11},{9,10},{10,... | collective-permute-start | bytes 786440 | tf_op jit(solution)/shard_map/ppermute | solution.py:390
  5.8 0.5 %collective-permute-start.4 = (bf16[2,64,1024]{2,1,0:T(8,128)(2,1)S(1)}, bf16[2,64,1024]{2,1,0:T(8,128)(2,1)S(1)}, u32[]{:S(2)}, u32[]{:S(2)}) collective-permute-start(bf16[2,64,1024]{2,1,0:T(8,128)(2,1)S(1)} %get-tuple-element.48.refs_6_), channel_id=1, source_target_pairs={{0,2},{1,3},{2,0},{3,1},{4,6},{5,7},{6,4},{7,5},{8,10},{9,11},{10,... | collective-permute-start | bytes 786440 | tf_op jit(solution)/shard_map/ppermute | solution.py:390
  6.3 0.1 collective-permute-start.3
  6.5 3.0 %collective-permute-start = (bf16[1,264,128]{2,1,0:T(8,128)(2,1)S(1)}, bf16[1,264,128]{2,1,0:T(8,128)(2,1)S(1)}, u32[]{:S(2)}, u32[]{:S(2)}) collective-permute-start(bf16[1,264,128]{2,1,0:T(8,128)(2,1)S(1)} %get-tuple-element.34.query_ref), channel_id=1, source_target_pairs={{0,16},{4,20},{8,24},{12,28},{16,0},{20,4},{24,8},{28,12},{1,17},{... | collective-permute-start | bytes 202760 | tf_op jit(solution)/shard_map/ppermute | solution.py:403
  9.5 1.8 %split_pairs.2 = (bf16[256,1024]{1,0:T(8,128)(2,1)S(1)}, bf16[256,1024]{1,0:T(8,128)(2,1)S(1)}) custom-call(bf16[8192,128]{1,0:T(8,128)(2,1)} %bitcast.30), custom_call_target="tpu_custom_call" | custom-call | tf_op jit(solution)/shard_map/split_pairs/pallas_call | solution.py:137
  11.3 0.5 %collective-permute-done = bf16[1,264,128]{2,1,0:T(8,128)(2,1)S(1)} collective-permute-done((bf16[1,264,128]{2,1,0:T(8,128)(2,1)S(1)}, bf16[1,264,128]{2,1,0:T(8,128)(2,1)S(1)}, u32[]{:S(2)}, u32[]{:S(2)}) %collective-permute-start) | collective-permute-done | bytes 67616 | tf_op jit(solution)/shard_map/ppermute | solution.py:403
  11.8 1.9 %collective-permute-start.2 = (bf16[2,264,128]{2,1,0:T(8,128)(2,1)S(1)}, bf16[2,264,128]{2,1,0:T(8,128)(2,1)S(1)}, u32[]{:S(2)}, u32[]{:S(2)}) collective-permute-start(bf16[2,264,128]{2,1,0:T(8,128)(2,1)S(1)} %constant_dynamic-update-slice_fusion.refs_0_), channel_id=1, source_target_pairs={{0,8},{4,12},{8,0},{12,4},{16,24},{20,28},{24,16},{28,20},{1,9},{5... | collective-permute-start | bytes 405512 | tf_op jit(solution)/shard_map/ppermute | solution.py:403
  13.7 1.8 %split_pairs.3 = (bf16[256,1024]{1,0:T(8,128)(2,1)S(1)}, bf16[256,1024]{1,0:T(8,128)(2,1)S(1)}) custom-call(bf16[8192,128]{1,0:T(8,128)(2,1)} %bitcast.31), custom_call_target="tpu_custom_call" | custom-call | tf_op jit(solution)/shard_map/split_pairs/pallas_call | solution.py:137
  15.5 0.1 collective-permute-start.1
  15.6 1.3 %collective-permute-done.2.refs_1_ = bf16[2,264,128]{2,1,0:T(8,128)(2,1)S(1)} collective-permute-done((bf16[2,264,128]{2,1,0:T(8,128)(2,1)S(1)}, bf16[2,264,128]{2,1,0:T(8,128)(2,1)S(1)}, u32[]{:S(2)}, u32[]{:S(2)}) %collective-permute-start.2) | collective-permute-done | bytes 135200 | tf_op jit(solution)/shard_map/ppermute | solution.py:403
  16.9 0.0 collective-permute-done.5.refs_9_
  16.9 0.8 %collective-permute-done.4.refs_8_ = bf16[2,64,1024]{2,1,0:T(8,128)(2,1)S(1)} collective-permute-done((bf16[2,64,1024]{2,1,0:T(8,128)(2,1)S(1)}, bf16[2,64,1024]{2,1,0:T(8,128)(2,1)S(1)}, u32[]{:S(2)}, u32[]{:S(2)}) %collective-permute-start.4) | collective-permute-done | bytes 262176 | tf_op jit(solution)/shard_map/ppermute | solution.py:390
  17.7 0.3 collective-permute-done.3.refs_7_
  18.0 0.9 %context_states.3.low_ref = f32[4,5,32,128]{3,2,1,0:T(8,128)S(1)} custom-call(f32[1,256]{1,0:T(1,128)S(1)} %fusion.1.column_slot_ref, bf16[2,264,128]{2,1,0:T(8,128)(2,1)S(1)} %constant_dynamic-update-slice_fusion.refs_0_, bf16[2,264,128]{2,1,0:T(8,128)(2,1)S(1)} %collective-permute-done.2.refs_1_, bf16[256,1024]{1,0:T(8,128)(2,1)S(1)} %get-tuple-element.44.refs_2_, ...), custom_call_target="tpu_custom_call" | custom-call | flops 201326592 | bytes 1 | tf_op jit(solution)/shard_map/context_states/pallas_call | solution.py:210
  18.9 0.0 collective-permute-done.1.refs_0_
  18.9 0.6 %collective-permute-done.6.refs_1_ = bf16[2,264,128]{2,1,0:T(8,128)(2,1)} collective-permute-done((bf16[2,264,128]{2,1,0:T(8,128)(2,1)S(1)}, bf16[2,264,128]{2,1,0:T(8,128)(2,1)}, u32[]{:S(2)}, u32[]{:S(2)}) %collective-permute-start.6) | collective-permute-done | bytes 135200 | tf_op jit(solution)/shard_map/ppermute | solution.py:406
  19.5 2.4 %context_states.4 = (f32[1,9,32,128]{3,2,1,0:T(8,128)S(1)}, f32[3,9,32,128]{3,2,1,0:T(8,128)S(1)}) custom-call(f32[1,256]{1,0:T(1,128)S(1)} %fusion.1.column_slot_ref, bf16[2,264,128]{2,1,0:T(8,128)(2,1)} %collective-permute-done.1.refs_0_, bf16[2,264,128]{2,1,0:T(8,128)(2,1)} %collective-permute-done.6.refs_1_, ...), custom_call_target="tpu_custom_call" | custom-call | flops 402653184 | bytes 1 | tf_op jit(solution)/shard_map/context_states/pallas_call | solution.py:210
  21.9 0.2 collective-permute-start.8
  22.1 0.4 %collective-permute-start.7 = (f32[1,9,32,128]{3,2,1,0:T(8,128)S(1)}, f32[1,9,32,128]{3,2,1,0:T(8,128)S(1)}, u32[]{:S(2)}, u32[]{:S(2)}) collective-permute-start(f32[1,9,32,128]{3,2,1,0:T(8,128)S(1)} %get-tuple-element.58), channel_id=1, source_target_pairs={{0,4},{4,0},{8,12},{12,8},{16,20},{20,16},{24,28},{28,24},{1,5},{5... | collective-permute-start | bytes 442376 | tf_op jit(solution)/shard_map/ppermute | solution.py:416
  22.5 0.9 %context_states.5.high_ref = f32[4,5,32,128]{3,2,1,0:T(8,128)S(1)} custom-call(f32[1,256]{1,0:T(1,128)S(1)} %fusion.1.column_slot_ref, bf16[2,264,128]{2,1,0:T(8,128)(2,1)S(1)} %constant_dynamic-update-slice_fusion.refs_0_, bf16[2,264,128]{2,1,0:T(8,128)(2,1)S(1)} %collective-permute-done.2.refs_1_, bf16[256,1024]{1,0:T(8,128)(2,1)S(1)} %get-tuple-element.44.refs_2_, ...), custom_call_target="tpu_custom_call" | custom-call | flops 201326592 | bytes 1 | tf_op jit(solution)/shard_map/context_states/pallas_call | solution.py:210
  23.4 0.4 %collective-permute-done.8.other_ref = f32[3,9,32,128]{3,2,1,0:T(8,128)S(1)} collective-permute-done((f32[3,9,32,128]{3,2,1,0:T(8,128)S(1)}, f32[3,9,32,128]{3,2,1,0:T(8,128)S(1)}, u32[]{:S(2)}, u32[]{:S(2)}) %collective-permute-start.8) | collective-permute-done | bytes 442400 | tf_op jit(solution)/shard_map/ppermute | solution.py:415
  23.8 1.0 %pair_states.1 = (s16[264,128]{1,0:T(8,128)(2,1)S(1)}, s16[264,128]{1,0:T(8,128)(2,1)S(1)}, s16[264,128]{1,0:T(8,128)(2,1)S(1)}) custom-call(f32[4,5,32,128]{3,2,1,0:T(8,128)S(1)} %context_states.3.low_ref, f32[4,5,32,128]{3,2,1,0:T(8,128)S(1)} %context_states.5.high_ref, f32[3,9,32,128]{3,2,1,0:T(8,128)S(1)} %collective-permute-done.8.other_ref), custom_call_target="tpu_custom_call" | custom-call | tf_op jit(solution)/shard_map/pair_states/pallas_call | solution.py:324
  24.8 1.6 %collective-permute-start.9 = (s16[264,128]{1,0:T(8,128)(2,1)S(1)}, s16[264,128]{1,0:T(8,128)(2,1)S(1)}, u32[]{:S(2)}, u32[]{:S(2)}) collective-permute-start(s16[264,128]{1,0:T(8,128)(2,1)S(1)} %get-tuple-element.60.refs_0_), channel_id=1, source_target_pairs={{0,8},{4,12},{8,0},{12,4},{16,24},{20,28},{24,16},{28,20},{1,9},{5... | collective-permute-start | bytes 202760 | tf_op jit(solution)/shard_map/ppermute | solution.py:421
  26.4 2.6 %collective-permute-start.10 = (s16[264,128]{1,0:T(8,128)(2,1)S(1)}, s16[264,128]{1,0:T(8,128)(2,1)S(1)}, u32[]{:S(2)}, u32[]{:S(2)}) collective-permute-start(s16[264,128]{1,0:T(8,128)(2,1)S(1)} %get-tuple-element.61.refs_1_), channel_id=1, source_target_pairs={{0,16},{4,20},{8,24},{12,28},{16,0},{20,4},{24,8},{28,12},{1,17},{... | collective-permute-start | bytes 202760 | tf_op jit(solution)/shard_map/ppermute | solution.py:421
  29.0 0.2 collective-permute-start.11
  29.9 0.0 collective-permute-done.7.other_ref
  29.9 2.1 %home_state.1.home_ref = f32[9,32,128]{2,1,0:T(8,128)S(1)} custom-call(s32[1]{0:T(128)S(6)} %copy.17.length_ref, bf16[1,264,128]{2,1,0:T(8,128)(2,1)S(1)} %get-tuple-element.34.query_ref, bf16[4096,128]{1,0:T(8,128)(2,1)S(1)} %bitcast.27, bf16[4,1024]{1,0:T(4,128)(2,1)S(1)} %bitcast.28, bf16[4,1024]{1,0:T(4,128)(2,1)S(1)} %bitcast.29, ...), custom_call_target="tpu_custom_call" | custom-call | flops 33554432 | bytes 2097152 | tf_op jit(solution)/shard_map/home_state/pallas_call | solution.py:275
  32.0 0.0 collective-permute-done.9.refs_0_
  32.0 2.1 %collective-permute-done.10.refs_1_ = s16[264,128]{1,0:T(8,128)(2,1)S(1)} collective-permute-done((s16[264,128]{1,0:T(8,128)(2,1)S(1)}, s16[264,128]{1,0:T(8,128)(2,1)S(1)}, u32[]{:S(2)}, u32[]{:S(2)}) %collective-permute-start.10) | collective-permute-done | bytes 67616 | tf_op jit(solution)/shard_map/ppermute | solution.py:421
  34.1 1.1 %collective-permute-done.11.refs_2_ = s16[264,128]{1,0:T(8,128)(2,1)S(1)} collective-permute-done((s16[264,128]{1,0:T(8,128)(2,1)S(1)}, s16[264,128]{1,0:T(8,128)(2,1)S(1)}, u32[]{:S(2)}, u32[]{:S(2)}) %collective-permute-start.11) | collective-permute-done | bytes 67616 | tf_op jit(solution)/shard_map/ppermute | solution.py:421
  35.2 1.0 %final_output.1 = bf16[8,32,128]{2,1,0:T(8,128)(2,1)} custom-call(f32[9,32,128]{2,1,0:T(8,128)S(1)} %home_state.1.home_ref, s16[264,128]{1,0:T(8,128)(2,1)S(1)} %collective-permute-done.9.refs_0_, s16[264,128]{1,0:T(8,128)(2,1)S(1)} %collective-permute-done.10.refs_1_, s16[264,128]{1,0:T(8,128)(2,1)S(1)} %collective-permute-done.11.refs_2_), custom_call_target="tpu_custom_call" | custom-call | tf_op jit(solution)/shard_map/final_output/pallas_call | solution.py:358
  (10 shorter events, 0.0 us)
Async XLA Ops:
  1.9 15.0 %collective-permute-start.5 = (bf16[2,64,1024]{2,1,0:T(8,128)(2,1)S(1)}, bf16[2,64,1024]{2,1,0:T(8,128)(2,1)S(1)}, u32[]{:S(2)}, u32[]{:S(2)}) collective-permute-start(bf16[2,64,1024]{2,1,0:T(8,128)(2,1)S(1)} %get-tuple-element.48.refs_6_), channel_id=1, source_target_pairs={{0,3},{1,2},{2,1},{3,0},{4,7},{5,6},{6,5},{7,4},{8,11},{9,10},{10,... | collective-permute-start | bytes 786440 | tf_op jit(solution)/shard_map/ppermute | solution.py:390
  5.8 11.9 %collective-permute-start.4 = (bf16[2,64,1024]{2,1,0:T(8,128)(2,1)S(1)}, bf16[2,64,1024]{2,1,0:T(8,128)(2,1)S(1)}, u32[]{:S(2)}, u32[]{:S(2)}) collective-permute-start(bf16[2,64,1024]{2,1,0:T(8,128)(2,1)S(1)} %get-tuple-element.48.refs_6_), channel_id=1, source_target_pairs={{0,2},{1,3},{2,0},{3,1},{4,6},{5,7},{6,4},{7,5},{8,10},{9,11},{10,... | collective-permute-start | bytes 786440 | tf_op jit(solution)/shard_map/ppermute | solution.py:390
  6.3 11.7 %collective-permute-start.3 = (bf16[2,64,1024]{2,1,0:T(8,128)(2,1)S(1)}, bf16[2,64,1024]{2,1,0:T(8,128)(2,1)S(1)}, u32[]{:S(2)}, u32[]{:S(2)}) collective-permute-start(bf16[2,64,1024]{2,1,0:T(8,128)(2,1)S(1)} %get-tuple-element.48.refs_6_), channel_id=1, source_target_pairs={{0,1},{1,0},{2,3},{3,2},{4,5},{5,4},{6,7},{7,6},{8,9},{9,8},{10,11... | collective-permute-start | bytes 786440 | tf_op jit(solution)/shard_map/ppermute | solution.py:390
  6.5 5.3 %collective-permute-start = (bf16[1,264,128]{2,1,0:T(8,128)(2,1)S(1)}, bf16[1,264,128]{2,1,0:T(8,128)(2,1)S(1)}, u32[]{:S(2)}, u32[]{:S(2)}) collective-permute-start(bf16[1,264,128]{2,1,0:T(8,128)(2,1)S(1)} %get-tuple-element.34.query_ref), channel_id=1, source_target_pairs={{0,16},{4,20},{8,24},{12,28},{16,0},{20,4},{24,8},{28,12},{1,17},{... | collective-permute-start | bytes 202760 | tf_op jit(solution)/shard_map/ppermute | solution.py:403
  11.8 5.1 %collective-permute-start.2 = (bf16[2,264,128]{2,1,0:T(8,128)(2,1)S(1)}, bf16[2,264,128]{2,1,0:T(8,128)(2,1)S(1)}, u32[]{:S(2)}, u32[]{:S(2)}) collective-permute-start(bf16[2,264,128]{2,1,0:T(8,128)(2,1)S(1)} %constant_dynamic-update-slice_fusion.refs_0_), channel_id=1, source_target_pairs={{0,8},{4,12},{8,0},{12,4},{16,24},{20,28},{24,16},{28,20},{1,9},{5... | collective-permute-start | bytes 405512 | tf_op jit(solution)/shard_map/ppermute | solution.py:403
  15.5 3.4 %collective-permute-start.1 = (bf16[2,264,128]{2,1,0:T(8,128)(2,1)S(1)}, bf16[2,264,128]{2,1,0:T(8,128)(2,1)}, u32[]{:S(2)}, u32[]{:S(2)}) collective-permute-start(bf16[2,264,128]{2,1,0:T(8,128)(2,1)S(1)} %constant_dynamic-update-slice_fusion.refs_0_), channel_id=1, source_target_pairs={{0,4},{4,0},{8,12},{12,8},{16,20},{20,16},{24,28},{28,24},{1,5},{5... | collective-permute-start | bytes 405512 | tf_op jit(solution)/shard_map/ppermute | solution.py:406
  18.0 1.5 %collective-permute-start.6 = (bf16[2,264,128]{2,1,0:T(8,128)(2,1)S(1)}, bf16[2,264,128]{2,1,0:T(8,128)(2,1)}, u32[]{:S(2)}, u32[]{:S(2)}) collective-permute-start(bf16[2,264,128]{2,1,0:T(8,128)(2,1)S(1)} %collective-permute-done.2.refs_1_), channel_id=1, source_target_pairs={{0,4},{4,0},{8,12},{12,8},{16,20},{20,16},{24,28},{28,24},{1,5},{5... | collective-permute-start | bytes 405512 | tf_op jit(solution)/shard_map/ppermute | solution.py:406
  21.9 1.9 %collective-permute-start.8 = (f32[3,9,32,128]{3,2,1,0:T(8,128)S(1)}, f32[3,9,32,128]{3,2,1,0:T(8,128)S(1)}, u32[]{:S(2)}, u32[]{:S(2)}) collective-permute-start(f32[3,9,32,128]{3,2,1,0:T(8,128)S(1)} %get-tuple-element.59), channel_id=1, source_target_pairs={{0,4},{4,0},{8,12},{12,8},{16,20},{20,16},{24,28},{28,24},{1,5},{5... | collective-permute-start | bytes 1327112 | tf_op jit(solution)/shard_map/ppermute | solution.py:415
  22.1 7.8 %copy-start = (bf16[1,256,2,1024]{3,2,1,0:T(2,128)(2,1)S(1)}, bf16[1,256,2,1024]{3,2,1,0:T(2,128)(2,1)}, u32[]{:S(2)}) copy-start(bf16[1,256,2,1024]{3,2,1,0:T(2,128)(2,1)} %param.14) | copy-start | bytes 3145732
  22.1 7.8 %copy-start.1 = (bf16[1,4,1024]{2,1,0:T(4,128)(2,1)S(1)}, bf16[1,4,1024]{2,1,0:T(4,128)(2,1)}, u32[]{:S(2)}) copy-start(bf16[1,4,1024]{2,1,0:T(4,128)(2,1)} %param.16) | copy-start | bytes 24580
  22.1 7.8 %copy-start.2 = (bf16[1,4,1024]{2,1,0:T(4,128)(2,1)S(1)}, bf16[1,4,1024]{2,1,0:T(4,128)(2,1)}, u32[]{:S(2)}) copy-start(bf16[1,4,1024]{2,1,0:T(4,128)(2,1)} %param.17) | copy-start | bytes 24580
  22.1 7.8 %collective-permute-start.7 = (f32[1,9,32,128]{3,2,1,0:T(8,128)S(1)}, f32[1,9,32,128]{3,2,1,0:T(8,128)S(1)}, u32[]{:S(2)}, u32[]{:S(2)}) collective-permute-start(f32[1,9,32,128]{3,2,1,0:T(8,128)S(1)} %get-tuple-element.58), channel_id=1, source_target_pairs={{0,4},{4,0},{8,12},{12,8},{16,20},{20,16},{24,28},{28,24},{1,5},{5... | collective-permute-start | bytes 442376 | tf_op jit(solution)/shard_map/ppermute | solution.py:416
  24.8 7.2 %collective-permute-start.9 = (s16[264,128]{1,0:T(8,128)(2,1)S(1)}, s16[264,128]{1,0:T(8,128)(2,1)S(1)}, u32[]{:S(2)}, u32[]{:S(2)}) collective-permute-start(s16[264,128]{1,0:T(8,128)(2,1)S(1)} %get-tuple-element.60.refs_0_), channel_id=1, source_target_pairs={{0,8},{4,12},{8,0},{12,4},{16,24},{20,28},{24,16},{28,20},{1,9},{5... | collective-permute-start | bytes 202760 | tf_op jit(solution)/shard_map/ppermute | solution.py:421
  26.4 7.7 %collective-permute-start.10 = (s16[264,128]{1,0:T(8,128)(2,1)S(1)}, s16[264,128]{1,0:T(8,128)(2,1)S(1)}, u32[]{:S(2)}, u32[]{:S(2)}) collective-permute-start(s16[264,128]{1,0:T(8,128)(2,1)S(1)} %get-tuple-element.61.refs_1_), channel_id=1, source_target_pairs={{0,16},{4,20},{8,24},{12,28},{16,0},{20,4},{24,8},{28,12},{1,17},{... | collective-permute-start | bytes 202760 | tf_op jit(solution)/shard_map/ppermute | solution.py:421
  29.0 6.2 %collective-permute-start.11 = (s16[264,128]{1,0:T(8,128)(2,1)S(1)}, s16[264,128]{1,0:T(8,128)(2,1)S(1)}, u32[]{:S(2)}, u32[]{:S(2)}) collective-permute-start(s16[264,128]{1,0:T(8,128)(2,1)S(1)} %get-tuple-element.62.refs_2_), channel_id=1, source_target_pairs={{0,24},{4,28},{8,16},{12,20},{16,8},{20,12},{24,0},{28,4},{1,25},{... | collective-permute-start | bytes 202760 | tf_op jit(solution)/shard_map/ppermute | solution.py:421

commit v5 on v4

--- a/solution.py
+++ b/solution.py
@@ -407,7 +407,7 @@
     keys, values = zip(*splits)
     shared = (keys, values, column_slot, tabs)
     heads = tuple(range(KEY_VALUE_HEADS))
-    first, second = heads[: len(heads) // 2], heads[len(heads) // 2 :]
+    first, second = heads[:5], heads[5:]
     (low,) = context_states(first, (pair_count,), pieces, *shared)
     other_pieces, low = lax.optimization_barrier((other_pieces, low))
     near, far = context_states(heads, (1, pair_count - 1), other_pieces, *shared)

time: 36.4 us -> 35.3 us (0.970)
  Pallas kernels: 13 us -> 12.1 us
    pallas_call x3, Pallas kernels: 4.13 us -> 3.2 us  [context_states(): pl.pallas_call(functools.partial(context_kernel, heads, sizes, len(pieces...]
  transfers between devices with their start and end apart: 12 -> 12, of which waited for: 8 -> 8; matrix products, arithmetic and copies ran while one was open for 0% -> 0% of each run, Pallas kernels for 23% -> 24%
where the time goes in v5:
time: 35.3 us; the launch traced here: 35.1 us
  starting transfers between devices  14.6 us (41%)
  Pallas kernels  12.1 us (34%)
  waiting for transfers between devices  6.95 us (20%)
  between operations  1.43 us (4%)
    ppermute x2, starting transfers between devices, shards(): pieces = [column, lax.ppermute(column, 'ctx', swap(ctx_count, 2 * bit))]  4.87 us
    ppermute x3, starting transfers between devices, shards(): lax.ppermute(tab_block, 'tab', swap(tab_count, k))  4.6 us
    ppermute x3, starting transfers between devices, shards(): lax.ppermute(code, 'ctx', swap(ctx_count, 2 * masks[i]))  4.45 us
    pallas_call x2, Pallas kernels, split_pairs(): pl.pallas_call(functools.partial(split_kernel, first, chunks), in_specs=i...  3.64 us
    pallas_call x3, Pallas kernels, context_states(): pl.pallas_call(functools.partial(context_kernel, heads, sizes, len(pieces...  3.2 us
    ppermute x3, waiting for transfers between devices, shards(): lax.ppermute(code, 'ctx', swap(ctx_count, 2 * masks[i]))  3.17 us
    pallas_call x1, Pallas kernels, home_state(): pl.pallas_call(functools.partial(home_kernel, steps), in_specs=in_smem(1)...  2.09 us
    ppermute x2, waiting for transfers between devices, shards(): pieces = [column, lax.ppermute(column, 'ctx', swap(ctx_count, 2 * bit))]  1.81 us
  transfers between devices with their start and end apart: 12, of which 8 were waited for; matrix products, arithmetic and copies ran while one was open for 0% of the time, Pallas kernels for 24%

profile of v5, /device:TPU:0, one launch (start us, length us, event | category | flops | bytes accessed | tf_op | source)
XLA Modules:
  0.0 35.1 jit_solution(16738576999933935640)
XLA Ops:
  0.7 1.2 %prepare.1 = (bf16[1,264,128]{2,1,0:T(8,128)(2,1)S(1)}, bf16[2,64,1024]{2,1,0:T(8,128)(2,1)S(1)}) custom-call(s32[1]{0:T(128)S(6)} %copy.16.session, s32[4]{0:T(128)} %owner_hbm.1, bf16[256,128]{1,0:T(8,128)(2,1)} %bitcast.33, bf16[1024,128]{1,0:T(8,128)(2,1)} %bitcast.32), custom_call_target="tpu_custom_call" | custom-call | tf_op jit(solution)/shard_map/prepare/pallas_call | solution.py:97
  1.9 4.0 %collective-permute-start.5 = (bf16[2,64,1024]{2,1,0:T(8,128)(2,1)S(1)}, bf16[2,64,1024]{2,1,0:T(8,128)(2,1)S(1)}, u32[]{:S(2)}, u32[]{:S(2)}) collective-permute-start(bf16[2,64,1024]{2,1,0:T(8,128)(2,1)S(1)} %get-tuple-element.48.refs_6_), channel_id=1, source_target_pairs={{0,3},{1,2},{2,1},{3,0},{4,7},{5,6},{6,5},{7,4},{8,11},{9,10},{10,... | collective-permute-start | bytes 786440 | tf_op jit(solution)/shard_map/ppermute | solution.py:390
  5.8 0.5 %collective-permute-start.4 = (bf16[2,64,1024]{2,1,0:T(8,128)(2,1)S(1)}, bf16[2,64,1024]{2,1,0:T(8,128)(2,1)S(1)}, u32[]{:S(2)}, u32[]{:S(2)}) collective-permute-start(bf16[2,64,1024]{2,1,0:T(8,128)(2,1)S(1)} %get-tuple-element.48.refs_6_), channel_id=1, source_target_pairs={{0,2},{1,3},{2,0},{3,1},{4,6},{5,7},{6,4},{7,5},{8,10},{9,11},{10,... | collective-permute-start | bytes 786440 | tf_op jit(solution)/shard_map/ppermute | solution.py:390
  6.3 0.1 collective-permute-start.3
  6.5 3.0 %collective-permute-start = (bf16[1,264,128]{2,1,0:T(8,128)(2,1)S(1)}, bf16[1,264,128]{2,1,0:T(8,128)(2,1)S(1)}, u32[]{:S(2)}, u32[]{:S(2)}) collective-permute-start(bf16[1,264,128]{2,1,0:T(8,128)(2,1)S(1)} %get-tuple-element.34.query_ref), channel_id=1, source_target_pairs={{0,16},{4,20},{8,24},{12,28},{16,0},{20,4},{24,8},{28,12},{1,17},{... | collective-permute-start | bytes 202760 | tf_op jit(solution)/shard_map/ppermute | solution.py:403
  9.5 1.8 %split_pairs.2 = (bf16[256,1024]{1,0:T(8,128)(2,1)S(1)}, bf16[256,1024]{1,0:T(8,128)(2,1)S(1)}) custom-call(bf16[8192,128]{1,0:T(8,128)(2,1)} %bitcast.30), custom_call_target="tpu_custom_call" | custom-call | tf_op jit(solution)/shard_map/split_pairs/pallas_call | solution.py:137
  11.3 0.5 %collective-permute-done = bf16[1,264,128]{2,1,0:T(8,128)(2,1)S(1)} collective-permute-done((bf16[1,264,128]{2,1,0:T(8,128)(2,1)S(1)}, bf16[1,264,128]{2,1,0:T(8,128)(2,1)S(1)}, u32[]{:S(2)}, u32[]{:S(2)}) %collective-permute-start) | collective-permute-done | bytes 67616 | tf_op jit(solution)/shard_map/ppermute | solution.py:403
  11.8 1.9 %collective-permute-start.2 = (bf16[2,264,128]{2,1,0:T(8,128)(2,1)S(1)}, bf16[2,264,128]{2,1,0:T(8,128)(2,1)S(1)}, u32[]{:S(2)}, u32[]{:S(2)}) collective-permute-start(bf16[2,264,128]{2,1,0:T(8,128)(2,1)S(1)} %constant_dynamic-update-slice_fusion.refs_0_), channel_id=1, source_target_pairs={{0,8},{4,12},{8,0},{12,4},{16,24},{20,28},{24,16},{28,20},{1,9},{5... | collective-permute-start | bytes 405512 | tf_op jit(solution)/shard_map/ppermute | solution.py:403
  13.7 1.8 %split_pairs.3 = (bf16[256,1024]{1,0:T(8,128)(2,1)S(1)}, bf16[256,1024]{1,0:T(8,128)(2,1)S(1)}) custom-call(bf16[8192,128]{1,0:T(8,128)(2,1)} %bitcast.31), custom_call_target="tpu_custom_call" | custom-call | tf_op jit(solution)/shard_map/split_pairs/pallas_call | solution.py:137
  15.5 0.1 collective-permute-start.1
  15.6 1.3 %collective-permute-done.2.refs_1_ = bf16[2,264,128]{2,1,0:T(8,128)(2,1)S(1)} collective-permute-done((bf16[2,264,128]{2,1,0:T(8,128)(2,1)S(1)}, bf16[2,264,128]{2,1,0:T(8,128)(2,1)S(1)}, u32[]{:S(2)}, u32[]{:S(2)}) %collective-permute-start.2) | collective-permute-done | bytes 135200 | tf_op jit(solution)/shard_map/ppermute | solution.py:403
  16.9 0.0 collective-permute-done.5.refs_9_
  16.9 0.8 %collective-permute-done.4.refs_8_ = bf16[2,64,1024]{2,1,0:T(8,128)(2,1)S(1)} collective-permute-done((bf16[2,64,1024]{2,1,0:T(8,128)(2,1)S(1)}, bf16[2,64,1024]{2,1,0:T(8,128)(2,1)S(1)}, u32[]{:S(2)}, u32[]{:S(2)}) %collective-permute-start.4) | collective-permute-done | bytes 262176 | tf_op jit(solution)/shard_map/ppermute | solution.py:390
  17.7 0.3 collective-permute-done.3.refs_7_
  18.0 0.0 collective-permute-start.6
  18.0 1.0 %context_states.3.low_ref = f32[4,6,32,128]{3,2,1,0:T(8,128)S(1)} custom-call(f32[1,256]{1,0:T(1,128)S(1)} %fusion.1.column_slot_ref, bf16[2,264,128]{2,1,0:T(8,128)(2,1)S(1)} %constant_dynamic-update-slice_fusion.refs_0_, bf16[2,264,128]{2,1,0:T(8,128)(2,1)S(1)} %collective-permute-done.2.refs_1_, bf16[256,1024]{1,0:T(8,128)(2,1)S(1)} %get-tuple-element.44.refs_2_, ...), custom_call_target="tpu_custom_call" | custom-call | flops 251658240 | bytes 1 | tf_op jit(solution)/shard_map/context_states/pallas_call | solution.py:210
  19.1 0.0 collective-permute-done.1.refs_0_
  19.1 0.3 collective-permute-done.6.refs_1_
  19.4 1.4 %context_states.4 = (f32[1,9,32,128]{3,2,1,0:T(8,128)S(1)}, f32[3,9,32,128]{3,2,1,0:T(8,128)S(1)}) custom-call(f32[1,256]{1,0:T(1,128)S(1)} %fusion.1.column_slot_ref, bf16[2,264,128]{2,1,0:T(8,128)(2,1)S(1)} %collective-permute-done.1.refs_0_, bf16[2,264,128]{2,1,0:T(8,128)(2,1)S(1)} %collective-permute-done.6.refs_1_, ...), custom_call_target="tpu_custom_call" | custom-call | flops 402653184 | bytes 1 | tf_op jit(solution)/shard_map/context_states/pallas_call | solution.py:210
  20.8 0.3 collective-permute-start.8
  21.1 0.3 collective-permute-start.7
  21.4 0.7 %context_states.5.high_ref = f32[4,4,32,128]{3,2,1,0:T(8,128)S(1)} custom-call(f32[1,256]{1,0:T(1,128)S(1)} %fusion.1.column_slot_ref, bf16[2,264,128]{2,1,0:T(8,128)(2,1)S(1)} %constant_dynamic-update-slice_fusion.refs_0_, bf16[2,264,128]{2,1,0:T(8,128)(2,1)S(1)} %collective-permute-done.2.refs_1_, bf16[256,1024]{1,0:T(8,128)(2,1)S(1)} %get-tuple-element.44.refs_2_, ...), custom_call_target="tpu_custom_call" | custom-call | flops 150994944 | bytes 1 | tf_op jit(solution)/shard_map/context_states/pallas_call | solution.py:210
  22.2 0.5 %collective-permute-done.8.other_ref = f32[3,9,32,128]{3,2,1,0:T(8,128)S(1)} collective-permute-done((f32[3,9,32,128]{3,2,1,0:T(8,128)S(1)}, f32[3,9,32,128]{3,2,1,0:T(8,128)S(1)}, u32[]{:S(2)}, u32[]{:S(2)}) %collective-permute-start.8) | collective-permute-done | bytes 442400 | tf_op jit(solution)/shard_map/ppermute | solution.py:415
  22.7 1.0 %pair_states.1 = (s16[264,128]{1,0:T(8,128)(2,1)S(1)}, s16[264,128]{1,0:T(8,128)(2,1)S(1)}, s16[264,128]{1,0:T(8,128)(2,1)S(1)}) custom-call(f32[4,6,32,128]{3,2,1,0:T(8,128)S(1)} %context_states.3.low_ref, f32[4,4,32,128]{3,2,1,0:T(8,128)S(1)} %context_states.5.high_ref, f32[3,9,32,128]{3,2,1,0:T(8,128)S(1)} %collective-permute-done.8.other_ref), custom_call_target="tpu_custom_call" | custom-call | tf_op jit(solution)/shard_map/pair_states/pallas_call | solution.py:324
  23.7 1.6 %collective-permute-start.9 = (s16[264,128]{1,0:T(8,128)(2,1)S(1)}, s16[264,128]{1,0:T(8,128)(2,1)S(1)}, u32[]{:S(2)}, u32[]{:S(2)}) collective-permute-start(s16[264,128]{1,0:T(8,128)(2,1)S(1)} %get-tuple-element.60.refs_0_), channel_id=1, source_target_pairs={{0,8},{4,12},{8,0},{12,4},{16,24},{20,28},{24,16},{28,20},{1,9},{5... | collective-permute-start | bytes 202760 | tf_op jit(solution)/shard_map/ppermute | solution.py:421
  25.3 2.6 %collective-permute-start.10 = (s16[264,128]{1,0:T(8,128)(2,1)S(1)}, s16[264,128]{1,0:T(8,128)(2,1)S(1)}, u32[]{:S(2)}, u32[]{:S(2)}) collective-permute-start(s16[264,128]{1,0:T(8,128)(2,1)S(1)} %get-tuple-element.61.refs_1_), channel_id=1, source_target_pairs={{0,16},{4,20},{8,24},{12,28},{16,0},{20,4},{24,8},{28,12},{1,17},{... | collective-permute-start | bytes 202760 | tf_op jit(solution)/shard_map/ppermute | solution.py:421
  27.9 0.2 collective-permute-start.11
  28.8 0.0 collective-permute-done.7.other_ref
  28.8 2.1 %home_state.1.home_ref = f32[9,32,128]{2,1,0:T(8,128)S(1)} custom-call(s32[1]{0:T(128)S(6)} %copy.17.length_ref, bf16[1,264,128]{2,1,0:T(8,128)(2,1)S(1)} %get-tuple-element.34.query_ref, bf16[4096,128]{1,0:T(8,128)(2,1)S(1)} %bitcast.27, bf16[4,1024]{1,0:T(4,128)(2,1)S(1)} %bitcast.28, bf16[4,1024]{1,0:T(4,128)(2,1)S(1)} %bitcast.29, ...), custom_call_target="tpu_custom_call" | custom-call | flops 33554432 | bytes 2097152 | tf_op jit(solution)/shard_map/home_state/pallas_call | solution.py:275
  30.9 2.1 %collective-permute-done.10.refs_1_ = s16[264,128]{1,0:T(8,128)(2,1)S(1)} collective-permute-done((s16[264,128]{1,0:T(8,128)(2,1)S(1)}, s16[264,128]{1,0:T(8,128)(2,1)S(1)}, u32[]{:S(2)}, u32[]{:S(2)}) %collective-permute-start.10) | collective-permute-done | bytes 67616 | tf_op jit(solution)/shard_map/ppermute | solution.py:421
  33.0 1.1 %collective-permute-done.11.refs_2_ = s16[264,128]{1,0:T(8,128)(2,1)S(1)} collective-permute-done((s16[264,128]{1,0:T(8,128)(2,1)S(1)}, s16[264,128]{1,0:T(8,128)(2,1)S(1)}, u32[]{:S(2)}, u32[]{:S(2)}) %collective-permute-start.11) | collective-permute-done | bytes 67616 | tf_op jit(solution)/shard_map/ppermute | solution.py:421
  34.1 1.0 %final_output.1 = bf16[8,32,128]{2,1,0:T(8,128)(2,1)} custom-call(f32[9,32,128]{2,1,0:T(8,128)S(1)} %home_state.1.home_ref, s16[264,128]{1,0:T(8,128)(2,1)S(1)} %collective-permute-done.9.refs_0_, s16[264,128]{1,0:T(8,128)(2,1)S(1)} %collective-permute-done.10.refs_1_, s16[264,128]{1,0:T(8,128)(2,1)S(1)} %collective-permute-done.11.refs_2_), custom_call_target="tpu_custom_call" | custom-call | tf_op jit(solution)/shard_map/final_output/pallas_call | solution.py:358
  (10 shorter events, 0.0 us)
Async XLA Ops:
  1.9 15.0 %collective-permute-start.5 = (bf16[2,64,1024]{2,1,0:T(8,128)(2,1)S(1)}, bf16[2,64,1024]{2,1,0:T(8,128)(2,1)S(1)}, u32[]{:S(2)}, u32[]{:S(2)}) collective-permute-start(bf16[2,64,1024]{2,1,0:T(8,128)(2,1)S(1)} %get-tuple-element.48.refs_6_), channel_id=1, source_target_pairs={{0,3},{1,2},{2,1},{3,0},{4,7},{5,6},{6,5},{7,4},{8,11},{9,10},{10,... | collective-permute-start | bytes 786440 | tf_op jit(solution)/shard_map/ppermute | solution.py:390
  5.8 11.9 %collective-permute-start.4 = (bf16[2,64,1024]{2,1,0:T(8,128)(2,1)S(1)}, bf16[2,64,1024]{2,1,0:T(8,128)(2,1)S(1)}, u32[]{:S(2)}, u32[]{:S(2)}) collective-permute-start(bf16[2,64,1024]{2,1,0:T(8,128)(2,1)S(1)} %get-tuple-element.48.refs_6_), channel_id=1, source_target_pairs={{0,2},{1,3},{2,0},{3,1},{4,6},{5,7},{6,4},{7,5},{8,10},{9,11},{10,... | collective-permute-start | bytes 786440 | tf_op jit(solution)/shard_map/ppermute | solution.py:390
  6.3 11.7 %collective-permute-start.3 = (bf16[2,64,1024]{2,1,0:T(8,128)(2,1)S(1)}, bf16[2,64,1024]{2,1,0:T(8,128)(2,1)S(1)}, u32[]{:S(2)}, u32[]{:S(2)}) collective-permute-start(bf16[2,64,1024]{2,1,0:T(8,128)(2,1)S(1)} %get-tuple-element.48.refs_6_), channel_id=1, source_target_pairs={{0,1},{1,0},{2,3},{3,2},{4,5},{5,4},{6,7},{7,6},{8,9},{9,8},{10,11... | collective-permute-start | bytes 786440 | tf_op jit(solution)/shard_map/ppermute | solution.py:390
  6.5 5.3 %collective-permute-start = (bf16[1,264,128]{2,1,0:T(8,128)(2,1)S(1)}, bf16[1,264,128]{2,1,0:T(8,128)(2,1)S(1)}, u32[]{:S(2)}, u32[]{:S(2)}) collective-permute-start(bf16[1,264,128]{2,1,0:T(8,128)(2,1)S(1)} %get-tuple-element.34.query_ref), channel_id=1, source_target_pairs={{0,16},{4,20},{8,24},{12,28},{16,0},{20,4},{24,8},{28,12},{1,17},{... | collective-permute-start | bytes 202760 | tf_op jit(solution)/shard_map/ppermute | solution.py:403
  11.8 5.1 %collective-permute-start.2 = (bf16[2,264,128]{2,1,0:T(8,128)(2,1)S(1)}, bf16[2,264,128]{2,1,0:T(8,128)(2,1)S(1)}, u32[]{:S(2)}, u32[]{:S(2)}) collective-permute-start(bf16[2,264,128]{2,1,0:T(8,128)(2,1)S(1)} %constant_dynamic-update-slice_fusion.refs_0_), channel_id=1, source_target_pairs={{0,8},{4,12},{8,0},{12,4},{16,24},{20,28},{24,16},{28,20},{1,9},{5... | collective-permute-start | bytes 405512 | tf_op jit(solution)/shard_map/ppermute | solution.py:403
  15.5 3.5 %collective-permute-start.1 = (bf16[2,264,128]{2,1,0:T(8,128)(2,1)S(1)}, bf16[2,264,128]{2,1,0:T(8,128)(2,1)S(1)}, u32[]{:S(2)}, u32[]{:S(2)}) collective-permute-start(bf16[2,264,128]{2,1,0:T(8,128)(2,1)S(1)} %constant_dynamic-update-slice_fusion.refs_0_), channel_id=1, source_target_pairs={{0,4},{4,0},{8,12},{12,8},{16,20},{20,16},{24,28},{28,24},{1,5},{5... | collective-permute-start | bytes 405512 | tf_op jit(solution)/shard_map/ppermute | solution.py:406
  18.0 1.4 %collective-permute-start.6 = (bf16[2,264,128]{2,1,0:T(8,128)(2,1)S(1)}, bf16[2,264,128]{2,1,0:T(8,128)(2,1)S(1)}, u32[]{:S(2)}, u32[]{:S(2)}) collective-permute-start(bf16[2,264,128]{2,1,0:T(8,128)(2,1)S(1)} %collective-permute-done.2.refs_1_), channel_id=1, source_target_pairs={{0,4},{4,0},{8,12},{12,8},{16,20},{20,16},{24,28},{28,24},{1,5},{5... | collective-permute-start | bytes 405512 | tf_op jit(solution)/shard_map/ppermute | solution.py:406
  20.8 1.9 %collective-permute-start.8 = (f32[3,9,32,128]{3,2,1,0:T(8,128)S(1)}, f32[3,9,32,128]{3,2,1,0:T(8,128)S(1)}, u32[]{:S(2)}, u32[]{:S(2)}) collective-permute-start(f32[3,9,32,128]{3,2,1,0:T(8,128)S(1)} %get-tuple-element.59), channel_id=1, source_target_pairs={{0,4},{4,0},{8,12},{12,8},{16,20},{20,16},{24,28},{28,24},{1,5},{5... | collective-permute-start | bytes 1327112 | tf_op jit(solution)/shard_map/ppermute | solution.py:415
  21.1 7.7 %copy-start = (bf16[1,256,2,1024]{3,2,1,0:T(2,128)(2,1)S(1)}, bf16[1,256,2,1024]{3,2,1,0:T(2,128)(2,1)}, u32[]{:S(2)}) copy-start(bf16[1,256,2,1024]{3,2,1,0:T(2,128)(2,1)} %param.14) | copy-start | bytes 3145732
  21.1 7.7 %copy-start.1 = (bf16[1,4,1024]{2,1,0:T(4,128)(2,1)S(1)}, bf16[1,4,1024]{2,1,0:T(4,128)(2,1)}, u32[]{:S(2)}) copy-start(bf16[1,4,1024]{2,1,0:T(4,128)(2,1)} %param.16) | copy-start | bytes 24580
  21.1 7.7 %copy-start.2 = (bf16[1,4,1024]{2,1,0:T(4,128)(2,1)S(1)}, bf16[1,4,1024]{2,1,0:T(4,128)(2,1)}, u32[]{:S(2)}) copy-start(bf16[1,4,1024]{2,1,0:T(4,128)(2,1)} %param.17) | copy-start | bytes 24580
  21.1 7.7 %collective-permute-start.7 = (f32[1,9,32,128]{3,2,1,0:T(8,128)S(1)}, f32[1,9,32,128]{3,2,1,0:T(8,128)S(1)}, u32[]{:S(2)}, u32[]{:S(2)}) collective-permute-start(f32[1,9,32,128]{3,2,1,0:T(8,128)S(1)} %get-tuple-element.58), channel_id=1, source_target_pairs={{0,4},{4,0},{8,12},{12,8},{16,20},{20,16},{24,28},{28,24},{1,5},{5... | collective-permute-start | bytes 442376 | tf_op jit(solution)/shard_map/ppermute | solution.py:416
  23.7 7.2 %collective-permute-start.9 = (s16[264,128]{1,0:T(8,128)(2,1)S(1)}, s16[264,128]{1,0:T(8,128)(2,1)S(1)}, u32[]{:S(2)}, u32[]{:S(2)}) collective-permute-start(s16[264,128]{1,0:T(8,128)(2,1)S(1)} %get-tuple-element.60.refs_0_), channel_id=1, source_target_pairs={{0,8},{4,12},{8,0},{12,4},{16,24},{20,28},{24,16},{28,20},{1,9},{5... | collective-permute-start | bytes 202760 | tf_op jit(solution)/shard_map/ppermute | solution.py:421
  25.3 7.7 %collective-permute-start.10 = (s16[264,128]{1,0:T(8,128)(2,1)S(1)}, s16[264,128]{1,0:T(8,128)(2,1)S(1)}, u32[]{:S(2)}, u32[]{:S(2)}) collective-permute-start(s16[264,128]{1,0:T(8,128)(2,1)S(1)} %get-tuple-element.61.refs_1_), channel_id=1, source_target_pairs={{0,16},{4,20},{8,24},{12,28},{16,0},{20,4},{24,8},{28,12},{1,17},{... | collective-permute-start | bytes 202760 | tf_op jit(solution)/shard_map/ppermute | solution.py:421
  27.9 6.2 %collective-permute-start.11 = (s16[264,128]{1,0:T(8,128)(2,1)S(1)}, s16[264,128]{1,0:T(8,128)(2,1)S(1)}, u32[]{:S(2)}, u32[]{:S(2)}) collective-permute-start(s16[264,128]{1,0:T(8,128)(2,1)S(1)} %get-tuple-element.62.refs_2_), channel_id=1, source_target_pairs={{0,24},{4,28},{8,16},{12,20},{16,8},{20,12},{24,0},{28,4},{1,25},{... | collective-permute-start | bytes 202760 | tf_op jit(solution)/shard_map/ppermute | solution.py:421

commit v6 on v5

--- a/solution.py
+++ b/solution.py
@@ -415,7 +415,7 @@
     far = lax.ppermute(far, "ctx", swap(ctx_count, 1))
     near = lax.ppermute(near, "ctx", swap(ctx_count, 1))
     (high,) = context_states(second, (pair_count,), pieces, *shared)
-    order = sorted(range(1, pair_count), key=lambda i: masks[i])
+    order = sorted(range(1, pair_count), key=lambda i: (masks[i] < pair_count // 2, masks[i]))
     coded = pair_states(order, low, high, far)
     received = [
         lax.ppermute(code, "ctx", swap(ctx_count, 2 * masks[i])) for i, code in zip(order, coded)

time: 35.3 us -> 34.4 us (0.975)
  waiting for transfers between devices: 6.95 us -> 6.28 us
    ppermute x3, waiting for transfers between devices: 3.17 us -> 2.51 us  [shards(): lax.ppermute(code, 'ctx', swap(ctx_count, 2 * masks[i]))]
  transfers between devices with their start and end apart: 12 -> 12, of which waited for: 8 -> 8; matrix products, arithmetic and copies ran while one was open for 0% -> 0% of each run, Pallas kernels for 24% -> 25%
where the time goes in v6:
time: 34.4 us; the launch traced here: 34.2 us
  starting transfers between devices  14.4 us (42%)
  Pallas kernels  12.1 us (35%)
  waiting for transfers between devices  6.28 us (18%)
  between operations  1.43 us (4%)
    ppermute x2, starting transfers between devices, shards(): pieces = [column, lax.ppermute(column, 'ctx', swap(ctx_count, 2 * bit))]  4.87 us
    ppermute x3, starting transfers between devices, shards(): lax.ppermute(tab_block, 'tab', swap(tab_count, k))  4.6 us
    ppermute x3, starting transfers between devices, shards(): lax.ppermute(code, 'ctx', swap(ctx_count, 2 * masks[i]))  4.23 us
    pallas_call x2, Pallas kernels, split_pairs(): pl.pallas_call(functools.partial(split_kernel, first, chunks), in_specs=i...  3.64 us
    pallas_call x3, Pallas kernels, context_states(): pl.pallas_call(functools.partial(context_kernel, heads, sizes, len(pieces...  3.2 us
    ppermute x3, waiting for transfers between devices, shards(): lax.ppermute(code, 'ctx', swap(ctx_count, 2 * masks[i]))  2.51 us
    pallas_call x1, Pallas kernels, home_state(): pl.pallas_call(functools.partial(home_kernel, steps), in_specs=in_smem(1)...  2.09 us
    ppermute x2, waiting for transfers between devices, shards(): pieces = [column, lax.ppermute(column, 'ctx', swap(ctx_count, 2 * bit))]  1.81 us
  transfers between devices with their start and end apart: 12, of which 8 were waited for; matrix products, arithmetic and copies ran while one was open for 0% of the time, Pallas kernels for 25%

profile of v6, /device:TPU:0, one launch (start us, length us, event | category | flops | bytes accessed | tf_op | source)
XLA Modules:
  0.0 34.2 jit_solution(8643177517600662969)
XLA Ops:
  0.7 1.2 %prepare.1 = (bf16[1,264,128]{2,1,0:T(8,128)(2,1)S(1)}, bf16[2,64,1024]{2,1,0:T(8,128)(2,1)S(1)}) custom-call(s32[1]{0:T(128)S(6)} %copy.16.session, s32[4]{0:T(128)} %owner_hbm.1, bf16[256,128]{1,0:T(8,128)(2,1)} %bitcast.33, bf16[1024,128]{1,0:T(8,128)(2,1)} %bitcast.32), custom_call_target="tpu_custom_call" | custom-call | tf_op jit(solution)/shard_map/prepare/pallas_call | solution.py:97
  1.9 4.0 %collective-permute-start.5 = (bf16[2,64,1024]{2,1,0:T(8,128)(2,1)S(1)}, bf16[2,64,1024]{2,1,0:T(8,128)(2,1)S(1)}, u32[]{:S(2)}, u32[]{:S(2)}) collective-permute-start(bf16[2,64,1024]{2,1,0:T(8,128)(2,1)S(1)} %get-tuple-element.48.refs_6_), channel_id=1, source_target_pairs={{0,3},{1,2},{2,1},{3,0},{4,7},{5,6},{6,5},{7,4},{8,11},{9,10},{10,... | collective-permute-start | bytes 786440 | tf_op jit(solution)/shard_map/ppermute | solution.py:390
  5.8 0.5 %collective-permute-start.4 = (bf16[2,64,1024]{2,1,0:T(8,128)(2,1)S(1)}, bf16[2,64,1024]{2,1,0:T(8,128)(2,1)S(1)}, u32[]{:S(2)}, u32[]{:S(2)}) collective-permute-start(bf16[2,64,1024]{2,1,0:T(8,128)(2,1)S(1)} %get-tuple-element.48.refs_6_), channel_id=1, source_target_pairs={{0,2},{1,3},{2,0},{3,1},{4,6},{5,7},{6,4},{7,5},{8,10},{9,11},{10,... | collective-permute-start | bytes 786440 | tf_op jit(solution)/shard_map/ppermute | solution.py:390
  6.3 0.1 collective-permute-start.3
  6.5 3.0 %collective-permute-start = (bf16[1,264,128]{2,1,0:T(8,128)(2,1)S(1)}, bf16[1,264,128]{2,1,0:T(8,128)(2,1)S(1)}, u32[]{:S(2)}, u32[]{:S(2)}) collective-permute-start(bf16[1,264,128]{2,1,0:T(8,128)(2,1)S(1)} %get-tuple-element.34.query_ref), channel_id=1, source_target_pairs={{0,16},{4,20},{8,24},{12,28},{16,0},{20,4},{24,8},{28,12},{1,17},{... | collective-permute-start | bytes 202760 | tf_op jit(solution)/shard_map/ppermute | solution.py:403
  9.5 1.8 %split_pairs.2 = (bf16[256,1024]{1,0:T(8,128)(2,1)S(1)}, bf16[256,1024]{1,0:T(8,128)(2,1)S(1)}) custom-call(bf16[8192,128]{1,0:T(8,128)(2,1)} %bitcast.30), custom_call_target="tpu_custom_call" | custom-call | tf_op jit(solution)/shard_map/split_pairs/pallas_call | solution.py:137
  11.3 0.5 %collective-permute-done = bf16[1,264,128]{2,1,0:T(8,128)(2,1)S(1)} collective-permute-done((bf16[1,264,128]{2,1,0:T(8,128)(2,1)S(1)}, bf16[1,264,128]{2,1,0:T(8,128)(2,1)S(1)}, u32[]{:S(2)}, u32[]{:S(2)}) %collective-permute-start) | collective-permute-done | bytes 67616 | tf_op jit(solution)/shard_map/ppermute | solution.py:403
  11.8 1.9 %collective-permute-start.2 = (bf16[2,264,128]{2,1,0:T(8,128)(2,1)S(1)}, bf16[2,264,128]{2,1,0:T(8,128)(2,1)S(1)}, u32[]{:S(2)}, u32[]{:S(2)}) collective-permute-start(bf16[2,264,128]{2,1,0:T(8,128)(2,1)S(1)} %constant_dynamic-update-slice_fusion.refs_0_), channel_id=1, source_target_pairs={{0,8},{4,12},{8,0},{12,4},{16,24},{20,28},{24,16},{28,20},{1,9},{5... | collective-permute-start | bytes 405512 | tf_op jit(solution)/shard_map/ppermute | solution.py:403
  13.7 1.8 %split_pairs.3 = (bf16[256,1024]{1,0:T(8,128)(2,1)S(1)}, bf16[256,1024]{1,0:T(8,128)(2,1)S(1)}) custom-call(bf16[8192,128]{1,0:T(8,128)(2,1)} %bitcast.31), custom_call_target="tpu_custom_call" | custom-call | tf_op jit(solution)/shard_map/split_pairs/pallas_call | solution.py:137
  15.5 0.1 collective-permute-start.1
  15.6 1.3 %collective-permute-done.2.refs_1_ = bf16[2,264,128]{2,1,0:T(8,128)(2,1)S(1)} collective-permute-done((bf16[2,264,128]{2,1,0:T(8,128)(2,1)S(1)}, bf16[2,264,128]{2,1,0:T(8,128)(2,1)S(1)}, u32[]{:S(2)}, u32[]{:S(2)}) %collective-permute-start.2) | collective-permute-done | bytes 135200 | tf_op jit(solution)/shard_map/ppermute | solution.py:403
  16.9 0.0 collective-permute-done.5.refs_9_
  16.9 0.8 %collective-permute-done.4.refs_8_ = bf16[2,64,1024]{2,1,0:T(8,128)(2,1)S(1)} collective-permute-done((bf16[2,64,1024]{2,1,0:T(8,128)(2,1)S(1)}, bf16[2,64,1024]{2,1,0:T(8,128)(2,1)S(1)}, u32[]{:S(2)}, u32[]{:S(2)}) %collective-permute-start.4) | collective-permute-done | bytes 262176 | tf_op jit(solution)/shard_map/ppermute | solution.py:390
  17.7 0.3 collective-permute-done.3.refs_7_
  18.0 0.0 collective-permute-start.6
  18.0 1.0 %context_states.3.low_ref = f32[4,6,32,128]{3,2,1,0:T(8,128)S(1)} custom-call(f32[1,256]{1,0:T(1,128)S(1)} %fusion.1.column_slot_ref, bf16[2,264,128]{2,1,0:T(8,128)(2,1)S(1)} %constant_dynamic-update-slice_fusion.refs_0_, bf16[2,264,128]{2,1,0:T(8,128)(2,1)S(1)} %collective-permute-done.2.refs_1_, bf16[256,1024]{1,0:T(8,128)(2,1)S(1)} %get-tuple-element.44.refs_2_, ...), custom_call_target="tpu_custom_call" | custom-call | flops 251658240 | bytes 1 | tf_op jit(solution)/shard_map/context_states/pallas_call | solution.py:210
  19.1 0.0 collective-permute-done.1.refs_0_
  19.1 0.3 collective-permute-done.6.refs_1_
  19.4 1.4 %context_states.4 = (f32[1,9,32,128]{3,2,1,0:T(8,128)S(1)}, f32[3,9,32,128]{3,2,1,0:T(8,128)S(1)}) custom-call(f32[1,256]{1,0:T(1,128)S(1)} %fusion.1.column_slot_ref, bf16[2,264,128]{2,1,0:T(8,128)(2,1)S(1)} %collective-permute-done.1.refs_0_, bf16[2,264,128]{2,1,0:T(8,128)(2,1)S(1)} %collective-permute-done.6.refs_1_, ...), custom_call_target="tpu_custom_call" | custom-call | flops 402653184 | bytes 1 | tf_op jit(solution)/shard_map/context_states/pallas_call | solution.py:210
  20.8 0.3 collective-permute-start.8
  21.1 0.3 collective-permute-start.7
  21.4 0.7 %context_states.5.high_ref = f32[4,4,32,128]{3,2,1,0:T(8,128)S(1)} custom-call(f32[1,256]{1,0:T(1,128)S(1)} %fusion.1.column_slot_ref, bf16[2,264,128]{2,1,0:T(8,128)(2,1)S(1)} %constant_dynamic-update-slice_fusion.refs_0_, bf16[2,264,128]{2,1,0:T(8,128)(2,1)S(1)} %collective-permute-done.2.refs_1_, bf16[256,1024]{1,0:T(8,128)(2,1)S(1)} %get-tuple-element.44.refs_2_, ...), custom_call_target="tpu_custom_call" | custom-call | flops 150994944 | bytes 1 | tf_op jit(solution)/shard_map/context_states/pallas_call | solution.py:210
  22.2 0.5 %collective-permute-done.8.other_ref = f32[3,9,32,128]{3,2,1,0:T(8,128)S(1)} collective-permute-done((f32[3,9,32,128]{3,2,1,0:T(8,128)S(1)}, f32[3,9,32,128]{3,2,1,0:T(8,128)S(1)}, u32[]{:S(2)}, u32[]{:S(2)}) %collective-permute-start.8) | collective-permute-done | bytes 442400 | tf_op jit(solution)/shard_map/ppermute | solution.py:415
  22.7 1.0 %pair_states.1 = (s16[264,128]{1,0:T(8,128)(2,1)S(1)}, s16[264,128]{1,0:T(8,128)(2,1)S(1)}, s16[264,128]{1,0:T(8,128)(2,1)S(1)}) custom-call(f32[4,6,32,128]{3,2,1,0:T(8,128)S(1)} %context_states.3.low_ref, f32[4,4,32,128]{3,2,1,0:T(8,128)S(1)} %context_states.5.high_ref, f32[3,9,32,128]{3,2,1,0:T(8,128)S(1)} %collective-permute-done.8.other_ref), custom_call_target="tpu_custom_call" | custom-call | tf_op jit(solution)/shard_map/pair_states/pallas_call | solution.py:324
  23.7 2.7 %collective-permute-start.9 = (s16[264,128]{1,0:T(8,128)(2,1)S(1)}, s16[264,128]{1,0:T(8,128)(2,1)S(1)}, u32[]{:S(2)}, u32[]{:S(2)}) collective-permute-start(s16[264,128]{1,0:T(8,128)(2,1)S(1)} %get-tuple-element.60.refs_0_), channel_id=1, source_target_pairs={{0,16},{4,20},{8,24},{12,28},{16,0},{20,4},{24,8},{28,12},{1,17},{... | collective-permute-start | bytes 202760 | tf_op jit(solution)/shard_map/ppermute | solution.py:421
  26.3 1.3 %collective-permute-start.10 = (s16[264,128]{1,0:T(8,128)(2,1)S(1)}, s16[264,128]{1,0:T(8,128)(2,1)S(1)}, u32[]{:S(2)}, u32[]{:S(2)}) collective-permute-start(s16[264,128]{1,0:T(8,128)(2,1)S(1)} %get-tuple-element.61.refs_1_), channel_id=1, source_target_pairs={{0,24},{4,28},{8,16},{12,20},{16,8},{20,12},{24,0},{28,4},{1,25},{... | collective-permute-start | bytes 202760 | tf_op jit(solution)/shard_map/ppermute | solution.py:421
  27.7 0.2 collective-permute-start.11
  28.6 2.1 %home_state.1.home_ref = f32[9,32,128]{2,1,0:T(8,128)S(1)} custom-call(s32[1]{0:T(128)S(6)} %copy.17.length_ref, bf16[1,264,128]{2,1,0:T(8,128)(2,1)S(1)} %get-tuple-element.34.query_ref, bf16[4096,128]{1,0:T(8,128)(2,1)S(1)} %bitcast.27, bf16[4,1024]{1,0:T(4,128)(2,1)S(1)} %bitcast.28, bf16[4,1024]{1,0:T(4,128)(2,1)S(1)} %bitcast.29, ...), custom_call_target="tpu_custom_call" | custom-call | flops 33554432 | bytes 2097152 | tf_op jit(solution)/shard_map/home_state/pallas_call | solution.py:275
  30.7 0.0 collective-permute-done.9.refs_0_
  30.7 2.2 %collective-permute-done.10.refs_1_ = s16[264,128]{1,0:T(8,128)(2,1)S(1)} collective-permute-done((s16[264,128]{1,0:T(8,128)(2,1)S(1)}, s16[264,128]{1,0:T(8,128)(2,1)S(1)}, u32[]{:S(2)}, u32[]{:S(2)}) %collective-permute-start.10) | collective-permute-done | bytes 67616 | tf_op jit(solution)/shard_map/ppermute | solution.py:421
  32.9 0.4 %collective-permute-done.11.refs_2_ = s16[264,128]{1,0:T(8,128)(2,1)S(1)} collective-permute-done((s16[264,128]{1,0:T(8,128)(2,1)S(1)}, s16[264,128]{1,0:T(8,128)(2,1)S(1)}, u32[]{:S(2)}, u32[]{:S(2)}) %collective-permute-start.11) | collective-permute-done | bytes 67616 | tf_op jit(solution)/shard_map/ppermute | solution.py:421
  33.2 1.0 %final_output.1 = bf16[8,32,128]{2,1,0:T(8,128)(2,1)} custom-call(f32[9,32,128]{2,1,0:T(8,128)S(1)} %home_state.1.home_ref, s16[264,128]{1,0:T(8,128)(2,1)S(1)} %collective-permute-done.9.refs_0_, s16[264,128]{1,0:T(8,128)(2,1)S(1)} %collective-permute-done.10.refs_1_, s16[264,128]{1,0:T(8,128)(2,1)S(1)} %collective-permute-done.11.refs_2_), custom_call_target="tpu_custom_call" | custom-call | tf_op jit(solution)/shard_map/final_output/pallas_call | solution.py:358
  (10 shorter events, 0.0 us)
Async XLA Ops:
  1.9 15.0 %collective-permute-start.5 = (bf16[2,64,1024]{2,1,0:T(8,128)(2,1)S(1)}, bf16[2,64,1024]{2,1,0:T(8,128)(2,1)S(1)}, u32[]{:S(2)}, u32[]{:S(2)}) collective-permute-start(bf16[2,64,1024]{2,1,0:T(8,128)(2,1)S(1)} %get-tuple-element.48.refs_6_), channel_id=1, source_target_pairs={{0,3},{1,2},{2,1},{3,0},{4,7},{5,6},{6,5},{7,4},{8,11},{9,10},{10,... | collective-permute-start | bytes 786440 | tf_op jit(solution)/shard_map/ppermute | solution.py:390
  5.8 11.9 %collective-permute-start.4 = (bf16[2,64,1024]{2,1,0:T(8,128)(2,1)S(1)}, bf16[2,64,1024]{2,1,0:T(8,128)(2,1)S(1)}, u32[]{:S(2)}, u32[]{:S(2)}) collective-permute-start(bf16[2,64,1024]{2,1,0:T(8,128)(2,1)S(1)} %get-tuple-element.48.refs_6_), channel_id=1, source_target_pairs={{0,2},{1,3},{2,0},{3,1},{4,6},{5,7},{6,4},{7,5},{8,10},{9,11},{10,... | collective-permute-start | bytes 786440 | tf_op jit(solution)/shard_map/ppermute | solution.py:390
  6.3 11.7 %collective-permute-start.3 = (bf16[2,64,1024]{2,1,0:T(8,128)(2,1)S(1)}, bf16[2,64,1024]{2,1,0:T(8,128)(2,1)S(1)}, u32[]{:S(2)}, u32[]{:S(2)}) collective-permute-start(bf16[2,64,1024]{2,1,0:T(8,128)(2,1)S(1)} %get-tuple-element.48.refs_6_), channel_id=1, source_target_pairs={{0,1},{1,0},{2,3},{3,2},{4,5},{5,4},{6,7},{7,6},{8,9},{9,8},{10,11... | collective-permute-start | bytes 786440 | tf_op jit(solution)/shard_map/ppermute | solution.py:390
  6.5 5.3 %collective-permute-start = (bf16[1,264,128]{2,1,0:T(8,128)(2,1)S(1)}, bf16[1,264,128]{2,1,0:T(8,128)(2,1)S(1)}, u32[]{:S(2)}, u32[]{:S(2)}) collective-permute-start(bf16[1,264,128]{2,1,0:T(8,128)(2,1)S(1)} %get-tuple-element.34.query_ref), channel_id=1, source_target_pairs={{0,16},{4,20},{8,24},{12,28},{16,0},{20,4},{24,8},{28,12},{1,17},{... | collective-permute-start | bytes 202760 | tf_op jit(solution)/shard_map/ppermute | solution.py:403
  11.8 5.1 %collective-permute-start.2 = (bf16[2,264,128]{2,1,0:T(8,128)(2,1)S(1)}, bf16[2,264,128]{2,1,0:T(8,128)(2,1)S(1)}, u32[]{:S(2)}, u32[]{:S(2)}) collective-permute-start(bf16[2,264,128]{2,1,0:T(8,128)(2,1)S(1)} %constant_dynamic-update-slice_fusion.refs_0_), channel_id=1, source_target_pairs={{0,8},{4,12},{8,0},{12,4},{16,24},{20,28},{24,16},{28,20},{1,9},{5... | collective-permute-start | bytes 405512 | tf_op jit(solution)/shard_map/ppermute | solution.py:403
  15.5 3.5 %collective-permute-start.1 = (bf16[2,264,128]{2,1,0:T(8,128)(2,1)S(1)}, bf16[2,264,128]{2,1,0:T(8,128)(2,1)S(1)}, u32[]{:S(2)}, u32[]{:S(2)}) collective-permute-start(bf16[2,264,128]{2,1,0:T(8,128)(2,1)S(1)} %constant_dynamic-update-slice_fusion.refs_0_), channel_id=1, source_target_pairs={{0,4},{4,0},{8,12},{12,8},{16,20},{20,16},{24,28},{28,24},{1,5},{5... | collective-permute-start | bytes 405512 | tf_op jit(solution)/shard_map/ppermute | solution.py:406
  18.0 1.4 %collective-permute-start.6 = (bf16[2,264,128]{2,1,0:T(8,128)(2,1)S(1)}, bf16[2,264,128]{2,1,0:T(8,128)(2,1)S(1)}, u32[]{:S(2)}, u32[]{:S(2)}) collective-permute-start(bf16[2,264,128]{2,1,0:T(8,128)(2,1)S(1)} %collective-permute-done.2.refs_1_), channel_id=1, source_target_pairs={{0,4},{4,0},{8,12},{12,8},{16,20},{20,16},{24,28},{28,24},{1,5},{5... | collective-permute-start | bytes 405512 | tf_op jit(solution)/shard_map/ppermute | solution.py:406
  20.8 1.9 %collective-permute-start.8 = (f32[3,9,32,128]{3,2,1,0:T(8,128)S(1)}, f32[3,9,32,128]{3,2,1,0:T(8,128)S(1)}, u32[]{:S(2)}, u32[]{:S(2)}) collective-permute-start(f32[3,9,32,128]{3,2,1,0:T(8,128)S(1)} %get-tuple-element.59), channel_id=1, source_target_pairs={{0,4},{4,0},{8,12},{12,8},{16,20},{20,16},{24,28},{28,24},{1,5},{5... | collective-permute-start | bytes 1327112 | tf_op jit(solution)/shard_map/ppermute | solution.py:415
  21.1 7.5 %copy-start = (bf16[1,256,2,1024]{3,2,1,0:T(2,128)(2,1)S(1)}, bf16[1,256,2,1024]{3,2,1,0:T(2,128)(2,1)}, u32[]{:S(2)}) copy-start(bf16[1,256,2,1024]{3,2,1,0:T(2,128)(2,1)} %param.14) | copy-start | bytes 3145732
  21.1 7.5 %copy-start.1 = (bf16[1,4,1024]{2,1,0:T(4,128)(2,1)S(1)}, bf16[1,4,1024]{2,1,0:T(4,128)(2,1)}, u32[]{:S(2)}) copy-start(bf16[1,4,1024]{2,1,0:T(4,128)(2,1)} %param.16) | copy-start | bytes 24580
  21.1 7.5 %copy-start.2 = (bf16[1,4,1024]{2,1,0:T(4,128)(2,1)S(1)}, bf16[1,4,1024]{2,1,0:T(4,128)(2,1)}, u32[]{:S(2)}) copy-start(bf16[1,4,1024]{2,1,0:T(4,128)(2,1)} %param.17) | copy-start | bytes 24580
  21.1 7.5 %collective-permute-start.7 = (f32[1,9,32,128]{3,2,1,0:T(8,128)S(1)}, f32[1,9,32,128]{3,2,1,0:T(8,128)S(1)}, u32[]{:S(2)}, u32[]{:S(2)}) collective-permute-start(f32[1,9,32,128]{3,2,1,0:T(8,128)S(1)} %get-tuple-element.58), channel_id=1, source_target_pairs={{0,4},{4,0},{8,12},{12,8},{16,20},{20,16},{24,28},{28,24},{1,5},{5... | collective-permute-start | bytes 442376 | tf_op jit(solution)/shard_map/ppermute | solution.py:416
  23.7 7.0 %collective-permute-start.9 = (s16[264,128]{1,0:T(8,128)(2,1)S(1)}, s16[264,128]{1,0:T(8,128)(2,1)S(1)}, u32[]{:S(2)}, u32[]{:S(2)}) collective-permute-start(s16[264,128]{1,0:T(8,128)(2,1)S(1)} %get-tuple-element.60.refs_0_), channel_id=1, source_target_pairs={{0,16},{4,20},{8,24},{12,28},{16,0},{20,4},{24,8},{28,12},{1,17},{... | collective-permute-start | bytes 202760 | tf_op jit(solution)/shard_map/ppermute | solution.py:421
  26.3 6.5 %collective-permute-start.10 = (s16[264,128]{1,0:T(8,128)(2,1)S(1)}, s16[264,128]{1,0:T(8,128)(2,1)S(1)}, u32[]{:S(2)}, u32[]{:S(2)}) collective-permute-start(s16[264,128]{1,0:T(8,128)(2,1)S(1)} %get-tuple-element.61.refs_1_), channel_id=1, source_target_pairs={{0,24},{4,28},{8,16},{12,20},{16,8},{20,12},{24,0},{28,4},{1,25},{... | collective-permute-start | bytes 202760 | tf_op jit(solution)/shard_map/ppermute | solution.py:421
  27.7 5.5 %collective-permute-start.11 = (s16[264,128]{1,0:T(8,128)(2,1)S(1)}, s16[264,128]{1,0:T(8,128)(2,1)S(1)}, u32[]{:S(2)}, u32[]{:S(2)}) collective-permute-start(s16[264,128]{1,0:T(8,128)(2,1)S(1)} %get-tuple-element.62.refs_2_), channel_id=1, source_target_pairs={{0,8},{4,12},{8,0},{12,4},{16,24},{20,28},{24,16},{28,20},{1,9},{5... | collective-permute-start | bytes 202760 | tf_op jit(solution)/shard_map/ppermute | solution.py:421

commit v7 on v6

--- a/solution.py
+++ b/solution.py
@@ -175,12 +175,12 @@
     return ref[pl.ds(ref.shape[0] - EXTRA, EXTRA)]
 
 
-def context_kernel(heads, sizes, pieces, shares, slots, column_slot_ref, *refs):
+def context_kernel(heads, groups, pieces, shares, slots, column_slot_ref, *refs):
     query_refs = [r.at[i] for r in refs[:pieces] for i in range(r.shape[0])]
     refs = refs[pieces:]
     key_refs, value_refs, refs = refs[:shares], refs[shares : 2 * shares], refs[2 * shares :]
     tab_refs, out_refs, members = refs[:slots], refs[slots:], len(query_refs)
-    places = [r.at[i] for r, size in zip(out_refs, sizes) for i in range(size)]
+    places = [(i, r.at[n]) for r, group in zip(out_refs, groups) for n, i in enumerate(group)]
     rows = row_count(query_refs[0])
     owner = jnp.concatenate([extra_of(q)[:, 0:1] for q in query_refs for _ in range(rows // EXTRA)])
     mine = owner.astype(jnp.float32) == column_slot_ref[0:1, :]
@@ -196,24 +196,24 @@
         ]
         scores[-1] = jnp.where(mine, scores[-1], FILLER)
         mean, end = block_softmax(scores, [r[:, at] for r in value_refs] + [tab_values])
-        for i, place in enumerate(places):
+        for i, place in places:
             place[n] = mean[i * rows : (i + 1) * rows]
         ends = put_lane(ends, h, end)
-    for i, place in enumerate(places):
+    for i, place in places:
         place[len(heads)] = ends[i * rows : (i + 1) * rows]
 
 
-def context_states(heads, sizes, pieces, keys, values, column_slot, tabs):
-    members, rows = sum(sizes), row_count(pieces[0])
+def context_states(heads, groups, pieces, keys, values, column_slot, tabs):
+    members, rows = sum(len(group) for group in groups), row_count(pieces[0])
     key_count = sum(k.shape[0] for k in keys) + column_slot.shape[1]
     work = members * rows * len(heads) * key_count
     return pl.pallas_call(
-        functools.partial(context_kernel, heads, sizes, len(pieces), len(keys), len(tabs)),
+        functools.partial(context_kernel, heads, groups, len(pieces), len(keys), len(tabs)),
         in_specs=in_vmem(1 + len(pieces) + 2 * len(keys) + len(tabs)),
-        out_specs=in_vmem(len(sizes)),
+        out_specs=in_vmem(len(groups)),
         out_shape=[
-            jax.ShapeDtypeStruct((size, len(heads) + 1, rows, HEAD_SIZE), jnp.float32)
-            for size in sizes
+            jax.ShapeDtypeStruct((len(group), len(heads) + 1, rows, HEAD_SIZE), jnp.float32)
+            for group in groups
         ],
         compiler_params=pltpu.CompilerParams(vmem_limit_bytes=vmem_limit(members, len(tabs))),
         cost_estimate=pl.CostEstimate(
@@ -291,11 +291,11 @@
 
 def pair_kernel(order, low_ref, high_ref, other_ref, *coded_refs):
     rows = other_ref.shape[2]
-    for i, coded_ref in zip(order, coded_refs):
+    for (i, at), coded_ref in zip(order, coded_refs):
         own, own_end = both_halves(i, low_ref, high_ref)
-        shares, end = shares_of([own_end, other_ref[i - 1, KEY_VALUE_HEADS]])
+        shares, end = shares_of([own_end, other_ref[at, KEY_VALUE_HEADS]])
         means = [
-            mixed([own[h][...], other_ref[i - 1, h]], shares, h) for h in range(KEY_VALUE_HEADS)
+            mixed([own[h][...], other_ref[at, h]], shares, h) for h in range(KEY_VALUE_HEADS)
         ]
         reach = jnp.ones((rows, HEAD_SIZE), jnp.float32)
         for h, mean in enumerate(means):
@@ -307,14 +307,14 @@
             coded_ref[pl.ds(h * rows, rows)] = code.astype(jnp.int32).astype(jnp.int16)
         near = jnp.round(end)
         rest = jnp.round((end - near) * REST_TOP)
-        at = lax.broadcasted_iota(jnp.int32, (EXTRA, HEAD_SIZE), 1) // KEY_VALUE_HEADS
+        lane = lax.broadcasted_iota(jnp.int32, (EXTRA, HEAD_SIZE), 1) // KEY_VALUE_HEADS
         slab, kinds = jnp.zeros((EXTRA, HEAD_SIZE), jnp.float32), (near, rest, exponent)
         for r in range(rows // EXTRA):
             for k, kind in enumerate(kinds):
                 place = r * len(kinds) + k
                 part = kind[r * EXTRA : (r + 1) * EXTRA]
                 moved = pltpu.roll(part, place * KEY_VALUE_HEADS, 1) if place else part
-                slab = jnp.where(at == place, moved, slab)
+                slab = jnp.where(lane == place, moved, slab)
         coded_ref[pl.ds(KEY_VALUE_HEADS * rows, EXTRA)] = slab.astype(jnp.int32).astype(jnp.int16)
 
 
@@ -408,18 +408,29 @@
     shared = (keys, values, column_slot, tabs)
     heads = tuple(range(KEY_VALUE_HEADS))
     first, second = heads[:5], heads[5:]
-    (low,) = context_states(first, (pair_count,), pieces, *shared)
+    members = range(pair_count)
+    far = [i for i in members if masks[i] >= pair_count // 2]
+    rest = [i for i in members if i not in far]
+    (low,) = context_states(first, [members], pieces, *shared)
     other_pieces, low = lax.optimization_barrier((other_pieces, low))
-    near, far = context_states(heads, (1, pair_count - 1), other_pieces, *shared)
-    pieces, far = lax.optimization_barrier((pieces, far))
-    far = lax.ppermute(far, "ctx", swap(ctx_count, 1))
-    near = lax.ppermute(near, "ctx", swap(ctx_count, 1))
-    (high,) = context_states(second, (pair_count,), pieces, *shared)
-    order = sorted(range(1, pair_count), key=lambda i: (masks[i] < pair_count // 2, masks[i]))
-    coded = pair_states(order, low, high, far)
-    received = [
-        lax.ppermute(code, "ctx", swap(ctx_count, 2 * masks[i])) for i, code in zip(order, coded)
-    ]
+    others = context_states(heads, [far, rest], other_pieces, *shared)
+    pieces, others = lax.optimization_barrier((pieces, others))
+    others = list(others)
+    others[0] = lax.ppermute(others[0], "ctx", swap(ctx_count, 1))
+    (high,) = context_states(second, [members], pieces, *shared)
+    coded, received = [], []
+    for group, other in zip((far, rest), others):
+        if coded:
+            coded, other = lax.optimization_barrier((coded, other))
+            other = others[1] = lax.ppermute(other, "ctx", swap(ctx_count, 1))
+        order = [(i, at) for at, i in enumerate(group) if i]
+        if order:
+            codes = pair_states(order, low, high, other)
+            coded += codes
+            received += [
+                lax.ppermute(code, "ctx", swap(ctx_count, 2 * masks[i]))
+                for (i, _), code in zip(order, codes)
+            ]
     home = home_state(
         message,
         suffix_key_value[0],
@@ -428,7 +439,7 @@
         token_values[0],
         low,
         high,
-        near,
+        others[1],
         after=coded,
     )
     result = final_output(home, received)

time: 34.4 us -> 34.4 us (level)
    pallas_call x1 -> x2, Pallas kernels: 1 us -> 1.08 us  [pair_states(): pl.pallas_call(functools.partial(pair_kernel, order), out_shape=[jax.Shap...]
  transfers between devices with their start and end apart: 12 -> 12, of which waited for: 8 -> 8; matrix products, arithmetic and copies ran while one was open for 0% -> 0% of each run, Pallas kernels for 25% -> 23%
where the time goes in v7:
time: 34.4 us; the launch traced here: 34.2 us
  starting transfers between devices  14.3 us (42%)
  Pallas kernels  12.2 us (35%)
  waiting for transfers between devices  6.19 us (18%)
  between operations  1.45 us (4%)
    ppermute x2, starting transfers between devices, shards(): pieces = [column, lax.ppermute(column, 'ctx', swap(ctx_count, 2 * bit))]  4.87 us
    ppermute x3, starting transfers between devices, shards(): lax.ppermute(tab_block, 'tab', swap(tab_count, k))  4.6 us
    ppermute x3, starting transfers between devices, shards(): lax.ppermute(code, 'ctx', swap(ctx_count, 2 * masks[i]))  4.23 us
    pallas_call x2, Pallas kernels, split_pairs(): pl.pallas_call(functools.partial(split_kernel, first, chunks), in_specs=i...  3.64 us
    pallas_call x3, Pallas kernels, context_states(): pl.pallas_call(functools.partial(context_kernel, heads, groups, len(piece...  3.2 us
    ppermute x3, waiting for transfers between devices, shards(): lax.ppermute(code, 'ctx', swap(ctx_count, 2 * masks[i]))  2.32 us
    pallas_call x1, Pallas kernels, home_state(): pl.pallas_call(functools.partial(home_kernel, steps), in_specs=in_smem(1)...  2.1 us
    ppermute x2, waiting for transfers between devices, shards(): pieces = [column, lax.ppermute(column, 'ctx', swap(ctx_count, 2 * bit))]  1.81 us
  transfers between devices with their start and end apart: 12, of which 8 were waited for; matrix products, arithmetic and copies ran while one was open for 0% of the time, Pallas kernels for 23%

profile of v7, /device:TPU:0, one launch (start us, length us, event | category | flops | bytes accessed | tf_op | source)
XLA Modules:
  0.0 34.2 jit_solution(1089611649090378960)
XLA Ops:
  0.7 1.2 %prepare.1 = (bf16[1,264,128]{2,1,0:T(8,128)(2,1)S(1)}, bf16[2,64,1024]{2,1,0:T(8,128)(2,1)S(1)}) custom-call(s32[1]{0:T(128)S(6)} %copy.16.session, s32[4]{0:T(128)} %owner_hbm.1, bf16[256,128]{1,0:T(8,128)(2,1)} %bitcast.33, bf16[1024,128]{1,0:T(8,128)(2,1)} %bitcast.32), custom_call_target="tpu_custom_call" | custom-call | tf_op jit(solution)/shard_map/prepare/pallas_call | solution.py:97
  1.9 4.0 %collective-permute-start.5 = (bf16[2,64,1024]{2,1,0:T(8,128)(2,1)S(1)}, bf16[2,64,1024]{2,1,0:T(8,128)(2,1)S(1)}, u32[]{:S(2)}, u32[]{:S(2)}) collective-permute-start(bf16[2,64,1024]{2,1,0:T(8,128)(2,1)S(1)} %get-tuple-element.51.refs_6_), channel_id=1, source_target_pairs={{0,3},{1,2},{2,1},{3,0},{4,7},{5,6},{6,5},{7,4},{8,11},{9,10},{10,... | collective-permute-start | bytes 786440 | tf_op jit(solution)/shard_map/ppermute | solution.py:390
  5.8 0.5 %collective-permute-start.4 = (bf16[2,64,1024]{2,1,0:T(8,128)(2,1)S(1)}, bf16[2,64,1024]{2,1,0:T(8,128)(2,1)S(1)}, u32[]{:S(2)}, u32[]{:S(2)}) collective-permute-start(bf16[2,64,1024]{2,1,0:T(8,128)(2,1)S(1)} %get-tuple-element.51.refs_6_), channel_id=1, source_target_pairs={{0,2},{1,3},{2,0},{3,1},{4,6},{5,7},{6,4},{7,5},{8,10},{9,11},{10,... | collective-permute-start | bytes 786440 | tf_op jit(solution)/shard_map/ppermute | solution.py:390
  6.3 0.1 collective-permute-start.3
  6.5 3.0 %collective-permute-start = (bf16[1,264,128]{2,1,0:T(8,128)(2,1)S(1)}, bf16[1,264,128]{2,1,0:T(8,128)(2,1)S(1)}, u32[]{:S(2)}, u32[]{:S(2)}) collective-permute-start(bf16[1,264,128]{2,1,0:T(8,128)(2,1)S(1)} %get-tuple-element.37.query_ref), channel_id=1, source_target_pairs={{0,16},{4,20},{8,24},{12,28},{16,0},{20,4},{24,8},{28,12},{1,17},{... | collective-permute-start | bytes 202760 | tf_op jit(solution)/shard_map/ppermute | solution.py:403
  9.5 1.8 %split_pairs.2 = (bf16[256,1024]{1,0:T(8,128)(2,1)S(1)}, bf16[256,1024]{1,0:T(8,128)(2,1)S(1)}) custom-call(bf16[8192,128]{1,0:T(8,128)(2,1)} %bitcast.30), custom_call_target="tpu_custom_call" | custom-call | tf_op jit(solution)/shard_map/split_pairs/pallas_call | solution.py:137
  11.3 0.5 %collective-permute-done = bf16[1,264,128]{2,1,0:T(8,128)(2,1)S(1)} collective-permute-done((bf16[1,264,128]{2,1,0:T(8,128)(2,1)S(1)}, bf16[1,264,128]{2,1,0:T(8,128)(2,1)S(1)}, u32[]{:S(2)}, u32[]{:S(2)}) %collective-permute-start) | collective-permute-done | bytes 67616 | tf_op jit(solution)/shard_map/ppermute | solution.py:403
  11.8 1.9 %collective-permute-start.2 = (bf16[2,264,128]{2,1,0:T(8,128)(2,1)S(1)}, bf16[2,264,128]{2,1,0:T(8,128)(2,1)S(1)}, u32[]{:S(2)}, u32[]{:S(2)}) collective-permute-start(bf16[2,264,128]{2,1,0:T(8,128)(2,1)S(1)} %constant_dynamic-update-slice_fusion.refs_0_), channel_id=1, source_target_pairs={{0,8},{4,12},{8,0},{12,4},{16,24},{20,28},{24,16},{28,20},{1,9},{5... | collective-permute-start | bytes 405512 | tf_op jit(solution)/shard_map/ppermute | solution.py:403
  13.7 1.8 %split_pairs.3 = (bf16[256,1024]{1,0:T(8,128)(2,1)S(1)}, bf16[256,1024]{1,0:T(8,128)(2,1)S(1)}) custom-call(bf16[8192,128]{1,0:T(8,128)(2,1)} %bitcast.31), custom_call_target="tpu_custom_call" | custom-call | tf_op jit(solution)/shard_map/split_pairs/pallas_call | solution.py:137
  15.5 0.1 collective-permute-start.1
  15.6 1.3 %collective-permute-done.2.refs_1_ = bf16[2,264,128]{2,1,0:T(8,128)(2,1)S(1)} collective-permute-done((bf16[2,264,128]{2,1,0:T(8,128)(2,1)S(1)}, bf16[2,264,128]{2,1,0:T(8,128)(2,1)S(1)}, u32[]{:S(2)}, u32[]{:S(2)}) %collective-permute-start.2) | collective-permute-done | bytes 135200 | tf_op jit(solution)/shard_map/ppermute | solution.py:403
  16.9 0.8 %collective-permute-done.4.refs_8_ = bf16[2,64,1024]{2,1,0:T(8,128)(2,1)S(1)} collective-permute-done((bf16[2,64,1024]{2,1,0:T(8,128)(2,1)S(1)}, bf16[2,64,1024]{2,1,0:T(8,128)(2,1)S(1)}, u32[]{:S(2)}, u32[]{:S(2)}) %collective-permute-start.4) | collective-permute-done | bytes 262176 | tf_op jit(solution)/shard_map/ppermute | solution.py:390
  17.7 0.3 collective-permute-done.3.refs_7_
  18.0 1.0 %context_states.3.low_ref = f32[4,6,32,128]{3,2,1,0:T(8,128)S(1)} custom-call(f32[1,256]{1,0:T(1,128)S(1)} %fusion.1.column_slot_ref, bf16[2,264,128]{2,1,0:T(8,128)(2,1)S(1)} %constant_dynamic-update-slice_fusion.refs_0_, bf16[2,264,128]{2,1,0:T(8,128)(2,1)S(1)} %collective-permute-done.2.refs_1_, bf16[256,1024]{1,0:T(8,128)(2,1)S(1)} %get-tuple-element.47.refs_2_, ...), custom_call_target="tpu_custom_call" | custom-call | flops 251658240 | bytes 1 | tf_op jit(solution)/shard_map/context_states/pallas_call | solution.py:210
  19.1 0.3 collective-permute-done.6.refs_1_
  19.4 1.4 %context_states.4 = (f32[2,9,32,128]{3,2,1,0:T(8,128)S(1)}, f32[2,9,32,128]{3,2,1,0:T(8,128)S(1)}) custom-call(f32[1,256]{1,0:T(1,128)S(1)} %fusion.1.column_slot_ref, bf16[2,264,128]{2,1,0:T(8,128)(2,1)S(1)} %collective-permute-done.1.refs_0_, bf16[2,264,128]{2,1,0:T(8,128)(2,1)S(1)} %collective-permute-done.6.refs_1_, ...), custom_call_target="tpu_custom_call" | custom-call | flops 402653184 | bytes 1 | tf_op jit(solution)/shard_map/context_states/pallas_call | solution.py:210
  20.8 0.0 copy-start
  20.8 0.0 copy-start.1
  20.9 0.0 copy-start.2
  20.9 0.3 collective-permute-start.7
  21.1 0.7 %context_states.5.high_ref = f32[4,4,32,128]{3,2,1,0:T(8,128)S(1)} custom-call(f32[1,256]{1,0:T(1,128)S(1)} %fusion.1.column_slot_ref, bf16[2,264,128]{2,1,0:T(8,128)(2,1)S(1)} %constant_dynamic-update-slice_fusion.refs_0_, bf16[2,264,128]{2,1,0:T(8,128)(2,1)S(1)} %collective-permute-done.2.refs_1_, bf16[256,1024]{1,0:T(8,128)(2,1)S(1)} %get-tuple-element.47.refs_2_, ...), custom_call_target="tpu_custom_call" | custom-call | flops 150994944 | bytes 1 | tf_op jit(solution)/shard_map/context_states/pallas_call | solution.py:210
  21.9 0.6 %collective-permute-done.7.other_ref = f32[2,9,32,128]{3,2,1,0:T(8,128)S(1)} collective-permute-done((f32[2,9,32,128]{3,2,1,0:T(8,128)S(1)}, f32[2,9,32,128]{3,2,1,0:T(8,128)S(1)}, u32[]{:S(2)}, u32[]{:S(2)}) %collective-permute-start.7) | collective-permute-done | bytes 294944 | tf_op jit(solution)/shard_map/ppermute | solution.py:419
  22.5 0.7 %pair_states.2 = (s16[264,128]{1,0:T(8,128)(2,1)S(1)}, s16[264,128]{1,0:T(8,128)(2,1)S(1)}) custom-call(f32[4,6,32,128]{3,2,1,0:T(8,128)S(1)} %context_states.3.low_ref, f32[4,4,32,128]{3,2,1,0:T(8,128)S(1)} %context_states.5.high_ref, f32[2,9,32,128]{3,2,1,0:T(8,128)S(1)} %collective-permute-done.7.other_ref), custom_call_target="tpu_custom_call" | custom-call | tf_op jit(solution)/shard_map/pair_states/pallas_call | solution.py:324
  23.2 0.3 collective-permute-start.8
  23.5 2.6 %collective-permute-start.9 = (s16[264,128]{1,0:T(8,128)(2,1)S(1)}, s16[264,128]{1,0:T(8,128)(2,1)S(1)}, u32[]{:S(2)}, u32[]{:S(2)}) collective-permute-start(s16[264,128]{1,0:T(8,128)(2,1)S(1)} %get-tuple-element.67.refs_0_), channel_id=1, source_target_pairs={{0,16},{4,20},{8,24},{12,28},{16,0},{20,4},{24,8},{28,12},{1,17},{... | collective-permute-start | bytes 202760 | tf_op jit(solution)/shard_map/ppermute | solution.py:431
  26.1 1.4 %collective-permute-start.10 = (s16[264,128]{1,0:T(8,128)(2,1)S(1)}, s16[264,128]{1,0:T(8,128)(2,1)S(1)}, u32[]{:S(2)}, u32[]{:S(2)}) collective-permute-start(s16[264,128]{1,0:T(8,128)(2,1)S(1)} %get-tuple-element.68.refs_1_), channel_id=1, source_target_pairs={{0,24},{4,28},{8,16},{12,20},{16,8},{20,12},{24,0},{28,4},{1,25},{... | collective-permute-start | bytes 202760 | tf_op jit(solution)/shard_map/ppermute | solution.py:431
  27.4 0.4 %pair_states.3.refs_2_ = s16[264,128]{1,0:T(8,128)(2,1)S(1)} custom-call(f32[4,6,32,128]{3,2,1,0:T(8,128)S(1)} %context_states.3.low_ref, f32[4,4,32,128]{3,2,1,0:T(8,128)S(1)} %context_states.5.high_ref, f32[2,9,32,128]{3,2,1,0:T(8,128)S(1)} %collective-permute-done.8.other_ref), custom_call_target="tpu_custom_call" | custom-call | tf_op jit(solution)/shard_map/pair_states/pallas_call | solution.py:324
  27.8 0.3 collective-permute-start.11
  28.8 2.1 %home_state.1.home_ref = f32[9,32,128]{2,1,0:T(8,128)S(1)} custom-call(s32[1]{0:T(128)S(6)} %copy.17.length_ref, bf16[1,264,128]{2,1,0:T(8,128)(2,1)S(1)} %get-tuple-element.37.query_ref, bf16[4096,128]{1,0:T(8,128)(2,1)S(1)} %bitcast.27, bf16[4,1024]{1,0:T(4,128)(2,1)S(1)} %bitcast.28, bf16[4,1024]{1,0:T(4,128)(2,1)S(1)} %bitcast.29, ...), custom_call_target="tpu_custom_call" | custom-call | flops 33554432 | bytes 2097152 | tf_op jit(solution)/shard_map/home_state/pallas_call | solution.py:275
  30.9 1.9 %collective-permute-done.10.refs_1_ = s16[264,128]{1,0:T(8,128)(2,1)S(1)} collective-permute-done((s16[264,128]{1,0:T(8,128)(2,1)S(1)}, s16[264,128]{1,0:T(8,128)(2,1)S(1)}, u32[]{:S(2)}, u32[]{:S(2)}) %collective-permute-start.10) | collective-permute-done | bytes 67616 | tf_op jit(solution)/shard_map/ppermute | solution.py:431
  32.8 0.4 %collective-permute-done.11.refs_2_ = s16[264,128]{1,0:T(8,128)(2,1)S(1)} collective-permute-done((s16[264,128]{1,0:T(8,128)(2,1)S(1)}, s16[264,128]{1,0:T(8,128)(2,1)S(1)}, u32[]{:S(2)}, u32[]{:S(2)}) %collective-permute-start.11) | collective-permute-done | bytes 67616 | tf_op jit(solution)/shard_map/ppermute | solution.py:431
  33.2 1.0 %final_output.1 = bf16[8,32,128]{2,1,0:T(8,128)(2,1)} custom-call(f32[9,32,128]{2,1,0:T(8,128)S(1)} %home_state.1.home_ref, s16[264,128]{1,0:T(8,128)(2,1)S(1)} %collective-permute-done.9.refs_0_, s16[264,128]{1,0:T(8,128)(2,1)S(1)} %collective-permute-done.10.refs_1_, s16[264,128]{1,0:T(8,128)(2,1)S(1)} %collective-permute-done.11.refs_2_), custom_call_target="tpu_custom_call" | custom-call | tf_op jit(solution)/shard_map/final_output/pallas_call | solution.py:358
  (11 shorter events, 0.0 us)
Async XLA Ops:
  1.9 15.0 %collective-permute-start.5 = (bf16[2,64,1024]{2,1,0:T(8,128)(2,1)S(1)}, bf16[2,64,1024]{2,1,0:T(8,128)(2,1)S(1)}, u32[]{:S(2)}, u32[]{:S(2)}) collective-permute-start(bf16[2,64,1024]{2,1,0:T(8,128)(2,1)S(1)} %get-tuple-element.51.refs_6_), channel_id=1, source_target_pairs={{0,3},{1,2},{2,1},{3,0},{4,7},{5,6},{6,5},{7,4},{8,11},{9,10},{10,... | collective-permute-start | bytes 786440 | tf_op jit(solution)/shard_map/ppermute | solution.py:390
  5.8 11.9 %collective-permute-start.4 = (bf16[2,64,1024]{2,1,0:T(8,128)(2,1)S(1)}, bf16[2,64,1024]{2,1,0:T(8,128)(2,1)S(1)}, u32[]{:S(2)}, u32[]{:S(2)}) collective-permute-start(bf16[2,64,1024]{2,1,0:T(8,128)(2,1)S(1)} %get-tuple-element.51.refs_6_), channel_id=1, source_target_pairs={{0,2},{1,3},{2,0},{3,1},{4,6},{5,7},{6,4},{7,5},{8,10},{9,11},{10,... | collective-permute-start | bytes 786440 | tf_op jit(solution)/shard_map/ppermute | solution.py:390
  6.3 11.7 %collective-permute-start.3 = (bf16[2,64,1024]{2,1,0:T(8,128)(2,1)S(1)}, bf16[2,64,1024]{2,1,0:T(8,128)(2,1)S(1)}, u32[]{:S(2)}, u32[]{:S(2)}) collective-permute-start(bf16[2,64,1024]{2,1,0:T(8,128)(2,1)S(1)} %get-tuple-element.51.refs_6_), channel_id=1, source_target_pairs={{0,1},{1,0},{2,3},{3,2},{4,5},{5,4},{6,7},{7,6},{8,9},{9,8},{10,11... | collective-permute-start | bytes 786440 | tf_op jit(solution)/shard_map/ppermute | solution.py:390
  6.5 5.3 %collective-permute-start = (bf16[1,264,128]{2,1,0:T(8,128)(2,1)S(1)}, bf16[1,264,128]{2,1,0:T(8,128)(2,1)S(1)}, u32[]{:S(2)}, u32[]{:S(2)}) collective-permute-start(bf16[1,264,128]{2,1,0:T(8,128)(2,1)S(1)} %get-tuple-element.37.query_ref), channel_id=1, source_target_pairs={{0,16},{4,20},{8,24},{12,28},{16,0},{20,4},{24,8},{28,12},{1,17},{... | collective-permute-start | bytes 202760 | tf_op jit(solution)/shard_map/ppermute | solution.py:403
  11.8 5.1 %collective-permute-start.2 = (bf16[2,264,128]{2,1,0:T(8,128)(2,1)S(1)}, bf16[2,264,128]{2,1,0:T(8,128)(2,1)S(1)}, u32[]{:S(2)}, u32[]{:S(2)}) collective-permute-start(bf16[2,264,128]{2,1,0:T(8,128)(2,1)S(1)} %constant_dynamic-update-slice_fusion.refs_0_), channel_id=1, source_target_pairs={{0,8},{4,12},{8,0},{12,4},{16,24},{20,28},{24,16},{28,20},{1,9},{5... | collective-permute-start | bytes 405512 | tf_op jit(solution)/shard_map/ppermute | solution.py:403
  15.5 3.5 %collective-permute-start.1 = (bf16[2,264,128]{2,1,0:T(8,128)(2,1)S(1)}, bf16[2,264,128]{2,1,0:T(8,128)(2,1)S(1)}, u32[]{:S(2)}, u32[]{:S(2)}) collective-permute-start(bf16[2,264,128]{2,1,0:T(8,128)(2,1)S(1)} %constant_dynamic-update-slice_fusion.refs_0_), channel_id=1, source_target_pairs={{0,4},{4,0},{8,12},{12,8},{16,20},{20,16},{24,28},{28,24},{1,5},{5... | collective-permute-start | bytes 405512 | tf_op jit(solution)/shard_map/ppermute | solution.py:406
  18.0 1.4 %collective-permute-start.6 = (bf16[2,264,128]{2,1,0:T(8,128)(2,1)S(1)}, bf16[2,264,128]{2,1,0:T(8,128)(2,1)S(1)}, u32[]{:S(2)}, u32[]{:S(2)}) collective-permute-start(bf16[2,264,128]{2,1,0:T(8,128)(2,1)S(1)} %collective-permute-done.2.refs_1_), channel_id=1, source_target_pairs={{0,4},{4,0},{8,12},{12,8},{16,20},{20,16},{24,28},{28,24},{1,5},{5... | collective-permute-start | bytes 405512 | tf_op jit(solution)/shard_map/ppermute | solution.py:406
  20.8 7.9 %copy-start = (bf16[1,256,2,1024]{3,2,1,0:T(2,128)(2,1)S(1)}, bf16[1,256,2,1024]{3,2,1,0:T(2,128)(2,1)}, u32[]{:S(2)}) copy-start(bf16[1,256,2,1024]{3,2,1,0:T(2,128)(2,1)} %param.14) | copy-start | bytes 3145732
  20.8 7.9 %copy-start.1 = (bf16[1,4,1024]{2,1,0:T(4,128)(2,1)S(1)}, bf16[1,4,1024]{2,1,0:T(4,128)(2,1)}, u32[]{:S(2)}) copy-start(bf16[1,4,1024]{2,1,0:T(4,128)(2,1)} %param.16) | copy-start | bytes 24580
  20.9 7.9 %copy-start.2 = (bf16[1,4,1024]{2,1,0:T(4,128)(2,1)S(1)}, bf16[1,4,1024]{2,1,0:T(4,128)(2,1)}, u32[]{:S(2)}) copy-start(bf16[1,4,1024]{2,1,0:T(4,128)(2,1)} %param.17) | copy-start | bytes 24580
  20.9 1.6 %collective-permute-start.7 = (f32[2,9,32,128]{3,2,1,0:T(8,128)S(1)}, f32[2,9,32,128]{3,2,1,0:T(8,128)S(1)}, u32[]{:S(2)}, u32[]{:S(2)}) collective-permute-start(f32[2,9,32,128]{3,2,1,0:T(8,128)S(1)} %get-tuple-element.62), channel_id=1, source_target_pairs={{0,4},{4,0},{8,12},{12,8},{16,20},{20,16},{24,28},{28,24},{1,5},{5... | collective-permute-start | bytes 884744 | tf_op jit(solution)/shard_map/ppermute | solution.py:419
  23.2 4.2 %collective-permute-start.8 = (f32[2,9,32,128]{3,2,1,0:T(8,128)S(1)}, f32[2,9,32,128]{3,2,1,0:T(8,128)S(1)}, u32[]{:S(2)}, u32[]{:S(2)}) collective-permute-start(f32[2,9,32,128]{3,2,1,0:T(8,128)S(1)} %get-tuple-element.66), channel_id=1, source_target_pairs={{0,4},{4,0},{8,12},{12,8},{16,20},{20,16},{24,28},{28,24},{1,5},{5... | collective-permute-start | bytes 884744 | tf_op jit(solution)/shard_map/ppermute | solution.py:425
  23.5 7.4 %collective-permute-start.9 = (s16[264,128]{1,0:T(8,128)(2,1)S(1)}, s16[264,128]{1,0:T(8,128)(2,1)S(1)}, u32[]{:S(2)}, u32[]{:S(2)}) collective-permute-start(s16[264,128]{1,0:T(8,128)(2,1)S(1)} %get-tuple-element.67.refs_0_), channel_id=1, source_target_pairs={{0,16},{4,20},{8,24},{12,28},{16,0},{20,4},{24,8},{28,12},{1,17},{... | collective-permute-start | bytes 202760 | tf_op jit(solution)/shard_map/ppermute | solution.py:431
  26.1 6.7 %collective-permute-start.10 = (s16[264,128]{1,0:T(8,128)(2,1)S(1)}, s16[264,128]{1,0:T(8,128)(2,1)S(1)}, u32[]{:S(2)}, u32[]{:S(2)}) collective-permute-start(s16[264,128]{1,0:T(8,128)(2,1)S(1)} %get-tuple-element.68.refs_1_), channel_id=1, source_target_pairs={{0,24},{4,28},{8,16},{12,20},{16,8},{20,12},{24,0},{28,4},{1,25},{... | collective-permute-start | bytes 202760 | tf_op jit(solution)/shard_map/ppermute | solution.py:431
  27.8 5.4 %collective-permute-start.11 = (s16[264,128]{1,0:T(8,128)(2,1)S(1)}, s16[264,128]{1,0:T(8,128)(2,1)S(1)}, u32[]{:S(2)}, u32[]{:S(2)}) collective-permute-start(s16[264,128]{1,0:T(8,128)(2,1)S(1)} %pair_states.3.refs_2_), channel_id=1, source_target_pairs={{0,8},{4,12},{8,0},{12,4},{16,24},{20,28},{24,16},{28,20},{1,9},{5... | collective-permute-start | bytes 202760 | tf_op jit(solution)/shard_map/ppermute | solution.py:431

commit v8 on v7

--- a/solution.py
+++ b/solution.py
@@ -69,9 +69,11 @@
 def prepare_kernel(
     session, owner_hbm, query_hbm, tab_hbm, message_ref, block_ref, tiles, wide, owner, sems
 ):
+    half = tiles.shape[0] // 2
     moves = [
-        (tab_hbm, tiles),
+        (tab_hbm.at[pl.ds(0, half)], tiles.at[pl.ds(0, half)]),
         (owner_hbm, owner),
+        (tab_hbm.at[pl.ds(half, half)], tiles.at[pl.ds(half, half)]),
         (query_hbm, message_ref.at[0, pl.ds(0, query_hbm.shape[0])]),
     ]
     copies = [pltpu.make_async_copy(*move, sems.at[i]) for i, move in enumerate(moves)]
@@ -84,8 +86,11 @@
     filled = jnp.full((EXTRA, HEAD_SIZE), slot.astype(jnp.float32), jnp.float32)
     message_ref[0, pl.ds(query_hbm.shape[0], EXTRA)] = filled.astype(jnp.bfloat16)
     copies[0].wait()
-    split_rows(tiles, wide, 0, block_ref.shape[1], block_ref.at[0], block_ref.at[1])
+    rows = block_ref.shape[1] // 2
+    split_rows(tiles, wide, 0, rows, block_ref.at[0], block_ref.at[1])
     copies[2].wait()
+    split_rows(tiles, wide, rows, rows, block_ref.at[0], block_ref.at[1])
+    copies[3].wait()
 
 
 def stay(arrays):
@@ -131,7 +136,7 @@
         split_rows(tiles, wide, i * rows, rows, key_ref, value_ref)
 
 
-def split_pairs(tiles, first, rows, chunks=4):
+def split_pairs(tiles, first, rows, chunks=2):
     shape = jax.ShapeDtypeStruct((rows, KEY_VALUE_HEADS * HEAD_SIZE), tiles.dtype)
     scratch = (rows * PER_ROW, HEAD_SIZE)
     return pl.pallas_call(

time: 34.4 us -> 34.3 us (level)
  no operation moved by 1% of the time
where the time goes in v8:
time: 34.3 us; the launch traced here: 34.2 us
  starting transfers between devices  14.3 us (42%)
  Pallas kernels  12.3 us (36%)
  waiting for transfers between devices  6.06 us (18%)
  between operations  1.45 us (4%)
    ppermute x2, starting transfers between devices, shards(): pieces = [column, lax.ppermute(column, 'ctx', swap(ctx_count, 2 * bit))]  4.87 us
    ppermute x3, starting transfers between devices, shards(): lax.ppermute(tab_block, 'tab', swap(tab_count, k))  4.6 us
    ppermute x3, starting transfers between devices, shards(): lax.ppermute(code, 'ctx', swap(ctx_count, 2 * masks[i]))  4.23 us
    pallas_call x2, Pallas kernels, split_pairs(): pl.pallas_call(functools.partial(split_kernel, first, chunks), in_specs=i...  3.78 us
    pallas_call x3, Pallas kernels, context_states(): pl.pallas_call(functools.partial(context_kernel, heads, groups, len(piece...  3.2 us
    ppermute x3, waiting for transfers between devices, shards(): lax.ppermute(code, 'ctx', swap(ctx_count, 2 * masks[i]))  2.33 us
    pallas_call x1, Pallas kernels, home_state(): pl.pallas_call(functools.partial(home_kernel, steps), in_specs=in_smem(1)...  2.09 us
    ppermute x2, waiting for transfers between devices, shards(): pieces = [column, lax.ppermute(column, 'ctx', swap(ctx_count, 2 * bit))]  1.67 us
  transfers between devices with their start and end apart: 12, of which 8 were waited for; matrix products, arithmetic and copies ran while one was open for 0% of the time, Pallas kernels for 23%

profile of v8, /device:TPU:0, one launch (start us, length us, event | category | flops | bytes accessed | tf_op | source)
XLA Modules:
  0.0 34.2 jit_solution(11185920303973155087)
XLA Ops:
  0.7 1.2 %prepare.1 = (bf16[1,264,128]{2,1,0:T(8,128)(2,1)S(1)}, bf16[2,64,1024]{2,1,0:T(8,128)(2,1)S(1)}) custom-call(s32[1]{0:T(128)S(6)} %copy.16.session, s32[4]{0:T(128)} %owner_hbm.1, bf16[256,128]{1,0:T(8,128)(2,1)} %bitcast.33, bf16[1024,128]{1,0:T(8,128)(2,1)} %bitcast.32), custom_call_target="tpu_custom_call" | custom-call | tf_op jit(solution)/shard_map/prepare/pallas_call | solution.py:102
  1.8 4.0 %collective-permute-start.5 = (bf16[2,64,1024]{2,1,0:T(8,128)(2,1)S(1)}, bf16[2,64,1024]{2,1,0:T(8,128)(2,1)S(1)}, u32[]{:S(2)}, u32[]{:S(2)}) collective-permute-start(bf16[2,64,1024]{2,1,0:T(8,128)(2,1)S(1)} %get-tuple-element.51.refs_6_), channel_id=1, source_target_pairs={{0,3},{1,2},{2,1},{3,0},{4,7},{5,6},{6,5},{7,4},{8,11},{9,10},{10,... | collective-permute-start | bytes 786440 | tf_op jit(solution)/shard_map/ppermute | solution.py:395
  5.8 0.5 %collective-permute-start.4 = (bf16[2,64,1024]{2,1,0:T(8,128)(2,1)S(1)}, bf16[2,64,1024]{2,1,0:T(8,128)(2,1)S(1)}, u32[]{:S(2)}, u32[]{:S(2)}) collective-permute-start(bf16[2,64,1024]{2,1,0:T(8,128)(2,1)S(1)} %get-tuple-element.51.refs_6_), channel_id=1, source_target_pairs={{0,2},{1,3},{2,0},{3,1},{4,6},{5,7},{6,4},{7,5},{8,10},{9,11},{10,... | collective-permute-start | bytes 786440 | tf_op jit(solution)/shard_map/ppermute | solution.py:395
  6.3 0.1 collective-permute-start.3
  6.4 3.0 %collective-permute-start = (bf16[1,264,128]{2,1,0:T(8,128)(2,1)S(1)}, bf16[1,264,128]{2,1,0:T(8,128)(2,1)S(1)}, u32[]{:S(2)}, u32[]{:S(2)}) collective-permute-start(bf16[1,264,128]{2,1,0:T(8,128)(2,1)S(1)} %get-tuple-element.37.query_ref), channel_id=1, source_target_pairs={{0,16},{4,20},{8,24},{12,28},{16,0},{20,4},{24,8},{28,12},{1,17},{... | collective-permute-start | bytes 202760 | tf_op jit(solution)/shard_map/ppermute | solution.py:408
  9.4 1.9 %split_pairs.2 = (bf16[256,1024]{1,0:T(8,128)(2,1)S(1)}, bf16[256,1024]{1,0:T(8,128)(2,1)S(1)}) custom-call(bf16[8192,128]{1,0:T(8,128)(2,1)} %bitcast.30), custom_call_target="tpu_custom_call" | custom-call | tf_op jit(solution)/shard_map/split_pairs/pallas_call | solution.py:142
  11.3 0.5 %collective-permute-done = bf16[1,264,128]{2,1,0:T(8,128)(2,1)S(1)} collective-permute-done((bf16[1,264,128]{2,1,0:T(8,128)(2,1)S(1)}, bf16[1,264,128]{2,1,0:T(8,128)(2,1)S(1)}, u32[]{:S(2)}, u32[]{:S(2)}) %collective-permute-start) | collective-permute-done | bytes 67616 | tf_op jit(solution)/shard_map/ppermute | solution.py:408
  11.8 1.9 %collective-permute-start.2 = (bf16[2,264,128]{2,1,0:T(8,128)(2,1)S(1)}, bf16[2,264,128]{2,1,0:T(8,128)(2,1)S(1)}, u32[]{:S(2)}, u32[]{:S(2)}) collective-permute-start(bf16[2,264,128]{2,1,0:T(8,128)(2,1)S(1)} %constant_dynamic-update-slice_fusion.refs_0_), channel_id=1, source_target_pairs={{0,8},{4,12},{8,0},{12,4},{16,24},{20,28},{24,16},{28,20},{1,9},{5... | collective-permute-start | bytes 405512 | tf_op jit(solution)/shard_map/ppermute | solution.py:408
  13.7 1.9 %split_pairs.3 = (bf16[256,1024]{1,0:T(8,128)(2,1)S(1)}, bf16[256,1024]{1,0:T(8,128)(2,1)S(1)}) custom-call(bf16[8192,128]{1,0:T(8,128)(2,1)} %bitcast.31), custom_call_target="tpu_custom_call" | custom-call | tf_op jit(solution)/shard_map/split_pairs/pallas_call | solution.py:142
  15.6 0.1 collective-permute-start.1
  15.6 1.2 %collective-permute-done.2.refs_1_ = bf16[2,264,128]{2,1,0:T(8,128)(2,1)S(1)} collective-permute-done((bf16[2,264,128]{2,1,0:T(8,128)(2,1)S(1)}, bf16[2,264,128]{2,1,0:T(8,128)(2,1)S(1)}, u32[]{:S(2)}, u32[]{:S(2)}) %collective-permute-start.2) | collective-permute-done | bytes 135200 | tf_op jit(solution)/shard_map/ppermute | solution.py:408
  16.9 0.8 %collective-permute-done.4.refs_8_ = bf16[2,64,1024]{2,1,0:T(8,128)(2,1)S(1)} collective-permute-done((bf16[2,64,1024]{2,1,0:T(8,128)(2,1)S(1)}, bf16[2,64,1024]{2,1,0:T(8,128)(2,1)S(1)}, u32[]{:S(2)}, u32[]{:S(2)}) %collective-permute-start.4) | collective-permute-done | bytes 262176 | tf_op jit(solution)/shard_map/ppermute | solution.py:395
  17.7 0.3 collective-permute-done.3.refs_7_
  18.0 1.0 %context_states.3.low_ref = f32[4,6,32,128]{3,2,1,0:T(8,128)S(1)} custom-call(f32[1,256]{1,0:T(1,128)S(1)} %fusion.1.column_slot_ref, bf16[2,264,128]{2,1,0:T(8,128)(2,1)S(1)} %constant_dynamic-update-slice_fusion.refs_0_, bf16[2,264,128]{2,1,0:T(8,128)(2,1)S(1)} %collective-permute-done.2.refs_1_, bf16[256,1024]{1,0:T(8,128)(2,1)S(1)} %get-tuple-element.47.refs_2_, ...), custom_call_target="tpu_custom_call" | custom-call | flops 251658240 | bytes 1 | tf_op jit(solution)/shard_map/context_states/pallas_call | solution.py:215
  19.0 0.3 collective-permute-done.6.refs_1_
  19.3 1.4 %context_states.4 = (f32[2,9,32,128]{3,2,1,0:T(8,128)S(1)}, f32[2,9,32,128]{3,2,1,0:T(8,128)S(1)}) custom-call(f32[1,256]{1,0:T(1,128)S(1)} %fusion.1.column_slot_ref, bf16[2,264,128]{2,1,0:T(8,128)(2,1)S(1)} %collective-permute-done.1.refs_0_, bf16[2,264,128]{2,1,0:T(8,128)(2,1)S(1)} %collective-permute-done.6.refs_1_, ...), custom_call_target="tpu_custom_call" | custom-call | flops 402653184 | bytes 1 | tf_op jit(solution)/shard_map/context_states/pallas_call | solution.py:215
  20.8 0.0 copy-start
  20.8 0.0 copy-start.1
  20.8 0.0 copy-start.2
  20.8 0.3 collective-permute-start.7
  21.1 0.7 %context_states.5.high_ref = f32[4,4,32,128]{3,2,1,0:T(8,128)S(1)} custom-call(f32[1,256]{1,0:T(1,128)S(1)} %fusion.1.column_slot_ref, bf16[2,264,128]{2,1,0:T(8,128)(2,1)S(1)} %constant_dynamic-update-slice_fusion.refs_0_, bf16[2,264,128]{2,1,0:T(8,128)(2,1)S(1)} %collective-permute-done.2.refs_1_, bf16[256,1024]{1,0:T(8,128)(2,1)S(1)} %get-tuple-element.47.refs_2_, ...), custom_call_target="tpu_custom_call" | custom-call | flops 150994944 | bytes 1 | tf_op jit(solution)/shard_map/context_states/pallas_call | solution.py:215
  21.9 0.6 %collective-permute-done.7.other_ref = f32[2,9,32,128]{3,2,1,0:T(8,128)S(1)} collective-permute-done((f32[2,9,32,128]{3,2,1,0:T(8,128)S(1)}, f32[2,9,32,128]{3,2,1,0:T(8,128)S(1)}, u32[]{:S(2)}, u32[]{:S(2)}) %collective-permute-start.7) | collective-permute-done | bytes 294944 | tf_op jit(solution)/shard_map/ppermute | solution.py:424
  22.5 0.7 %pair_states.2 = (s16[264,128]{1,0:T(8,128)(2,1)S(1)}, s16[264,128]{1,0:T(8,128)(2,1)S(1)}) custom-call(f32[4,6,32,128]{3,2,1,0:T(8,128)S(1)} %context_states.3.low_ref, f32[4,4,32,128]{3,2,1,0:T(8,128)S(1)} %context_states.5.high_ref, f32[2,9,32,128]{3,2,1,0:T(8,128)S(1)} %collective-permute-done.7.other_ref), custom_call_target="tpu_custom_call" | custom-call | tf_op jit(solution)/shard_map/pair_states/pallas_call | solution.py:329
  23.2 0.3 collective-permute-start.8
  23.4 2.6 %collective-permute-start.9 = (s16[264,128]{1,0:T(8,128)(2,1)S(1)}, s16[264,128]{1,0:T(8,128)(2,1)S(1)}, u32[]{:S(2)}, u32[]{:S(2)}) collective-permute-start(s16[264,128]{1,0:T(8,128)(2,1)S(1)} %get-tuple-element.67.refs_0_), channel_id=1, source_target_pairs={{0,16},{4,20},{8,24},{12,28},{16,0},{20,4},{24,8},{28,12},{1,17},{... | collective-permute-start | bytes 202760 | tf_op jit(solution)/shard_map/ppermute | solution.py:436
  26.0 1.3 %collective-permute-start.10 = (s16[264,128]{1,0:T(8,128)(2,1)S(1)}, s16[264,128]{1,0:T(8,128)(2,1)S(1)}, u32[]{:S(2)}, u32[]{:S(2)}) collective-permute-start(s16[264,128]{1,0:T(8,128)(2,1)S(1)} %get-tuple-element.68.refs_1_), channel_id=1, source_target_pairs={{0,24},{4,28},{8,16},{12,20},{16,8},{20,12},{24,0},{28,4},{1,25},{... | collective-permute-start | bytes 202760 | tf_op jit(solution)/shard_map/ppermute | solution.py:436
  27.4 0.4 %pair_states.3.refs_2_ = s16[264,128]{1,0:T(8,128)(2,1)S(1)} custom-call(f32[4,6,32,128]{3,2,1,0:T(8,128)S(1)} %context_states.3.low_ref, f32[4,4,32,128]{3,2,1,0:T(8,128)S(1)} %context_states.5.high_ref, f32[2,9,32,128]{3,2,1,0:T(8,128)S(1)} %collective-permute-done.8.other_ref), custom_call_target="tpu_custom_call" | custom-call | tf_op jit(solution)/shard_map/pair_states/pallas_call | solution.py:329
  27.8 0.3 collective-permute-start.11
  28.8 2.1 %home_state.1.home_ref = f32[9,32,128]{2,1,0:T(8,128)S(1)} custom-call(s32[1]{0:T(128)S(6)} %copy.17.length_ref, bf16[1,264,128]{2,1,0:T(8,128)(2,1)S(1)} %get-tuple-element.37.query_ref, bf16[4096,128]{1,0:T(8,128)(2,1)S(1)} %bitcast.27, bf16[4,1024]{1,0:T(4,128)(2,1)S(1)} %bitcast.28, bf16[4,1024]{1,0:T(4,128)(2,1)S(1)} %bitcast.29, ...), custom_call_target="tpu_custom_call" | custom-call | flops 33554432 | bytes 2097152 | tf_op jit(solution)/shard_map/home_state/pallas_call | solution.py:280
  30.9 1.9 %collective-permute-done.10.refs_1_ = s16[264,128]{1,0:T(8,128)(2,1)S(1)} collective-permute-done((s16[264,128]{1,0:T(8,128)(2,1)S(1)}, s16[264,128]{1,0:T(8,128)(2,1)S(1)}, u32[]{:S(2)}, u32[]{:S(2)}) %collective-permute-start.10) | collective-permute-done | bytes 67616 | tf_op jit(solution)/shard_map/ppermute | solution.py:436
  32.8 0.4 %collective-permute-done.11.refs_2_ = s16[264,128]{1,0:T(8,128)(2,1)S(1)} collective-permute-done((s16[264,128]{1,0:T(8,128)(2,1)S(1)}, s16[264,128]{1,0:T(8,128)(2,1)S(1)}, u32[]{:S(2)}, u32[]{:S(2)}) %collective-permute-start.11) | collective-permute-done | bytes 67616 | tf_op jit(solution)/shard_map/ppermute | solution.py:436
  33.2 1.0 %final_output.1 = bf16[8,32,128]{2,1,0:T(8,128)(2,1)} custom-call(f32[9,32,128]{2,1,0:T(8,128)S(1)} %home_state.1.home_ref, s16[264,128]{1,0:T(8,128)(2,1)S(1)} %collective-permute-done.9.refs_0_, s16[264,128]{1,0:T(8,128)(2,1)S(1)} %collective-permute-done.10.refs_1_, s16[264,128]{1,0:T(8,128)(2,1)S(1)} %collective-permute-done.11.refs_2_), custom_call_target="tpu_custom_call" | custom-call | tf_op jit(solution)/shard_map/final_output/pallas_call | solution.py:363
  (11 shorter events, 0.0 us)
Async XLA Ops:
  1.8 15.0 %collective-permute-start.5 = (bf16[2,64,1024]{2,1,0:T(8,128)(2,1)S(1)}, bf16[2,64,1024]{2,1,0:T(8,128)(2,1)S(1)}, u32[]{:S(2)}, u32[]{:S(2)}) collective-permute-start(bf16[2,64,1024]{2,1,0:T(8,128)(2,1)S(1)} %get-tuple-element.51.refs_6_), channel_id=1, source_target_pairs={{0,3},{1,2},{2,1},{3,0},{4,7},{5,6},{6,5},{7,4},{8,11},{9,10},{10,... | collective-permute-start | bytes 786440 | tf_op jit(solution)/shard_map/ppermute | solution.py:395
  5.8 11.9 %collective-permute-start.4 = (bf16[2,64,1024]{2,1,0:T(8,128)(2,1)S(1)}, bf16[2,64,1024]{2,1,0:T(8,128)(2,1)S(1)}, u32[]{:S(2)}, u32[]{:S(2)}) collective-permute-start(bf16[2,64,1024]{2,1,0:T(8,128)(2,1)S(1)} %get-tuple-element.51.refs_6_), channel_id=1, source_target_pairs={{0,2},{1,3},{2,0},{3,1},{4,6},{5,7},{6,4},{7,5},{8,10},{9,11},{10,... | collective-permute-start | bytes 786440 | tf_op jit(solution)/shard_map/ppermute | solution.py:395
  6.3 11.7 %collective-permute-start.3 = (bf16[2,64,1024]{2,1,0:T(8,128)(2,1)S(1)}, bf16[2,64,1024]{2,1,0:T(8,128)(2,1)S(1)}, u32[]{:S(2)}, u32[]{:S(2)}) collective-permute-start(bf16[2,64,1024]{2,1,0:T(8,128)(2,1)S(1)} %get-tuple-element.51.refs_6_), channel_id=1, source_target_pairs={{0,1},{1,0},{2,3},{3,2},{4,5},{5,4},{6,7},{7,6},{8,9},{9,8},{10,11... | collective-permute-start | bytes 786440 | tf_op jit(solution)/shard_map/ppermute | solution.py:395
  6.4 5.3 %collective-permute-start = (bf16[1,264,128]{2,1,0:T(8,128)(2,1)S(1)}, bf16[1,264,128]{2,1,0:T(8,128)(2,1)S(1)}, u32[]{:S(2)}, u32[]{:S(2)}) collective-permute-start(bf16[1,264,128]{2,1,0:T(8,128)(2,1)S(1)} %get-tuple-element.37.query_ref), channel_id=1, source_target_pairs={{0,16},{4,20},{8,24},{12,28},{16,0},{20,4},{24,8},{28,12},{1,17},{... | collective-permute-start | bytes 202760 | tf_op jit(solution)/shard_map/ppermute | solution.py:408
  11.8 5.1 %collective-permute-start.2 = (bf16[2,264,128]{2,1,0:T(8,128)(2,1)S(1)}, bf16[2,264,128]{2,1,0:T(8,128)(2,1)S(1)}, u32[]{:S(2)}, u32[]{:S(2)}) collective-permute-start(bf16[2,264,128]{2,1,0:T(8,128)(2,1)S(1)} %constant_dynamic-update-slice_fusion.refs_0_), channel_id=1, source_target_pairs={{0,8},{4,12},{8,0},{12,4},{16,24},{20,28},{24,16},{28,20},{1,9},{5... | collective-permute-start | bytes 405512 | tf_op jit(solution)/shard_map/ppermute | solution.py:408
  15.6 3.5 %collective-permute-start.1 = (bf16[2,264,128]{2,1,0:T(8,128)(2,1)S(1)}, bf16[2,264,128]{2,1,0:T(8,128)(2,1)S(1)}, u32[]{:S(2)}, u32[]{:S(2)}) collective-permute-start(bf16[2,264,128]{2,1,0:T(8,128)(2,1)S(1)} %constant_dynamic-update-slice_fusion.refs_0_), channel_id=1, source_target_pairs={{0,4},{4,0},{8,12},{12,8},{16,20},{20,16},{24,28},{28,24},{1,5},{5... | collective-permute-start | bytes 405512 | tf_op jit(solution)/shard_map/ppermute | solution.py:411
  18.0 1.4 %collective-permute-start.6 = (bf16[2,264,128]{2,1,0:T(8,128)(2,1)S(1)}, bf16[2,264,128]{2,1,0:T(8,128)(2,1)S(1)}, u32[]{:S(2)}, u32[]{:S(2)}) collective-permute-start(bf16[2,264,128]{2,1,0:T(8,128)(2,1)S(1)} %collective-permute-done.2.refs_1_), channel_id=1, source_target_pairs={{0,4},{4,0},{8,12},{12,8},{16,20},{20,16},{24,28},{28,24},{1,5},{5... | collective-permute-start | bytes 405512 | tf_op jit(solution)/shard_map/ppermute | solution.py:411
  20.8 7.9 %copy-start = (bf16[1,256,2,1024]{3,2,1,0:T(2,128)(2,1)S(1)}, bf16[1,256,2,1024]{3,2,1,0:T(2,128)(2,1)}, u32[]{:S(2)}) copy-start(bf16[1,256,2,1024]{3,2,1,0:T(2,128)(2,1)} %param.14) | copy-start | bytes 3145732
  20.8 7.9 %copy-start.1 = (bf16[1,4,1024]{2,1,0:T(4,128)(2,1)S(1)}, bf16[1,4,1024]{2,1,0:T(4,128)(2,1)}, u32[]{:S(2)}) copy-start(bf16[1,4,1024]{2,1,0:T(4,128)(2,1)} %param.16) | copy-start | bytes 24580
  20.8 7.9 %copy-start.2 = (bf16[1,4,1024]{2,1,0:T(4,128)(2,1)S(1)}, bf16[1,4,1024]{2,1,0:T(4,128)(2,1)}, u32[]{:S(2)}) copy-start(bf16[1,4,1024]{2,1,0:T(4,128)(2,1)} %param.17) | copy-start | bytes 24580
  20.8 1.6 %collective-permute-start.7 = (f32[2,9,32,128]{3,2,1,0:T(8,128)S(1)}, f32[2,9,32,128]{3,2,1,0:T(8,128)S(1)}, u32[]{:S(2)}, u32[]{:S(2)}) collective-permute-start(f32[2,9,32,128]{3,2,1,0:T(8,128)S(1)} %get-tuple-element.62), channel_id=1, source_target_pairs={{0,4},{4,0},{8,12},{12,8},{16,20},{20,16},{24,28},{28,24},{1,5},{5... | collective-permute-start | bytes 884744 | tf_op jit(solution)/shard_map/ppermute | solution.py:424
  23.2 4.2 %collective-permute-start.8 = (f32[2,9,32,128]{3,2,1,0:T(8,128)S(1)}, f32[2,9,32,128]{3,2,1,0:T(8,128)S(1)}, u32[]{:S(2)}, u32[]{:S(2)}) collective-permute-start(f32[2,9,32,128]{3,2,1,0:T(8,128)S(1)} %get-tuple-element.66), channel_id=1, source_target_pairs={{0,4},{4,0},{8,12},{12,8},{16,20},{20,16},{24,28},{28,24},{1,5},{5... | collective-permute-start | bytes 884744 | tf_op jit(solution)/shard_map/ppermute | solution.py:430
  23.4 7.4 %collective-permute-start.9 = (s16[264,128]{1,0:T(8,128)(2,1)S(1)}, s16[264,128]{1,0:T(8,128)(2,1)S(1)}, u32[]{:S(2)}, u32[]{:S(2)}) collective-permute-start(s16[264,128]{1,0:T(8,128)(2,1)S(1)} %get-tuple-element.67.refs_0_), channel_id=1, source_target_pairs={{0,16},{4,20},{8,24},{12,28},{16,0},{20,4},{24,8},{28,12},{1,17},{... | collective-permute-start | bytes 202760 | tf_op jit(solution)/shard_map/ppermute | solution.py:436
  26.0 6.7 %collective-permute-start.10 = (s16[264,128]{1,0:T(8,128)(2,1)S(1)}, s16[264,128]{1,0:T(8,128)(2,1)S(1)}, u32[]{:S(2)}, u32[]{:S(2)}) collective-permute-start(s16[264,128]{1,0:T(8,128)(2,1)S(1)} %get-tuple-element.68.refs_1_), channel_id=1, source_target_pairs={{0,24},{4,28},{8,16},{12,20},{16,8},{20,12},{24,0},{28,4},{1,25},{... | collective-permute-start | bytes 202760 | tf_op jit(solution)/shard_map/ppermute | solution.py:436
  27.8 5.4 %collective-permute-start.11 = (s16[264,128]{1,0:T(8,128)(2,1)S(1)}, s16[264,128]{1,0:T(8,128)(2,1)S(1)}, u32[]{:S(2)}, u32[]{:S(2)}) collective-permute-start(s16[264,128]{1,0:T(8,128)(2,1)S(1)} %pair_states.3.refs_2_), channel_id=1, source_target_pairs={{0,8},{4,12},{8,0},{12,4},{16,24},{20,28},{24,16},{28,20},{1,9},{5... | collective-permute-start | bytes 202760 | tf_op jit(solution)/shard_map/ppermute | solution.py:436

commit v9 on v7

--- a/solution.py
+++ b/solution.py
@@ -409,7 +409,7 @@
     heads = tuple(range(KEY_VALUE_HEADS))
     first, second = heads[:5], heads[5:]
     members = range(pair_count)
-    far = [i for i in members if masks[i] >= pair_count // 2]
+    far = [i for i in reversed(members) if masks[i] >= pair_count // 2]
     rest = [i for i in members if i not in far]
     (low,) = context_states(first, [members], pieces, *shared)
     other_pieces, low = lax.optimization_barrier((other_pieces, low))

time: 34.4 us -> 34.4 us (level)
  transfers between devices with their start and end apart: 12 -> 12, of which waited for: 8 -> 7; matrix products, arithmetic and copies ran while one was open for 0% -> 0% of each run, Pallas kernels for 23% -> 23%
where the time goes in v9:
time: 34.4 us; the launch traced here: 34.3 us
  starting transfers between devices  14.6 us (42%)
  Pallas kernels  12.2 us (35%)
  waiting for transfers between devices  6.04 us (18%)
  between operations  1.45 us (4%)
    ppermute x2, starting transfers between devices, shards(): pieces = [column, lax.ppermute(column, 'ctx', swap(ctx_count, 2 * bit))]  4.87 us
    ppermute x3, starting transfers between devices, shards(): lax.ppermute(tab_block, 'tab', swap(tab_count, k))  4.6 us
    ppermute x3, starting transfers between devices, shards(): lax.ppermute(code, 'ctx', swap(ctx_count, 2 * masks[i]))  4.45 us
    pallas_call x2, Pallas kernels, split_pairs(): pl.pallas_call(functools.partial(split_kernel, first, chunks), in_specs=i...  3.64 us
    pallas_call x3, Pallas kernels, context_states(): pl.pallas_call(functools.partial(context_kernel, heads, groups, len(piece...  3.19 us
    ppermute x3, waiting for transfers between devices, shards(): lax.ppermute(code, 'ctx', swap(ctx_count, 2 * masks[i]))  2.17 us
    pallas_call x1, Pallas kernels, home_state(): pl.pallas_call(functools.partial(home_kernel, steps), in_specs=in_smem(1)...  2.1 us
    ppermute x2, waiting for transfers between devices, shards(): pieces = [column, lax.ppermute(column, 'ctx', swap(ctx_count, 2 * bit))]  1.81 us
  transfers between devices with their start and end apart: 12, of which 7 were waited for; matrix products, arithmetic and copies ran while one was open for 0% of the time, Pallas kernels for 23%

profile of v9, /device:TPU:0, one launch (start us, length us, event | category | flops | bytes accessed | tf_op | source)
XLA Modules:
  0.0 34.3 jit_solution(7049114094262061027)
XLA Ops:
  0.7 1.2 %prepare.1 = (bf16[1,264,128]{2,1,0:T(8,128)(2,1)S(1)}, bf16[2,64,1024]{2,1,0:T(8,128)(2,1)S(1)}) custom-call(s32[1]{0:T(128)S(6)} %copy.16.session, s32[4]{0:T(128)} %owner_hbm.1, bf16[256,128]{1,0:T(8,128)(2,1)} %bitcast.33, bf16[1024,128]{1,0:T(8,128)(2,1)} %bitcast.32), custom_call_target="tpu_custom_call" | custom-call | tf_op jit(solution)/shard_map/prepare/pallas_call | solution.py:97
  1.9 4.0 %collective-permute-start.5 = (bf16[2,64,1024]{2,1,0:T(8,128)(2,1)S(1)}, bf16[2,64,1024]{2,1,0:T(8,128)(2,1)S(1)}, u32[]{:S(2)}, u32[]{:S(2)}) collective-permute-start(bf16[2,64,1024]{2,1,0:T(8,128)(2,1)S(1)} %get-tuple-element.51.refs_6_), channel_id=1, source_target_pairs={{0,3},{1,2},{2,1},{3,0},{4,7},{5,6},{6,5},{7,4},{8,11},{9,10},{10,... | collective-permute-start | bytes 786440 | tf_op jit(solution)/shard_map/ppermute | solution.py:390
  5.8 0.5 %collective-permute-start.4 = (bf16[2,64,1024]{2,1,0:T(8,128)(2,1)S(1)}, bf16[2,64,1024]{2,1,0:T(8,128)(2,1)S(1)}, u32[]{:S(2)}, u32[]{:S(2)}) collective-permute-start(bf16[2,64,1024]{2,1,0:T(8,128)(2,1)S(1)} %get-tuple-element.51.refs_6_), channel_id=1, source_target_pairs={{0,2},{1,3},{2,0},{3,1},{4,6},{5,7},{6,4},{7,5},{8,10},{9,11},{10,... | collective-permute-start | bytes 786440 | tf_op jit(solution)/shard_map/ppermute | solution.py:390
  6.3 0.1 collective-permute-start.3
  6.5 3.0 %collective-permute-start = (bf16[1,264,128]{2,1,0:T(8,128)(2,1)S(1)}, bf16[1,264,128]{2,1,0:T(8,128)(2,1)S(1)}, u32[]{:S(2)}, u32[]{:S(2)}) collective-permute-start(bf16[1,264,128]{2,1,0:T(8,128)(2,1)S(1)} %get-tuple-element.37.query_ref), channel_id=1, source_target_pairs={{0,16},{4,20},{8,24},{12,28},{16,0},{20,4},{24,8},{28,12},{1,17},{... | collective-permute-start | bytes 202760 | tf_op jit(solution)/shard_map/ppermute | solution.py:403
  9.5 1.8 %split_pairs.2 = (bf16[256,1024]{1,0:T(8,128)(2,1)S(1)}, bf16[256,1024]{1,0:T(8,128)(2,1)S(1)}) custom-call(bf16[8192,128]{1,0:T(8,128)(2,1)} %bitcast.30), custom_call_target="tpu_custom_call" | custom-call | tf_op jit(solution)/shard_map/split_pairs/pallas_call | solution.py:137
  11.3 0.5 %collective-permute-done = bf16[1,264,128]{2,1,0:T(8,128)(2,1)S(1)} collective-permute-done((bf16[1,264,128]{2,1,0:T(8,128)(2,1)S(1)}, bf16[1,264,128]{2,1,0:T(8,128)(2,1)S(1)}, u32[]{:S(2)}, u32[]{:S(2)}) %collective-permute-start) | collective-permute-done | bytes 67616 | tf_op jit(solution)/shard_map/ppermute | solution.py:403
  11.8 1.9 %collective-permute-start.2 = (bf16[2,264,128]{2,1,0:T(8,128)(2,1)S(1)}, bf16[2,264,128]{2,1,0:T(8,128)(2,1)S(1)}, u32[]{:S(2)}, u32[]{:S(2)}) collective-permute-start(bf16[2,264,128]{2,1,0:T(8,128)(2,1)S(1)} %constant_dynamic-update-slice_fusion.refs_0_), channel_id=1, source_target_pairs={{0,8},{4,12},{8,0},{12,4},{16,24},{20,28},{24,16},{28,20},{1,9},{5... | collective-permute-start | bytes 405512 | tf_op jit(solution)/shard_map/ppermute | solution.py:403
  13.7 1.8 %split_pairs.3 = (bf16[256,1024]{1,0:T(8,128)(2,1)S(1)}, bf16[256,1024]{1,0:T(8,128)(2,1)S(1)}) custom-call(bf16[8192,128]{1,0:T(8,128)(2,1)} %bitcast.31), custom_call_target="tpu_custom_call" | custom-call | tf_op jit(solution)/shard_map/split_pairs/pallas_call | solution.py:137
  15.5 0.1 collective-permute-start.1
  15.6 1.3 %collective-permute-done.2.refs_1_ = bf16[2,264,128]{2,1,0:T(8,128)(2,1)S(1)} collective-permute-done((bf16[2,264,128]{2,1,0:T(8,128)(2,1)S(1)}, bf16[2,264,128]{2,1,0:T(8,128)(2,1)S(1)}, u32[]{:S(2)}, u32[]{:S(2)}) %collective-permute-start.2) | collective-permute-done | bytes 135200 | tf_op jit(solution)/shard_map/ppermute | solution.py:403
  16.9 0.8 %collective-permute-done.4.refs_8_ = bf16[2,64,1024]{2,1,0:T(8,128)(2,1)S(1)} collective-permute-done((bf16[2,64,1024]{2,1,0:T(8,128)(2,1)S(1)}, bf16[2,64,1024]{2,1,0:T(8,128)(2,1)S(1)}, u32[]{:S(2)}, u32[]{:S(2)}) %collective-permute-start.4) | collective-permute-done | bytes 262176 | tf_op jit(solution)/shard_map/ppermute | solution.py:390
  17.7 0.3 collective-permute-done.3.refs_7_
  18.0 0.0 collective-permute-start.6
  18.0 1.0 %context_states.3.low_ref = f32[4,6,32,128]{3,2,1,0:T(8,128)S(1)} custom-call(f32[1,256]{1,0:T(1,128)S(1)} %fusion.1.column_slot_ref, bf16[2,264,128]{2,1,0:T(8,128)(2,1)S(1)} %constant_dynamic-update-slice_fusion.refs_0_, bf16[2,264,128]{2,1,0:T(8,128)(2,1)S(1)} %collective-permute-done.2.refs_1_, bf16[256,1024]{1,0:T(8,128)(2,1)S(1)} %get-tuple-element.47.refs_2_, ...), custom_call_target="tpu_custom_call" | custom-call | flops 251658240 | bytes 1 | tf_op jit(solution)/shard_map/context_states/pallas_call | solution.py:210
  19.1 0.0 collective-permute-done.1.refs_0_
  19.1 0.3 collective-permute-done.6.refs_1_
  19.4 1.4 %context_states.4 = (f32[2,9,32,128]{3,2,1,0:T(8,128)S(1)}, f32[2,9,32,128]{3,2,1,0:T(8,128)S(1)}) custom-call(f32[1,256]{1,0:T(1,128)S(1)} %fusion.1.column_slot_ref, bf16[2,264,128]{2,1,0:T(8,128)(2,1)S(1)} %collective-permute-done.1.refs_0_, bf16[2,264,128]{2,1,0:T(8,128)(2,1)S(1)} %collective-permute-done.6.refs_1_, ...), custom_call_target="tpu_custom_call" | custom-call | flops 402653184 | bytes 1 | tf_op jit(solution)/shard_map/context_states/pallas_call | solution.py:210
  20.8 0.0 copy-start
  20.8 0.0 copy-start.1
  20.8 0.0 copy-start.2
  20.9 0.3 collective-permute-start.7
  21.1 0.7 %context_states.5.high_ref = f32[4,4,32,128]{3,2,1,0:T(8,128)S(1)} custom-call(f32[1,256]{1,0:T(1,128)S(1)} %fusion.1.column_slot_ref, bf16[2,264,128]{2,1,0:T(8,128)(2,1)S(1)} %constant_dynamic-update-slice_fusion.refs_0_, bf16[2,264,128]{2,1,0:T(8,128)(2,1)S(1)} %collective-permute-done.2.refs_1_, bf16[256,1024]{1,0:T(8,128)(2,1)S(1)} %get-tuple-element.47.refs_2_, ...), custom_call_target="tpu_custom_call" | custom-call | flops 150994944 | bytes 1 | tf_op jit(solution)/shard_map/context_states/pallas_call | solution.py:210
  21.9 0.6 %collective-permute-done.7.other_ref = f32[2,9,32,128]{3,2,1,0:T(8,128)S(1)} collective-permute-done((f32[2,9,32,128]{3,2,1,0:T(8,128)S(1)}, f32[2,9,32,128]{3,2,1,0:T(8,128)S(1)}, u32[]{:S(2)}, u32[]{:S(2)}) %collective-permute-start.7) | collective-permute-done | bytes 294944 | tf_op jit(solution)/shard_map/ppermute | solution.py:419
  22.5 0.7 %pair_states.2 = (s16[264,128]{1,0:T(8,128)(2,1)S(1)}, s16[264,128]{1,0:T(8,128)(2,1)S(1)}) custom-call(f32[4,6,32,128]{3,2,1,0:T(8,128)S(1)} %context_states.3.low_ref, f32[4,4,32,128]{3,2,1,0:T(8,128)S(1)} %context_states.5.high_ref, f32[2,9,32,128]{3,2,1,0:T(8,128)S(1)} %collective-permute-done.7.other_ref), custom_call_target="tpu_custom_call" | custom-call | tf_op jit(solution)/shard_map/pair_states/pallas_call | solution.py:324
  23.2 0.3 collective-permute-start.8
  23.5 3.6 %collective-permute-start.9 = (s16[264,128]{1,0:T(8,128)(2,1)S(1)}, s16[264,128]{1,0:T(8,128)(2,1)S(1)}, u32[]{:S(2)}, u32[]{:S(2)}) collective-permute-start(s16[264,128]{1,0:T(8,128)(2,1)S(1)} %get-tuple-element.67.refs_0_), channel_id=1, source_target_pairs={{0,24},{4,28},{8,16},{12,20},{16,8},{20,12},{24,0},{28,4},{1,25},{... | collective-permute-start | bytes 202760 | tf_op jit(solution)/shard_map/ppermute | solution.py:431
  27.1 0.4 %pair_states.3.refs_2_ = s16[264,128]{1,0:T(8,128)(2,1)S(1)} custom-call(f32[4,6,32,128]{3,2,1,0:T(8,128)S(1)} %context_states.3.low_ref, f32[4,4,32,128]{3,2,1,0:T(8,128)S(1)} %context_states.5.high_ref, f32[2,9,32,128]{3,2,1,0:T(8,128)S(1)} %collective-permute-done.8.other_ref), custom_call_target="tpu_custom_call" | custom-call | tf_op jit(solution)/shard_map/pair_states/pallas_call | solution.py:324
  27.5 0.8 %collective-permute-start.11 = (s16[264,128]{1,0:T(8,128)(2,1)S(1)}, s16[264,128]{1,0:T(8,128)(2,1)S(1)}, u32[]{:S(2)}, u32[]{:S(2)}) collective-permute-start(s16[264,128]{1,0:T(8,128)(2,1)S(1)} %pair_states.3.refs_2_), channel_id=1, source_target_pairs={{0,8},{4,12},{8,0},{12,4},{16,24},{20,28},{24,16},{28,20},{1,9},{5... | collective-permute-start | bytes 202760 | tf_op jit(solution)/shard_map/ppermute | solution.py:431
  29.0 2.1 %home_state.1.home_ref = f32[9,32,128]{2,1,0:T(8,128)S(1)} custom-call(s32[1]{0:T(128)S(6)} %copy.17.length_ref, bf16[1,264,128]{2,1,0:T(8,128)(2,1)S(1)} %get-tuple-element.37.query_ref, bf16[4096,128]{1,0:T(8,128)(2,1)S(1)} %bitcast.27, bf16[4,1024]{1,0:T(4,128)(2,1)S(1)} %bitcast.28, bf16[4,1024]{1,0:T(4,128)(2,1)S(1)} %bitcast.29, ...), custom_call_target="tpu_custom_call" | custom-call | flops 33554432 | bytes 2097152 | tf_op jit(solution)/shard_map/home_state/pallas_call | solution.py:275
  31.1 2.2 %collective-permute-done.10.refs_1_ = s16[264,128]{1,0:T(8,128)(2,1)S(1)} collective-permute-done((s16[264,128]{1,0:T(8,128)(2,1)S(1)}, s16[264,128]{1,0:T(8,128)(2,1)S(1)}, u32[]{:S(2)}, u32[]{:S(2)}) %collective-permute-start.10) | collective-permute-done | bytes 67616 | tf_op jit(solution)/shard_map/ppermute | solution.py:431
  33.3 1.0 %final_output.1 = bf16[8,32,128]{2,1,0:T(8,128)(2,1)} custom-call(f32[9,32,128]{2,1,0:T(8,128)S(1)} %home_state.1.home_ref, s16[264,128]{1,0:T(8,128)(2,1)S(1)} %collective-permute-done.9.refs_0_, s16[264,128]{1,0:T(8,128)(2,1)S(1)} %collective-permute-done.10.refs_1_, s16[264,128]{1,0:T(8,128)(2,1)S(1)} %collective-permute-done.11.refs_2_), custom_call_target="tpu_custom_call" | custom-call | tf_op jit(solution)/shard_map/final_output/pallas_call | solution.py:358
  (11 shorter events, 0.0 us)
Async XLA Ops:
  1.9 15.0 %collective-permute-start.5 = (bf16[2,64,1024]{2,1,0:T(8,128)(2,1)S(1)}, bf16[2,64,1024]{2,1,0:T(8,128)(2,1)S(1)}, u32[]{:S(2)}, u32[]{:S(2)}) collective-permute-start(bf16[2,64,1024]{2,1,0:T(8,128)(2,1)S(1)} %get-tuple-element.51.refs_6_), channel_id=1, source_target_pairs={{0,3},{1,2},{2,1},{3,0},{4,7},{5,6},{6,5},{7,4},{8,11},{9,10},{10,... | collective-permute-start | bytes 786440 | tf_op jit(solution)/shard_map/ppermute | solution.py:390
  5.8 11.9 %collective-permute-start.4 = (bf16[2,64,1024]{2,1,0:T(8,128)(2,1)S(1)}, bf16[2,64,1024]{2,1,0:T(8,128)(2,1)S(1)}, u32[]{:S(2)}, u32[]{:S(2)}) collective-permute-start(bf16[2,64,1024]{2,1,0:T(8,128)(2,1)S(1)} %get-tuple-element.51.refs_6_), channel_id=1, source_target_pairs={{0,2},{1,3},{2,0},{3,1},{4,6},{5,7},{6,4},{7,5},{8,10},{9,11},{10,... | collective-permute-start | bytes 786440 | tf_op jit(solution)/shard_map/ppermute | solution.py:390
  6.3 11.7 %collective-permute-start.3 = (bf16[2,64,1024]{2,1,0:T(8,128)(2,1)S(1)}, bf16[2,64,1024]{2,1,0:T(8,128)(2,1)S(1)}, u32[]{:S(2)}, u32[]{:S(2)}) collective-permute-start(bf16[2,64,1024]{2,1,0:T(8,128)(2,1)S(1)} %get-tuple-element.51.refs_6_), channel_id=1, source_target_pairs={{0,1},{1,0},{2,3},{3,2},{4,5},{5,4},{6,7},{7,6},{8,9},{9,8},{10,11... | collective-permute-start | bytes 786440 | tf_op jit(solution)/shard_map/ppermute | solution.py:390
  6.5 5.3 %collective-permute-start = (bf16[1,264,128]{2,1,0:T(8,128)(2,1)S(1)}, bf16[1,264,128]{2,1,0:T(8,128)(2,1)S(1)}, u32[]{:S(2)}, u32[]{:S(2)}) collective-permute-start(bf16[1,264,128]{2,1,0:T(8,128)(2,1)S(1)} %get-tuple-element.37.query_ref), channel_id=1, source_target_pairs={{0,16},{4,20},{8,24},{12,28},{16,0},{20,4},{24,8},{28,12},{1,17},{... | collective-permute-start | bytes 202760 | tf_op jit(solution)/shard_map/ppermute | solution.py:403
  11.8 5.1 %collective-permute-start.2 = (bf16[2,264,128]{2,1,0:T(8,128)(2,1)S(1)}, bf16[2,264,128]{2,1,0:T(8,128)(2,1)S(1)}, u32[]{:S(2)}, u32[]{:S(2)}) collective-permute-start(bf16[2,264,128]{2,1,0:T(8,128)(2,1)S(1)} %constant_dynamic-update-slice_fusion.refs_0_), channel_id=1, source_target_pairs={{0,8},{4,12},{8,0},{12,4},{16,24},{20,28},{24,16},{28,20},{1,9},{5... | collective-permute-start | bytes 405512 | tf_op jit(solution)/shard_map/ppermute | solution.py:403
  15.5 3.5 %collective-permute-start.1 = (bf16[2,264,128]{2,1,0:T(8,128)(2,1)S(1)}, bf16[2,264,128]{2,1,0:T(8,128)(2,1)S(1)}, u32[]{:S(2)}, u32[]{:S(2)}) collective-permute-start(bf16[2,264,128]{2,1,0:T(8,128)(2,1)S(1)} %constant_dynamic-update-slice_fusion.refs_0_), channel_id=1, source_target_pairs={{0,4},{4,0},{8,12},{12,8},{16,20},{20,16},{24,28},{28,24},{1,5},{5... | collective-permute-start | bytes 405512 | tf_op jit(solution)/shard_map/ppermute | solution.py:406
  18.0 1.4 %collective-permute-start.6 = (bf16[2,264,128]{2,1,0:T(8,128)(2,1)S(1)}, bf16[2,264,128]{2,1,0:T(8,128)(2,1)S(1)}, u32[]{:S(2)}, u32[]{:S(2)}) collective-permute-start(bf16[2,264,128]{2,1,0:T(8,128)(2,1)S(1)} %collective-permute-done.2.refs_1_), channel_id=1, source_target_pairs={{0,4},{4,0},{8,12},{12,8},{16,20},{20,16},{24,28},{28,24},{1,5},{5... | collective-permute-start | bytes 405512 | tf_op jit(solution)/shard_map/ppermute | solution.py:406
  20.8 8.2 %copy-start = (bf16[1,256,2,1024]{3,2,1,0:T(2,128)(2,1)S(1)}, bf16[1,256,2,1024]{3,2,1,0:T(2,128)(2,1)}, u32[]{:S(2)}) copy-start(bf16[1,256,2,1024]{3,2,1,0:T(2,128)(2,1)} %param.14) | copy-start | bytes 3145732
  20.8 8.2 %copy-start.1 = (bf16[1,4,1024]{2,1,0:T(4,128)(2,1)S(1)}, bf16[1,4,1024]{2,1,0:T(4,128)(2,1)}, u32[]{:S(2)}) copy-start(bf16[1,4,1024]{2,1,0:T(4,128)(2,1)} %param.16) | copy-start | bytes 24580
  20.8 8.2 %copy-start.2 = (bf16[1,4,1024]{2,1,0:T(4,128)(2,1)S(1)}, bf16[1,4,1024]{2,1,0:T(4,128)(2,1)}, u32[]{:S(2)}) copy-start(bf16[1,4,1024]{2,1,0:T(4,128)(2,1)} %param.17) | copy-start | bytes 24580
  20.9 1.6 %collective-permute-start.7 = (f32[2,9,32,128]{3,2,1,0:T(8,128)S(1)}, f32[2,9,32,128]{3,2,1,0:T(8,128)S(1)}, u32[]{:S(2)}, u32[]{:S(2)}) collective-permute-start(f32[2,9,32,128]{3,2,1,0:T(8,128)S(1)} %get-tuple-element.62), channel_id=1, source_target_pairs={{0,4},{4,0},{8,12},{12,8},{16,20},{20,16},{24,28},{28,24},{1,5},{5... | collective-permute-start | bytes 884744 | tf_op jit(solution)/shard_map/ppermute | solution.py:419
  23.2 3.9 %collective-permute-start.8 = (f32[2,9,32,128]{3,2,1,0:T(8,128)S(1)}, f32[2,9,32,128]{3,2,1,0:T(8,128)S(1)}, u32[]{:S(2)}, u32[]{:S(2)}) collective-permute-start(f32[2,9,32,128]{3,2,1,0:T(8,128)S(1)} %get-tuple-element.66), channel_id=1, source_target_pairs={{0,4},{4,0},{8,12},{12,8},{16,20},{20,16},{24,28},{28,24},{1,5},{5... | collective-permute-start | bytes 884744 | tf_op jit(solution)/shard_map/ppermute | solution.py:425
  23.5 7.6 %collective-permute-start.9 = (s16[264,128]{1,0:T(8,128)(2,1)S(1)}, s16[264,128]{1,0:T(8,128)(2,1)S(1)}, u32[]{:S(2)}, u32[]{:S(2)}) collective-permute-start(s16[264,128]{1,0:T(8,128)(2,1)S(1)} %get-tuple-element.67.refs_0_), channel_id=1, source_target_pairs={{0,24},{4,28},{8,16},{12,20},{16,8},{20,12},{24,0},{28,4},{1,25},{... | collective-permute-start | bytes 202760 | tf_op jit(solution)/shard_map/ppermute | solution.py:431
  27.1 6.2 %collective-permute-start.10 = (s16[264,128]{1,0:T(8,128)(2,1)S(1)}, s16[264,128]{1,0:T(8,128)(2,1)S(1)}, u32[]{:S(2)}, u32[]{:S(2)}) collective-permute-start(s16[264,128]{1,0:T(8,128)(2,1)S(1)} %get-tuple-element.68.refs_1_), channel_id=1, source_target_pairs={{0,16},{4,20},{8,24},{12,28},{16,0},{20,4},{24,8},{28,12},{1,17},{... | collective-permute-start | bytes 202760 | tf_op jit(solution)/shard_map/ppermute | solution.py:431
  27.5 5.8 %collective-permute-start.11 = (s16[264,128]{1,0:T(8,128)(2,1)S(1)}, s16[264,128]{1,0:T(8,128)(2,1)S(1)}, u32[]{:S(2)}, u32[]{:S(2)}) collective-permute-start(s16[264,128]{1,0:T(8,128)(2,1)S(1)} %pair_states.3.refs_2_), channel_id=1, source_target_pairs={{0,8},{4,12},{8,0},{12,4},{16,24},{20,28},{24,16},{28,20},{1,9},{5... | collective-permute-start | bytes 202760 | tf_op jit(solution)/shard_map/ppermute | solution.py:431
